TPU v7x, 256 devices: a whole 4x4x8 slice. The times are simulated.
256 devices in a mesh: tm: 16 (over y, z_lo, core), bank: 16 (over x, z_hi).
Axes of the slice: x: 4, y: 4, z: 8 (z_hi: 4, z_lo: 2; z = z_hi * 2 + z_lo), core: 2. Of those that a mesh axis runs over, the one named last changes fastest.
Arguments:
- spectrum: float32 [2, 64, 16384], P(None, None, 'tm'), may hold values from -6 to 6
- filters: bfloat16 [2, 512, 64, 16384], P(None, 'bank', None, 'tm'), may hold values from -0.005859375 to 0.005859375
- mixing: bfloat16 [2, 16384, 512], P(None, 'bank'), may hold values from -0.25 to 0.25
Outputs:
- snr_series: bfloat16 [2, 64, 16384, 128], P(None, 'tm', 'bank')
All inputs are finite; a program needn't handle non-finite values.
Results may differ from a plain program's by a relative error of at most 0.007.
Values may be sent and summed in bfloat16 or wider, within the bound.
A program may use at most 128 MiB of HBM per device.

v0:
```python
import math

import jax
import jax.numpy as jnp
from jax import lax
from jax.sharding import PartitionSpec as P

NSAMP = 1048576
INNER = 64
WROWS = 128
START = 8128


def first_table(inner):
    index = jnp.arange(inner, dtype=jnp.int32)
    phase = index[:, None] * index[None, :] % inner
    angle = phase.astype(jnp.float32) * (2.0 * math.pi / inner)
    cosine = jnp.cos(angle).astype(jnp.bfloat16)
    sine = jnp.sin(angle).astype(jnp.bfloat16)
    upper = jnp.concatenate([cosine, -sine], axis=1)
    lower = jnp.concatenate([sine, cosine], axis=1)
    return jnp.concatenate([upper, lower], axis=0)


def wave_block(freqs, lags, period):
    phase = freqs[:, None] * lags[None, :] % period
    angle = phase.astype(jnp.float32) * (2.0 * math.pi / period)
    cosine = jnp.cos(angle).astype(jnp.bfloat16)
    sine = jnp.sin(angle).astype(jnp.bfloat16)
    upper = jnp.concatenate([cosine, sine], axis=1)
    lower = jnp.concatenate([-sine, cosine], axis=1)
    return jnp.concatenate([upper, lower], axis=0)


def twist_tables(freqs, inner, total):
    rows_index = jnp.arange(inner, dtype=jnp.int32)
    phase = rows_index[:, None] * freqs[None, :] % total
    angle = phase.astype(jnp.float32) * (2.0 * math.pi / total)
    return (jnp.cos(angle), jnp.sin(angle))


def on_device(spectrum, filters, mixing):
    tm_index = lax.axis_index("tm")
    local_freq = filters.shape[3]
    local_basis = filters.shape[1]
    inner = INNER
    outer = NSAMP // INNER
    table = first_table(inner)
    freqs = tm_index * local_freq + jnp.arange(local_freq, dtype=jnp.int32)
    twist_cos, twist_sin = twist_tables(freqs, inner, NSAMP)
    filt_real = filters[0].astype(jnp.float32)
    filt_imag = filters[1].astype(jnp.float32)
    prod_real = spectrum[0] * filt_real + spectrum[1] * filt_imag
    prod_imag = spectrum[1] * filt_real - spectrum[0] * filt_imag
    packed = jnp.concatenate([prod_real, prod_imag], axis=1).astype(jnp.bfloat16)
    section = jnp.einsum("uv,kvf->kuf", table, packed, preferred_element_type=jnp.float32)
    section_real = section[:, :inner]
    section_imag = section[:, inner:]
    quarter_real = (section_real * twist_cos - section_imag * twist_sin).astype(jnp.bfloat16)
    quarter_imag = (section_real * twist_sin + section_imag * twist_cos).astype(jnp.bfloat16)
    quarter = jnp.concatenate([quarter_real, quarter_imag], axis=2)
    lags = START + jnp.arange(WROWS, dtype=jnp.int32)
    wave = wave_block(freqs, lags, outer)
    partial = jnp.einsum("ktf,fs->tks", quarter, wave, preferred_element_type=jnp.float32)
    summed = lax.psum_scatter(partial, "tm", scatter_dimension=0, tiled=True)
    series = summed.astype(jnp.bfloat16)
    piece = lax.all_gather(series, "bank", axis=0, tiled=False)
    groups = piece.shape[0]
    rows = piece.shape[1]
    piece_real = piece[..., :WROWS]
    piece_imag = piece[..., WROWS:]
    templates = mixing.shape[1]
    mix_real = mixing[0].reshape(templates, groups, local_basis)
    mix_imag = mixing[1].reshape(templates, groups, local_basis)
    real_sum = jnp.einsum(
        "jgk,gtks->tjs", mix_real, piece_real, preferred_element_type=jnp.float32
    ) - jnp.einsum("jgk,gtks->tjs", mix_imag, piece_imag, preferred_element_type=jnp.float32)
    imag_sum = jnp.einsum(
        "jgk,gtks->tjs", mix_real, piece_imag, preferred_element_type=jnp.float32
    ) + jnp.einsum("jgk,gtks->tjs", mix_imag, piece_real, preferred_element_type=jnp.float32)
    del rows
    return jnp.stack([real_sum, imag_sum], axis=0).astype(jnp.bfloat16)


def solution(mesh):
    return jax.shard_map(
        on_device,
        mesh=mesh,
        in_specs=(P(None, None, "tm"), P(None, "bank", None, "tm"), P(None, "bank", None)),
        out_specs=P(None, "tm", "bank", None),
        check_vma=False,
    )
```

profile of v0, /device:TPU:6, one launch (start us, length us, event | category | flops | bytes accessed | tf_op | source)
XLA Modules:
  0.0 175.8 jit_solution(18180238068957756443)
XLA Ops:
  6.5 0.2 sine_convert_fusion.1
  6.7 0.1 fusion.54
  6.9 1.0 fusion.40
  7.9 2.5 %sine_convert_fusion = (bf16[1024,128]{1,0:T(8,128)(2,1)S(1)}, bf16[1024,128]{1,0:T(8,128)(2,1)S(1)}) fusion(s32[128]{0:T(128)S(1)} %iota_add_fusion.1, s32[1024]{0:T(1024)S(1)} %iota_add_fusion), kind=kLoop, calls=%fused_computation.41 | loop fusion | flops 2097152 | bytes 528896 | tf_op jit(solution)/shard_map/convert_element_type | solution.py:29
  10.4 2.3 %fusion.41 = bf16[1024,128]{1,0:T(8,128)(2,1)S(1)} fusion(s32[128]{0:T(128)S(1)} %iota_add_fusion.1, s32[1024]{0:T(1024)S(1)} %iota_add_fusion), kind=kLoop, calls=%fused_computation.65 | loop fusion | flops 2359296 | bytes 266752 | tf_op jit(solution)/shard_map/neg | solution.py:31
  12.7 1.1 slice_bitcast_fusion.1
  13.8 7.5 %fusion.1 = (bf16[32,64,1024]{2,1,0:T(8,128)(2,1)}, bf16[32,64,1024]{2,1,0:T(8,128)(2,1)}) fusion(f32[64,1024]{1,0:T(8,128)S(1)} %get-tuple-element.12, f32[64,1024]{1,0:T(8,128)S(1)} %get-tuple-element.11, bf16[2,32,64,1024]{3,2,1,0:T(8,128)(2,1)} %param.4), kind=kLoop, calls=%fused_computation.6 | loop fusion | flops 20971520 | bytes 17301504 | tf_op jit(solution)/shard_map/convert.8
  21.2 4.9 %convolution_bitcast_fusion = f32[32,128,1024]{2,1,0:T(8,128)S(1)} fusion(bf16[32,64,1024]{2,1,0:T(8,128)(2,1)} %get-tuple-element.8, bf16[32,64,1024]{2,1,0:T(8,128)(2,1)} %get-tuple-element.7, bf16[64,64]{1,0:T(8,128)(2,1)S(1)} %get-tuple-element.18, bf16[64,64]{1,0:T(8,128)(2,1)S(1)} %get-tuple-element.17, bf16[64,64]{1,0:T(8,128)(2,1)S(1)} %fusion.54), kind=kOutput, calls=%fused_computation.4 | convolution fusion | flops 1090650112 | bytes 25190400 | tf_op jit(solution)/shard_map/uv,kvf->kuf/dot_general | solution.py:56
  26.1 5.1 %subtract_convert_fusion = (bf16[32,64,1024]{2,1,0:T(8,128)(2,1)}, bf16[32,64,1024]{2,1,0:T(8,128)(2,1)}) fusion(f32[32,128,1024]{2,1,0:T(8,128)S(1)} %convolution_bitcast_fusion, f32[64,1024]{1,0:T(8,128)S(1)} %get-tuple-element.16, f32[64,1024]{1,0:T(8,128)S(1)} %get-tuple-element.15), kind=kLoop, calls=%fused_computation.17 | loop fusion | flops 16777216 | bytes 25690112 | tf_op jit(solution)/shard_map/convert_element_type | solution.py:59
  31.2 4.9 %fusion.13 = f32[64,32,256]{2,0,1:T(8,128)S(1)} fusion(bf16[32,64,1024]{2,1,0:T(8,128)(2,1)} %get-tuple-element.6, bf16[32,64,1024]{2,1,0:T(8,128)(2,1)} %get-tuple-element.5, bf16[1024,128]{1,0:T(8,128)(2,1)S(1)} %get-tuple-element.14, bf16[1024,128]{1,0:T(8,128)(2,1)S(1)} %fusion.41, bf16[1024,128]{1,0:T(8,128)(2,1)S(1)} %get-tuple-element.13), kind=kOutput, calls=%fused_computation.23 | convolution fusion | flops 2168455168 | bytes 11272192 | tf_op jit(solution)/shard_map/ktf,fs->tks/dot_general | solution.py:64
  36.1 2.5 %copy.13 = f32[64,32,256]{2,1,0:T(8,128)} copy(f32[64,32,256]{2,0,1:T(8,128)S(1)} %fusion.13) | data formatting | bytes 4194304 | tf_op jit(solution)/shard_map/ktf,fs->tks/transpose | solution.py:64
  38.7 0.2 all-gather.3.cloned.1.call-start
  38.9 69.9 %reduce-scatter.2.cloned.1.call-done = f32[4,32,256]{2,1,0:T(8,128)} async-done(((f32[64,32,256]{2,1,0:T(8,128)}), f32[4,32,256]{2,1,0:T(8,128)}) %reduce-scatter.2.cloned.1.call-update) | async-done | bytes 131088 | tf_op jit(solution)/shard_map/reduce_scatter | solution.py:65
  108.8 1.5 convert_element_type.74
  110.4 1.7 fusion.57
  112.1 0.5 copy.15
  112.6 0.5 copy.17
  113.2 47.9 %all-gather.3.cloned.1.call-done = bf16[64,32,256]{2,1,0:T(8,128)(2,1)} async-done(((bf16[4,32,256]{2,1,0:T(8,128)(2,1)}), bf16[64,32,256]{2,1,0:T(8,128)(2,1)}) %all-gather.3.cloned.1.call-update) | async-done | bytes 1048592 | tf_op jit(solution)/shard_map/all_gather | solution.py:67
  161.1 1.9 %fusion.30 = f32[4,128,1024,1]{2,1,0,3:T(8,128)S(1)} fusion(bf16[1024,16,32,1]{0,2,3,1:T(8,128)(2,1)S(1)} %bitcast.79, bf16[16,4,32,256]{3,2,1,0:T(8,128)(2,1)} %bitcast.83), kind=kOutput, calls=%fused_computation.46 | convolution fusion | flops 536870912 | bytes 3670016 | tf_op jit(solution)/shard_map/jgk,gtks->tjs/dot_general | solution.py:75
  162.9 1.8 %fusion.28 = f32[4,128,1024,1]{2,1,0,3:T(8,128)S(1)} fusion(bf16[1024,16,32,1]{0,2,3,1:T(8,128)(2,1)S(1)} %bitcast.80, bf16[16,4,32,256]{3,2,1,0:T(8,128)(2,1)} %bitcast.84), kind=kOutput, calls=%fused_computation.44 | convolution fusion | flops 536870912 | bytes 3670016 | tf_op jit(solution)/shard_map/jgk,gtks->tjs/dot_general | solution.py:78
  164.7 0.7 fusion.16
  165.4 0.7 fusion.17
  166.2 0.2 pad_maximum_fusion
  166.4 2.6 %copy.18 = bf16[2,4,1024,128]{3,2,1,0:T(8,128)(2,1)} copy(bf16[2,4,1024,128]{2,3,1,0:T(8,128)(2,1)S(1)} %pad_maximum_fusion) | data formatting | bytes 4194304 | tf_op jit(solution)/shard_map/stack | solution.py:82
  (7 shorter events, 0.0 us)
Async XLA Ops:
  6.5 102.3 %reduce-scatter.2.cloned.1.call-start = ((), (), s32[]{:S(2)}) async-start(), calls=%async_computation.1 | async-start | bytes 2228224 | tf_op jit(solution)/shard_map/reduce_scatter | solution.py:65
  38.7 122.4 %all-gather.3.cloned.1.call-start = ((), (), s32[]{:S(2)}) async-start(), calls=%async_computation.2 | async-start | bytes 1114112 | tf_op jit(solution)/shard_map/all_gather | solution.py:67
  161.1 3.6 %copy-start = (bf16[64,32,256]{2,1,0:T(8,128)(2,1)S(1)}, bf16[64,32,256]{2,1,0:T(8,128)(2,1)}, u32[]{:S(2)}) copy-start(bf16[64,32,256]{2,1,0:T(8,128)(2,1)} %all-gather.3.cloned.1.call-done) | copy-start | bytes 3145732
Sparse Core Ops, SparseCore 0:
  38.8 69.9 reduce-scatter.1
  111.3 49.7 all-gather.2
where the time goes:
time: 178 us; the launch traced here: 176 us
  waiting for transfers between devices  118 us (66%)
  other arithmetic  20.4 us (11%)
  matrix products  14.9 us (8%)
  between operations  13.5 us (8%)
  local copies, waits for them, and re-layouts  8.92 us (5%)
    reduce_scatter x1, waiting for transfers between devices, on_device(): summed = lax.psum_scatter(partial, 'tm', scatter_dimension=0, tiled=True)  69.9 us
    all_gather x1, waiting for transfers between devices, on_device(): piece = lax.all_gather(series, 'bank', axis=0, tiled=False)  47.9 us
    another operation x1, other arithmetic  7.47 us
    convert_element_type x1, other arithmetic, on_device(): (section_real * twist_cos - section_imag * twist_sin).astype(jnp.bfloat16)  5.06 us
    dot_general x1, matrix products, on_device(): jnp.einsum('ktf,fs->tks', quarter, wave, preferred_element_type=jnp.float32)  4.93 us
    dot_general x1, matrix products, on_device(): jnp.einsum('uv,kvf->kuf', table, packed, preferred_element_type=jnp.float32)  4.9 us
  transfers between devices with their start and end apart: 2, of which 2 were waited for; matrix products, arithmetic and copies ran while one was open for 2% of the time, Pallas kernels for 0%

commit v1 on v0

--- a/solution.py
+++ b/solution.py
@@ -1,8 +1,11 @@
+import functools
 import math
 
 import jax
 import jax.numpy as jnp
 from jax import lax
+from jax.experimental import pallas as pl
+from jax.experimental.pallas import tpu as pltpu
 from jax.sharding import PartitionSpec as P
 
 NSAMP = 1048576
@@ -37,6 +40,117 @@
     phase = rows_index[:, None] * freqs[None, :] % total
     angle = phase.astype(jnp.float32) * (2.0 * math.pi / total)
     return (jnp.cos(angle), jnp.sin(angle))
+
+
+MESH = pl.DeviceIdType.MESH
+
+
+def greet(axis, n, other):
+    me = lax.axis_index(axis)
+    barrier = pltpu.get_barrier_semaphore()
+    for step in range(1, n):
+        peer = (me + step) % n
+        pl.semaphore_signal(barrier, inc=1, device_id=other(peer), device_id_type=MESH)
+    pl.semaphore_wait(barrier, n - 1)
+    return me
+
+
+def scatter_sum_kernel(n, x_ref, o_ref, slots, send_sem, recv_sem):
+    bank = lax.axis_index("bank")
+    place = lambda peer: (peer, bank)
+    me = greet("tm", n, place)
+    rows = o_ref.shape[0]
+    sends = []
+    for step in range(1, n):
+        peer = (me + step) % n
+        copy = pltpu.make_async_remote_copy(
+            src_ref=x_ref.at[pl.ds(peer * rows, rows)],
+            dst_ref=slots.at[me],
+            send_sem=send_sem.at[peer],
+            recv_sem=recv_sem.at[me],
+            device_id=place(peer),
+            device_id_type=MESH,
+        )
+        copy.start()
+        sends.append(copy)
+    total = x_ref[pl.ds(me * rows, rows)]
+    for step in range(1, n):
+        source = (me + n - step) % n
+        pltpu.make_async_remote_copy(
+            src_ref=x_ref.at[pl.ds(0, rows)],
+            dst_ref=slots.at[source],
+            send_sem=send_sem.at[source],
+            recv_sem=recv_sem.at[source],
+            device_id=place(source),
+            device_id_type=MESH,
+        ).wait_recv()
+        total = total + slots[source]
+    for copy in sends:
+        copy.wait_send()
+    o_ref[...] = total.astype(o_ref.dtype)
+
+
+def scatter_sum(x, n):
+    rows = x.shape[0] // n
+    shape = (rows,) + x.shape[1:]
+    return pl.pallas_call(
+        functools.partial(scatter_sum_kernel, n),
+        out_shape=jax.ShapeDtypeStruct(shape, jnp.bfloat16),
+        in_specs=[pl.BlockSpec(memory_space=pltpu.VMEM)],
+        out_specs=pl.BlockSpec(memory_space=pltpu.VMEM),
+        scratch_shapes=[
+            pltpu.VMEM((n,) + shape, x.dtype),
+            pltpu.SemaphoreType.DMA((n,)),
+            pltpu.SemaphoreType.DMA((n,)),
+        ],
+        compiler_params=pltpu.CompilerParams(collective_id=0, has_side_effects=True),
+    )(x)
+
+
+def gather_kernel(n, x_ref, o_ref, send_sem, recv_sem):
+    tm = lax.axis_index("tm")
+    place = lambda peer: (tm, peer)
+    me = greet("bank", n, place)
+    sends = []
+    for step in range(1, n):
+        peer = (me + step) % n
+        copy = pltpu.make_async_remote_copy(
+            src_ref=x_ref,
+            dst_ref=o_ref.at[me],
+            send_sem=send_sem.at[peer],
+            recv_sem=recv_sem.at[me],
+            device_id=place(peer),
+            device_id_type=MESH,
+        )
+        copy.start()
+        sends.append(copy)
+    o_ref[me] = x_ref[...]
+    for step in range(1, n):
+        source = (me + n - step) % n
+        pltpu.make_async_remote_copy(
+            src_ref=x_ref,
+            dst_ref=o_ref.at[source],
+            send_sem=send_sem.at[source],
+            recv_sem=recv_sem.at[source],
+            device_id=place(source),
+            device_id_type=MESH,
+        ).wait_recv()
+    for copy in sends:
+        copy.wait_send()
+
+
+def gather(x, n):
+    return pl.pallas_call(
+        functools.partial(gather_kernel, n),
+        out_shape=jax.ShapeDtypeStruct((n,) + x.shape, x.dtype),
+        in_specs=[pl.BlockSpec(memory_space=pltpu.VMEM)],
+        out_specs=pl.BlockSpec(memory_space=pltpu.VMEM),
+        scratch_shapes=[
+            pltpu.SemaphoreType.DMA((n,)),
+            pltpu.SemaphoreType.DMA((n,)),
+        ],
+        compiler_params=pltpu.CompilerParams(collective_id=1, has_side_effects=True),
+    )(x)
 
 
 def on_device(spectrum, filters, mixing):
@@ -62,9 +176,8 @@
     lags = START + jnp.arange(WROWS, dtype=jnp.int32)
     wave = wave_block(freqs, lags, outer)
     partial = jnp.einsum("ktf,fs->tks", quarter, wave, preferred_element_type=jnp.float32)
-    summed = lax.psum_scatter(partial, "tm", scatter_dimension=0, tiled=True)
-    series = summed.astype(jnp.bfloat16)
-    piece = lax.all_gather(series, "bank", axis=0, tiled=False)
+    series = scatter_sum(partial, lax.axis_size("tm"))
+    piece = gather(series, lax.axis_size("bank"))
     groups = piece.shape[0]
     rows = piece.shape[1]
     piece_real = piece[..., :WROWS]

time: 178 us -> 130 us (0.73)
  the two profiles are of different devices: /device:TPU:6 before, /device:TPU:1 now
where the time goes in v1:
time: 130 us
  Pallas kernels  67.7 us (52%)
  other arithmetic  29 us (22%)
  matrix products  24.5 us (19%)
  local copies, waits for them, and re-layouts  8.43 us (6%)
    pallas_call x1, Pallas kernels, gather(): pl.pallas_call(functools.partial(gather_kernel, n), out_shape=jax.ShapeDt...  35 us
    pallas_call x1, Pallas kernels, scatter_sum(): pl.pallas_call(functools.partial(scatter_sum_kernel, n), out_shape=jax.Sh...  32.7 us
    dot_general x1, matrix products, on_device(): jnp.einsum('ktf,fs->tks', quarter, wave, preferred_element_type=jnp.float32)  10.5 us
    convert_element_type x1, other arithmetic, on_device(): (section_real * twist_cos - section_imag * twist_sin).astype(jnp.bfloat16)  9.36 us
    concatenate x1, other arithmetic, on_device(): quarter = jnp.concatenate([quarter_real, quarter_imag], axis=2)  8.17 us
    dot_general x1, matrix products, on_device(): jnp.einsum('uv,kvf->kuf', table, packed, preferred_element_type=jnp.float32)  7.11 us
    another operation x1, other arithmetic  5.03 us
    slice x2, local copies, waits for them, and re-layouts, on_device(): mix_real = mixing[0].reshape(templates, groups, local_basis)  3.32 us

profile of v1, /device:TPU:1, one launch (start us, length us, event | category | flops | bytes accessed | tf_op | source)
XLA Modules:
  0.0 129.7 jit_solution(9704905380672355728)
XLA Ops:
  0.0 1.1 slice_bitcast_fusion.1
  1.1 5.0 %fusion.1 = (bf16[32,64,1024]{2,1,0:T(8,128)(2,1)S(1)}, bf16[32,64,1024]{2,1,0:T(8,128)(2,1)S(1)}) fusion(f32[64,1024]{1,0:T(8,128)S(1)} %get-tuple-element.12, f32[64,1024]{1,0:T(8,128)S(1)} %get-tuple-element.11, bf16[2,32,64,1024]{3,2,1,0:T(8,128)(2,1)} %param.4), kind=kLoop, calls=%fused_computation.6 | loop fusion | flops 20971520 | bytes 17301504 | tf_op jit(solution)/shard_map/convert.8
  6.1 0.2 sine_convert_fusion.1
  6.3 0.1 fusion.52
  6.4 7.1 %convolution_bitcast_fusion = f32[32,128,1024]{2,1,0:T(8,128)} fusion(bf16[32,64,1024]{2,1,0:T(8,128)(2,1)S(1)} %get-tuple-element.8, bf16[32,64,1024]{2,1,0:T(8,128)(2,1)S(1)} %get-tuple-element.7, bf16[64,64]{1,0:T(8,128)(2,1)S(1)} %get-tuple-element.18, bf16[64,64]{1,0:T(8,128)(2,1)S(1)} %get-tuple-element.17, bf16[64,64]{1,0:T(8,128)(2,1)S(1)} %fusion.52), kind=kOutput, calls=%fused_computation.4 | convolution fusion | flops 1090650112 | bytes 25190400 | tf_op jit(solution)/shard_map/uv,kvf->kuf/dot_general | solution.py:170
  13.5 1.0 fusion.38
  14.6 9.4 %subtract_convert_fusion = (bf16[32,64,1024]{2,1,0:T(8,128)(2,1)}, bf16[32,64,1024]{2,1,0:T(8,128)(2,1)}) fusion(f32[32,128,1024]{2,1,0:T(8,128)} %convolution_bitcast_fusion, f32[64,1024]{1,0:T(8,128)S(1)} %get-tuple-element.16, f32[64,1024]{1,0:T(8,128)S(1)} %get-tuple-element.15), kind=kLoop, calls=%fused_computation.16 | loop fusion | flops 16777216 | bytes 25690112 | tf_op jit(solution)/shard_map/convert_element_type | solution.py:173
  23.9 8.2 %pad_maximum_fusion = bf16[32,64,2048]{2,1,0:T(8,128)(2,1)} fusion(bf16[32,64,1024]{2,1,0:T(8,128)(2,1)} %get-tuple-element.6, bf16[32,64,1024]{2,1,0:T(8,128)(2,1)} %get-tuple-element.5), kind=kLoop, calls=%fused_computation.12 | loop fusion | flops 16777216 | bytes 16777216 | tf_op jit(solution)/shard_map/concatenate | solution.py:175
  32.1 2.5 %sine_convert_fusion = (bf16[1024,128]{1,0:T(8,128)(2,1)S(1)}, bf16[1024,128]{1,0:T(8,128)(2,1)S(1)}) fusion(s32[128]{0:T(128)S(1)} %iota_add_fusion.1, s32[1024]{0:T(1024)S(1)} %iota_add_fusion), kind=kLoop, calls=%fused_computation.40 | loop fusion | flops 2097152 | bytes 528896 | tf_op jit(solution)/shard_map/convert_element_type | solution.py:32
  34.6 2.5 %fusion.39 = bf16[1024,128]{1,0:T(8,128)(2,1)S(1)} fusion(s32[128]{0:T(128)S(1)} %iota_add_fusion.1, s32[1024]{0:T(1024)S(1)} %iota_add_fusion), kind=kLoop, calls=%fused_computation.64 | loop fusion | flops 2359296 | bytes 266752 | tf_op jit(solution)/shard_map/neg | solution.py:34
  37.0 10.5 %fusion.11.x_ref = f32[64,32,256]{2,1,0:T(8,128)} fusion(bf16[32,64,2048]{2,1,0:T(8,128)(2,1)} %pad_maximum_fusion, bf16[1024,128]{1,0:T(8,128)(2,1)S(1)} %get-tuple-element.14, bf16[1024,128]{1,0:T(8,128)(2,1)S(1)} %fusion.39, bf16[1024,128]{1,0:T(8,128)(2,1)S(1)} %get-tuple-element.13), kind=kOutput, calls=%fused_computation.22 | convolution fusion | flops 2151677952 | bytes 11272192 | tf_op jit(solution)/shard_map/ktf,fs->tks/dot_general | solution.py:178
  47.6 32.7 %shard_map.37.x_ref = bf16[4,32,256]{2,1,0:T(8,128)(2,1)} custom-call(f32[64,32,256]{2,1,0:T(8,128)} %fusion.11.x_ref), custom_call_target="tpu_custom_call" | custom-call | tf_op jit(solution)/shard_map/pallas_call | solution.py:96
  80.3 35.0 %shard_map.38 = bf16[16,4,32,256]{3,2,1,0:T(8,128)(2,1)} custom-call(bf16[4,32,256]{2,1,0:T(8,128)(2,1)} %shard_map.37.x_ref), custom_call_target="tpu_custom_call" | custom-call | tf_op jit(solution)/shard_map/pallas_call | solution.py:143
  115.2 0.0 copy-start
  115.2 2.8 %fusion.55 = (bf16[1,1024,512]{2,1,0:T(8,128)(2,1)S(1)}, bf16[1,1024,512]{2,1,0:T(8,128)(2,1)}) fusion(bf16[2,1024,512]{2,1,0:T(8,128)(2,1)} %param.5), kind=kLoop, calls=%fused_computation.85 | loop fusion | bytes 4194304 | tf_op jit(solution)/shard_map/slice | solution.py:186
  118.0 0.5 copy.5
  118.6 3.1 %fusion.29 = f32[4,128,1024,1]{2,1,0,3:T(8,128)} fusion(bf16[1024,16,32,1]{0,2,3,1:T(8,128)(2,1)S(1)} %bitcast.64, bf16[16,4,32,256]{3,2,1,0:T(8,128)(2,1)} %shard_map.38), kind=kOutput, calls=%fused_computation.46 | convolution fusion | flops 536870912 | bytes 3670016 | tf_op jit(solution)/shard_map/jgk,gtks->tjs/dot_general | solution.py:188
  121.7 1.5 %copy.7 = bf16[1,1024,512]{1,2,0:T(8,128)(2,1)S(1)} copy(bf16[1,1024,512]{2,1,0:T(8,128)(2,1)} %get-tuple-element.10) | data formatting | bytes 2097152 | tf_op jit(solution)/shard_map/slice | solution.py:187
  123.2 0.0 copy-done
  123.2 2.3 %fusion.14 = bf16[1,4,1024,128]{2,3,1,0:T(8,128)(2,1)S(1)} fusion(bf16[1024,16,32,1]{0,2,3,1:T(8,128)(2,1)S(1)} %bitcast.66, f32[4,128,1024,1]{2,1,0,3:T(8,128)} %fusion.29, bf16[16,4,32,256]{3,2,1,0:T(8,128)(2,1)S(1)} %copy-done), kind=kOutput, calls=%fused_computation.23 | convolution fusion | flops 537919488 | bytes 4718592 | tf_op jit(solution)/shard_map/jgk,gtks->tjs/dot_general | solution.py:190
  125.5 0.7 fusion.25
  126.2 0.7 fusion.15
  127.0 0.2 pad_maximum_fusion.1
  127.2 2.6 %copy.11 = bf16[2,4,1024,128]{3,2,1,0:T(8,128)(2,1)} copy(bf16[2,4,1024,128]{2,3,1,0:T(8,128)(2,1)S(1)} %pad_maximum_fusion.1) | data formatting | bytes 4194304 | tf_op jit(solution)/shard_map/stack | solution.py:195
  (2 shorter events, 0.0 us)
Async XLA Ops:
  115.2 7.9 %copy-start = (bf16[16,4,32,256]{3,2,1,0:T(8,128)(2,1)S(1)}, bf16[16,4,32,256]{3,2,1,0:T(8,128)(2,1)}, u32[]{:S(2)}) copy-start(bf16[16,4,32,256]{3,2,1,0:T(8,128)(2,1)} %shard_map.38) | copy-start | bytes 3145732

commit v2 on v1

--- a/solution.py
+++ b/solution.py
@@ -153,6 +153,54 @@
     )(x)
 
 
+def front_kernel(spec_ref, filt_ref, table_ref, tcos_ref, tsin_ref, wave_ref, o_ref, quarter):
+    block, inner = filt_ref.shape[1], filt_ref.shape[2]
+    spec_real = spec_ref[0]
+    spec_imag = spec_ref[1]
+    table = table_ref[...]
+    twist_cos = tcos_ref[...]
+    twist_sin = tsin_ref[...]
+    for kk in range(block):
+        filt_real = filt_ref[0, kk].astype(jnp.float32)
+        filt_imag = filt_ref[1, kk].astype(jnp.float32)
+        prod_real = spec_real * filt_real + spec_imag * filt_imag
+        prod_imag = spec_imag * filt_real - spec_real * filt_imag
+        packed = jnp.concatenate([prod_real, prod_imag], axis=0).astype(jnp.bfloat16)
+        section = jnp.dot(table, packed, preferred_element_type=jnp.float32)
+        section_real = section[:inner]
+        section_imag = section[inner:]
+        quarter_real = section_real * twist_cos - section_imag * twist_sin
+        quarter_imag = section_real * twist_sin + section_imag * twist_cos
+        width = quarter_real.shape[1]
+        rows = pl.ds(kk * inner, inner)
+        quarter[rows, pl.ds(0, width)] = quarter_real.astype(jnp.bfloat16)
+        quarter[rows, pl.ds(width, width)] = quarter_imag.astype(jnp.bfloat16)
+    result = jnp.dot(quarter[...], wave_ref[...], preferred_element_type=jnp.float32)
+    o_ref[...] = result.reshape(o_ref.shape)
+
+
+def front(spectrum, filters, table, twist_cos, twist_sin, wave, block=8):
+    _, basis, inner, freq = filters.shape
+    cols = wave.shape[1]
+    whole = lambda *shape: pl.BlockSpec(shape, lambda i: (0,) * len(shape))
+    return pl.pallas_call(
+        front_kernel,
+        grid=(basis // block,),
+        out_shape=jax.ShapeDtypeStruct((basis, inner, cols), jnp.float32),
+        in_specs=[
+            whole(2, inner, freq),
+            pl.BlockSpec((2, block, inner, freq), lambda i: (0, i, 0, 0)),
+            whole(2 * inner, 2 * inner),
+            whole(inner, freq),
+            whole(inner, freq),
+            whole(2 * freq, cols),
+        ],
+        out_specs=pl.BlockSpec((block, inner, cols), lambda i: (i, 0, 0)),
+        scratch_shapes=[pltpu.VMEM((block * inner, 2 * freq), jnp.bfloat16)],
+        compiler_params=pltpu.CompilerParams(vmem_limit_bytes=48 * 1024 * 1024),
+    )(spectrum, filters, table, twist_cos, twist_sin, wave)
+
+
 def on_device(spectrum, filters, mixing):
     tm_index = lax.axis_index("tm")
     local_freq = filters.shape[3]
@@ -162,20 +210,9 @@
     table = first_table(inner)
     freqs = tm_index * local_freq + jnp.arange(local_freq, dtype=jnp.int32)
     twist_cos, twist_sin = twist_tables(freqs, inner, NSAMP)
-    filt_real = filters[0].astype(jnp.float32)
-    filt_imag = filters[1].astype(jnp.float32)
-    prod_real = spectrum[0] * filt_real + spectrum[1] * filt_imag
-    prod_imag = spectrum[1] * filt_real - spectrum[0] * filt_imag
-    packed = jnp.concatenate([prod_real, prod_imag], axis=1).astype(jnp.bfloat16)
-    section = jnp.einsum("uv,kvf->kuf", table, packed, preferred_element_type=jnp.float32)
-    section_real = section[:, :inner]
-    section_imag = section[:, inner:]
-    quarter_real = (section_real * twist_cos - section_imag * twist_sin).astype(jnp.bfloat16)
-    quarter_imag = (section_real * twist_sin + section_imag * twist_cos).astype(jnp.bfloat16)
-    quarter = jnp.concatenate([quarter_real, quarter_imag], axis=2)
     lags = START + jnp.arange(WROWS, dtype=jnp.int32)
     wave = wave_block(freqs, lags, outer)
-    partial = jnp.einsum("ktf,fs->tks", quarter, wave, preferred_element_type=jnp.float32)
+    partial = front(spectrum, filters, table, twist_cos, twist_sin, wave).transpose(1, 0, 2)
     series = scatter_sum(partial, lax.axis_size("tm"))
     piece = gather(series, lax.axis_size("bank"))
     groups = piece.shape[0]

time: 130 us -> 96.5 us (0.74)
  other arithmetic: 29 us -> 6.5 us
  matrix products: 24.5 us -> 2.92 us
  Pallas kernels: 67.7 us -> 78.6 us
    dot_general x2 -> x0, matrix products: 17.6 us -> none  [the longest x1 10.5 us: on_device(): jnp.einsum('ktf,fs->tks', quarter, wave, preferred_element_type=jnp.float32)]
    pallas_call x0 -> x1, Pallas kernels: none -> 10.8 us  [front(): pl.pallas_call(front_kernel, grid=(basis // block,), out_shape=jax.ShapeD...]
    convert_element_type x1 -> x0, other arithmetic: 9.36 us -> none  [on_device(): (section_real * twist_cos - section_imag * twist_sin).astype(jnp.bfloat16)]
    concatenate x1 -> x2, other arithmetic: 8.17 us -> 0.2 us  [the longest x1 0.11 us: wave_block(): return jnp.concatenate([upper, lower], axis=0)]
    another operation x1 -> x0, other arithmetic: 5.03 us -> none
    pallas_call x0 -> x1, local copies, waits for them, and re-layouts: none -> 2.54 us  [front(): pl.pallas_call(front_kernel, grid=(basis // block,), out_shape=jax.ShapeD...]
    dot_general x1, matrix products: 3.09 us -> 0.73 us  [on_device(): jnp.einsum('jgk,gtks->tjs', mix_real, piece_real, preferred_element_type=...]
    slice x2, local copies, waits for them, and re-layouts: 3.32 us -> 1.63 us  [on_device(): mix_real = mixing[0].reshape(templates, groups, local_basis)]
where the time goes in v2:
time: 96.5 us; the launch traced here: 96.4 us
  Pallas kernels  78.6 us (81%)
  local copies, waits for them, and re-layouts  8.23 us (9%)
  other arithmetic  6.5 us (7%)
  matrix products  2.92 us (3%)
    pallas_call x1, Pallas kernels, gather(): pl.pallas_call(functools.partial(gather_kernel, n), out_shape=jax.ShapeDt...  35 us
    pallas_call x1, Pallas kernels, scatter_sum(): pl.pallas_call(functools.partial(scatter_sum_kernel, n), out_shape=jax.Sh...  32.9 us
    pallas_call x1, Pallas kernels, front(): pl.pallas_call(front_kernel, grid=(basis // block,), out_shape=jax.ShapeD...  10.8 us
    another operation x1, local copies, waits for them, and re-layouts, on_device(): return jnp.stack([real_sum, imag_sum], axis=0).astype(jnp.bfloat16)  2.56 us
    pallas_call x1, local copies, waits for them, and re-layouts, front(): pl.pallas_call(front_kernel, grid=(basis // block,), out_shape=jax.ShapeD...  2.54 us
    convert_element_type x1, other arithmetic, wave_block(): sine = jnp.sin(angle).astype(jnp.bfloat16)  2.48 us
    neg x1, other arithmetic, wave_block(): lower = jnp.concatenate([-sine, cosine], axis=1)  2.29 us

profile of v2, /device:TPU:1, one launch (start us, length us, event | category | flops | bytes accessed | tf_op | source)
XLA Modules:
  0.0 96.4 jit_solution(14883802761922726464)
XLA Ops:
  0.0 0.0 copy-start
  0.0 0.1 fusion.28
  0.2 0.2 sine_convert_fusion.1
  0.3 0.1 maximum_maximum_fusion.1.table_ref
  0.4 2.3 %fusion.21 = bf16[1024,128]{1,0:T(8,128)(2,1)S(1)} fusion(s32[128]{0:T(128)S(1)} %iota_add_fusion.1, s32[1024]{0:T(1024)S(1)} %iota_add_fusion), kind=kLoop, calls=%fused_computation.39 | loop fusion | flops 2359296 | bytes 266752 | tf_op jit(solution)/shard_map/neg | solution.py:34
  2.7 2.5 %sine_convert_fusion = (bf16[1024,128]{1,0:T(8,128)(2,1)S(1)}, bf16[1024,128]{1,0:T(8,128)(2,1)S(1)}) fusion(s32[128]{0:T(128)S(1)} %iota_add_fusion.1, s32[1024]{0:T(1024)S(1)} %iota_add_fusion), kind=kLoop, calls=%fused_computation.17 | loop fusion | flops 2097152 | bytes 528896 | tf_op jit(solution)/shard_map/convert_element_type | solution.py:32
  5.2 0.1 maximum_maximum_fusion.wave_ref
  5.3 1.0 %fusion.19 = (f32[64,1024]{1,0:T(8,128)S(1)}, f32[64,1024]{1,0:T(8,128)S(1)}) fusion(s32[1024]{0:T(1024)S(1)} %iota_add_fusion), kind=kLoop, calls=%fused_computation.34 | loop fusion | flops 917504 | bytes 528384 | tf_op jit(solution)/shard_map/sin | solution.py:42
  6.3 0.0 copy-done
  6.4 10.8 %shard_map.37 = f32[32,64,256]{2,1,0:T(8,128)S(1)} custom-call(f32[2,64,1024]{2,1,0:T(8,128)S(1)} %copy-done, bf16[2,32,64,1024]{3,2,1,0:T(8,128)(2,1)} %filt_ref.1, bf16[128,128]{1,0:T(8,128)(2,1)S(1)} %maximum_maximum_fusion.1.table_ref, f32[64,1024]{1,0:T(8,128)S(1)} %get-tuple-element.10.tcos_ref, f32[64,1024]{1,0:T(8,128)S(1)} %get-tuple-element.9.tsin_ref, ...), custom_call_target="tpu_custom_call" | custom-call | tf_op jit(solution)/shard_map/pallas_call | solution.py:186
  17.1 2.5 %copy.19 = f32[32,64,256]{2,0,1:T(8,128)} copy(f32[32,64,256]{2,1,0:T(8,128)S(1)} %shard_map.37) | data formatting | bytes 4194304 | tf_op jit(solution)/shard_map/pallas_call | solution.py:186
  19.7 32.9 %shard_map.38.x_ref = bf16[4,32,256]{2,1,0:T(8,128)(2,1)} custom-call(f32[64,32,256]{2,1,0:T(8,128)} %bitcast.49), custom_call_target="tpu_custom_call" | custom-call | tf_op jit(solution)/shard_map/pallas_call | solution.py:96
  52.5 35.0 %shard_map.39 = bf16[16,4,32,256]{3,2,1,0:T(8,128)(2,1)} custom-call(bf16[4,32,256]{2,1,0:T(8,128)(2,1)} %shard_map.38.x_ref), custom_call_target="tpu_custom_call" | custom-call | tf_op jit(solution)/shard_map/pallas_call | solution.py:143
  87.5 0.0 copy-done.2
  87.5 1.1 %fusion.29 = (bf16[1,1024,512]{2,1,0:T(8,128)(2,1)S(1)}, bf16[1,1024,512]{2,1,0:T(8,128)(2,1)}) fusion(bf16[2,1024,512]{2,1,0:T(8,128)(2,1)S(1)} %copy-done.2), kind=kLoop, calls=%fused_computation.52 | loop fusion | bytes 4194304 | tf_op jit(solution)/shard_map/slice | solution.py:223
  88.6 0.5 copy.5
  89.2 1.5 %copy.7 = bf16[1,1024,512]{1,2,0:T(8,128)(2,1)S(1)} copy(bf16[1,1024,512]{2,1,0:T(8,128)(2,1)} %get-tuple-element.6) | data formatting | bytes 2097152 | tf_op jit(solution)/shard_map/slice | solution.py:224
  90.7 0.0 copy-done.1
  90.7 0.7 fusion.7
  91.4 0.7 fusion.3
  92.1 0.7 fusion.11
  92.9 0.7 fusion.2
  93.6 0.2 pad_maximum_fusion
  93.8 2.6 %copy.11 = bf16[2,4,1024,128]{3,2,1,0:T(8,128)(2,1)} copy(bf16[2,4,1024,128]{2,3,1,0:T(8,128)(2,1)S(1)} %pad_maximum_fusion) | data formatting | bytes 4194304 | tf_op jit(solution)/shard_map/stack | solution.py:232
  (4 shorter events, 0.0 us)
Async XLA Ops:
  0.0 6.3 %copy-start = (f32[2,64,1024]{2,1,0:T(8,128)S(1)}, f32[2,64,1024]{2,1,0:T(8,128)}, u32[]{:S(2)}) copy-start(f32[2,64,1024]{2,1,0:T(8,128)} %spec_ref.1) | copy-start | bytes 1572868
  19.7 67.8 %copy-start.2 = (bf16[2,1024,512]{2,1,0:T(8,128)(2,1)S(1)}, bf16[2,1024,512]{2,1,0:T(8,128)(2,1)}, u32[]{:S(2)}) copy-start(bf16[2,1024,512]{2,1,0:T(8,128)(2,1)} %param.5) | copy-start | bytes 6291460
  88.6 2.0 %copy-start.1 = (bf16[16,4,32,256]{3,2,1,0:T(8,128)(2,1)S(1)}, bf16[16,4,32,256]{3,2,1,0:T(8,128)(2,1)}, u32[]{:S(2)}) copy-start(bf16[16,4,32,256]{3,2,1,0:T(8,128)(2,1)} %shard_map.39) | copy-start | bytes 3145732

commit v3 on v2

--- a/solution.py
+++ b/solution.py
@@ -73,7 +73,7 @@
         )
         copy.start()
         sends.append(copy)
-    total = x_ref[pl.ds(me * rows, rows)]
+    total = x_ref[pl.ds(me * rows, rows)].astype(jnp.float32)
     for step in range(1, n):
         source = (me + n - step) % n
         pltpu.make_async_remote_copy(
@@ -84,7 +84,7 @@
             device_id=place(source),
             device_id_type=MESH,
         ).wait_recv()
-        total = total + slots[source]
+        total = total + slots[source].astype(jnp.float32)
     for copy in sends:
         copy.wait_send()
     o_ref[...] = total.astype(o_ref.dtype)
@@ -176,7 +176,7 @@
         quarter[rows, pl.ds(0, width)] = quarter_real.astype(jnp.bfloat16)
         quarter[rows, pl.ds(width, width)] = quarter_imag.astype(jnp.bfloat16)
     result = jnp.dot(quarter[...], wave_ref[...], preferred_element_type=jnp.float32)
-    o_ref[...] = result.reshape(o_ref.shape)
+    o_ref[...] = result.reshape(o_ref.shape).astype(o_ref.dtype)
 
 
 def front(spectrum, filters, table, twist_cos, twist_sin, wave, block=8):
@@ -186,7 +186,7 @@
     return pl.pallas_call(
         front_kernel,
         grid=(basis // block,),
-        out_shape=jax.ShapeDtypeStruct((basis, inner, cols), jnp.float32),
+        out_shape=jax.ShapeDtypeStruct((basis, inner, cols), jnp.bfloat16),
         in_specs=[
             whole(2, inner, freq),
             pl.BlockSpec((2, block, inner, freq), lambda i: (0, i, 0, 0)),

time: 96.5 us -> 82.8 us (0.86)
  the two profiles are of different devices: /device:TPU:1 before, /device:TPU:25 now
where the time goes in v3:
time: 82.8 us; the launch traced here: 82.7 us
  Pallas kernels  65.9 us (80%)
  local copies, waits for them, and re-layouts  7.25 us (9%)
  other arithmetic  6.5 us (8%)
  matrix products  2.91 us (4%)
    pallas_call x1, Pallas kernels, gather(): pl.pallas_call(functools.partial(gather_kernel, n), out_shape=jax.ShapeDt...  35.9 us
    pallas_call x1, Pallas kernels, scatter_sum(): pl.pallas_call(functools.partial(scatter_sum_kernel, n), out_shape=jax.Sh...  19.2 us
    pallas_call x1, Pallas kernels, front(): pl.pallas_call(front_kernel, grid=(basis // block,), out_shape=jax.ShapeD...  10.8 us
    another operation x1, local copies, waits for them, and re-layouts, on_device(): return jnp.stack([real_sum, imag_sum], axis=0).astype(jnp.bfloat16)  2.56 us
    convert_element_type x1, other arithmetic, wave_block(): sine = jnp.sin(angle).astype(jnp.bfloat16)  2.48 us
    neg x1, other arithmetic, wave_block(): lower = jnp.concatenate([-sine, cosine], axis=1)  2.29 us

profile of v3, /device:TPU:25, one launch (start us, length us, event | category | flops | bytes accessed | tf_op | source)
XLA Modules:
  0.0 82.7 jit_solution(11457512612694748)
XLA Ops:
  0.0 0.1 fusion.28
  0.2 0.2 sine_convert_fusion.1
  0.3 0.1 maximum_maximum_fusion.1.table_ref
  0.4 2.3 %fusion.21 = bf16[1024,128]{1,0:T(8,128)(2,1)S(1)} fusion(s32[128]{0:T(128)S(1)} %iota_add_fusion.1, s32[1024]{0:T(1024)S(1)} %iota_add_fusion), kind=kLoop, calls=%fused_computation.39 | loop fusion | flops 2359296 | bytes 266752 | tf_op jit(solution)/shard_map/neg | solution.py:34
  2.7 2.5 %sine_convert_fusion = (bf16[1024,128]{1,0:T(8,128)(2,1)S(1)}, bf16[1024,128]{1,0:T(8,128)(2,1)S(1)}) fusion(s32[128]{0:T(128)S(1)} %iota_add_fusion.1, s32[1024]{0:T(1024)S(1)} %iota_add_fusion), kind=kLoop, calls=%fused_computation.17 | loop fusion | flops 2097152 | bytes 528896 | tf_op jit(solution)/shard_map/convert_element_type | solution.py:32
  5.2 0.1 maximum_maximum_fusion.wave_ref
  5.3 1.0 %fusion.19 = (f32[64,1024]{1,0:T(8,128)S(1)}, f32[64,1024]{1,0:T(8,128)S(1)}) fusion(s32[1024]{0:T(1024)S(1)} %iota_add_fusion), kind=kLoop, calls=%fused_computation.34 | loop fusion | flops 917504 | bytes 528384 | tf_op jit(solution)/shard_map/sin | solution.py:42
  6.3 0.0 copy-done
  6.4 10.8 %shard_map.37 = bf16[32,64,256]{2,1,0:T(8,128)(2,1)S(1)} custom-call(f32[2,64,1024]{2,1,0:T(8,128)S(1)} %copy-done, bf16[2,32,64,1024]{3,2,1,0:T(8,128)(2,1)} %filt_ref.1, bf16[128,128]{1,0:T(8,128)(2,1)S(1)} %maximum_maximum_fusion.1.table_ref, f32[64,1024]{1,0:T(8,128)S(1)} %get-tuple-element.10.tcos_ref, f32[64,1024]{1,0:T(8,128)S(1)} %get-tuple-element.9.tsin_ref, ...), custom_call_target="tpu_custom_call" | custom-call | tf_op jit(solution)/shard_map/pallas_call | solution.py:186
  17.1 0.0 copy-start.2
  17.2 1.6 %copy.19 = bf16[32,64,256]{2,0,1:T(8,128)(2,1)} copy(bf16[32,64,256]{2,1,0:T(8,128)(2,1)S(1)} %shard_map.37) | data formatting | bytes 2097152 | tf_op jit(solution)/shard_map/pallas_call | solution.py:186
  18.7 19.2 %shard_map.38.x_ref = bf16[4,32,256]{2,1,0:T(8,128)(2,1)} custom-call(bf16[64,32,256]{2,1,0:T(8,128)(2,1)} %bitcast.49), custom_call_target="tpu_custom_call" | custom-call | tf_op jit(solution)/shard_map/pallas_call | solution.py:96
  37.9 35.9 %shard_map.39 = bf16[16,4,32,256]{3,2,1,0:T(8,128)(2,1)} custom-call(bf16[4,32,256]{2,1,0:T(8,128)(2,1)} %shard_map.38.x_ref), custom_call_target="tpu_custom_call" | custom-call | tf_op jit(solution)/shard_map/pallas_call | solution.py:143
  73.8 0.0 copy-done.2
  73.8 1.1 %fusion.29 = (bf16[1,1024,512]{2,1,0:T(8,128)(2,1)S(1)}, bf16[1,1024,512]{2,1,0:T(8,128)(2,1)}) fusion(bf16[2,1024,512]{2,1,0:T(8,128)(2,1)S(1)} %copy-done.2), kind=kLoop, calls=%fused_computation.52 | loop fusion | bytes 4194304 | tf_op jit(solution)/shard_map/slice | solution.py:223
  75.0 0.5 copy.5
  75.5 1.5 %copy.7 = bf16[1,1024,512]{1,2,0:T(8,128)(2,1)S(1)} copy(bf16[1,1024,512]{2,1,0:T(8,128)(2,1)} %get-tuple-element.6) | data formatting | bytes 2097152 | tf_op jit(solution)/shard_map/slice | solution.py:224
  77.0 0.0 copy-done.1
  77.0 0.7 fusion.7
  77.7 0.7 fusion.3
  78.5 0.7 fusion.11
  79.2 0.7 fusion.2
  79.9 0.2 pad_maximum_fusion
  80.1 2.6 %copy.11 = bf16[2,4,1024,128]{3,2,1,0:T(8,128)(2,1)} copy(bf16[2,4,1024,128]{2,3,1,0:T(8,128)(2,1)S(1)} %pad_maximum_fusion) | data formatting | bytes 4194304 | tf_op jit(solution)/shard_map/stack | solution.py:232
  (4 shorter events, 0.0 us)
Async XLA Ops:
  0.0 6.3 %copy-start = (f32[2,64,1024]{2,1,0:T(8,128)S(1)}, f32[2,64,1024]{2,1,0:T(8,128)}, u32[]{:S(2)}) copy-start(f32[2,64,1024]{2,1,0:T(8,128)} %spec_ref.1) | copy-start | bytes 1572868
  17.1 56.7 %copy-start.2 = (bf16[2,1024,512]{2,1,0:T(8,128)(2,1)S(1)}, bf16[2,1024,512]{2,1,0:T(8,128)(2,1)}, u32[]{:S(2)}) copy-start(bf16[2,1024,512]{2,1,0:T(8,128)(2,1)} %param.5) | copy-start | bytes 6291460
  74.9 2.0 %copy-start.1 = (bf16[16,4,32,256]{3,2,1,0:T(8,128)(2,1)S(1)}, bf16[16,4,32,256]{3,2,1,0:T(8,128)(2,1)}, u32[]{:S(2)}) copy-start(bf16[16,4,32,256]{3,2,1,0:T(8,128)(2,1)} %shard_map.39) | copy-start | bytes 3145732

commit v4 on v3

--- a/solution.py
+++ b/solution.py
@@ -107,47 +107,73 @@
     )(x)
 
 
-def gather_kernel(n, x_ref, o_ref, send_sem, recv_sem):
+def gather_kernel(width, x_ref, o_ref, own_sem, send_sem, recv_sem):
+    n = lax.axis_size("bank")
+    depth = n // width
+    half = width // 2
     tm = lax.axis_index("tm")
-    place = lambda peer: (tm, peer)
-    me = greet("bank", n, place)
+    bank = lax.axis_index("bank")
+    x = bank // depth
+    z = bank % depth
+    up = (z + 1) % depth
+    down = (z + depth - 1) % depth
+    across = (z + 2) % depth
+    place = lambda xx, zz: (tm, xx * depth + zz)
+    peers = [place((x + d) % width, z) for d in range(1, width)] + [place(x, up), place(x, down)]
+    barrier = pltpu.get_barrier_semaphore()
+    for peer in peers:
+        pl.semaphore_signal(barrier, inc=1, device_id=peer, device_id_type=MESH)
+    pl.semaphore_wait(barrier, len(peers))
+
+    def remote(src, dst, send, recv, device):
+        return pltpu.make_async_remote_copy(
+            src_ref=src, dst_ref=dst, send_sem=send_sem.at[send], recv_sem=recv_sem.at[recv],
+            device_id=device, device_id_type=MESH,
+        )
+
+    own = pltpu.make_async_copy(x_ref, o_ref.at[z * width + x], own_sem)
+    own.start()
     sends = []
-    for step in range(1, n):
-        peer = (me + step) % n
-        copy = pltpu.make_async_remote_copy(
-            src_ref=x_ref,
-            dst_ref=o_ref.at[me],
-            send_sem=send_sem.at[peer],
-            recv_sem=recv_sem.at[me],
-            device_id=place(peer),
-            device_id_type=MESH,
-        )
-        copy.start()
-        sends.append(copy)
-    o_ref[me] = x_ref[...]
-    for step in range(1, n):
-        source = (me + n - step) % n
-        pltpu.make_async_remote_copy(
-            src_ref=x_ref,
-            dst_ref=o_ref.at[source],
-            send_sem=send_sem.at[source],
-            recv_sem=recv_sem.at[source],
-            device_id=place(source),
-            device_id_type=MESH,
-        ).wait_recv()
+    for d in range(1, width):
+        xx = (x + d) % width
+        copy = remote(x_ref, o_ref.at[z * width + x], d - 1, x, place(xx, z))
+        copy.start()
+        sends.append(copy)
+    own.wait()
+    for d in range(1, width):
+        xx = (x + d) % width
+        remote(x_ref, o_ref.at[z * width + xx], d - 1, xx, place(xx, z)).wait_recv()
+    row = lambda zz, start, size: o_ref.at[pl.ds(zz * width + start, size)]
+    for slot, (target, step) in enumerate(((up, width - 1), (down, width))):
+        copy = remote(row(z, 0, width), row(z, 0, width), step, width + slot, place(x, target))
+        copy.start()
+        sends.append(copy)
+    remote(row(down, 0, width), row(down, 0, width), width - 1, width, place(x, down)).wait_recv()
+    remote(row(up, 0, width), row(up, 0, width), width, width + 1, place(x, up)).wait_recv()
+    forwards = (
+        (row(down, 0, half), up, width + 1, width + 2),
+        (row(up, half, half), down, width + 2, width + 3),
+    )
+    for src, target, send, recv in forwards:
+        copy = remote(src, src, send, recv, place(x, target))
+        copy.start()
+        sends.append(copy)
+    remote(row(across, 0, half), row(across, 0, half), width + 1, width + 2, place(x, down)).wait_recv()
+    remote(row(across, half, half), row(across, half, half), width + 2, width + 3, place(x, up)).wait_recv()
     for copy in sends:
         copy.wait_send()
 
 
-def gather(x, n):
+def gather(x, n, width):
     return pl.pallas_call(
-        functools.partial(gather_kernel, n),
+        functools.partial(gather_kernel, width),
         out_shape=jax.ShapeDtypeStruct((n,) + x.shape, x.dtype),
         in_specs=[pl.BlockSpec(memory_space=pltpu.VMEM)],
         out_specs=pl.BlockSpec(memory_space=pltpu.VMEM),
         scratch_shapes=[
-            pltpu.SemaphoreType.DMA((n,)),
-            pltpu.SemaphoreType.DMA((n,)),
+            pltpu.SemaphoreType.DMA(()),
+            pltpu.SemaphoreType.DMA((width + 3,)),
+            pltpu.SemaphoreType.DMA((width + 4,)),
         ],
         compiler_params=pltpu.CompilerParams(collective_id=1, has_side_effects=True),
     )(x)
@@ -214,7 +240,10 @@
     wave = wave_block(freqs, lags, outer)
     partial = front(spectrum, filters, table, twist_cos, twist_sin, wave).transpose(1, 0, 2)
     series = scatter_sum(partial, lax.axis_size("tm"))
-    piece = gather(series, lax.axis_size("bank"))
+    width = 4
+    slots = gather(series, lax.axis_size("bank"), width)
+    depth = slots.shape[0] // width
+    piece = slots.reshape((depth, width) + slots.shape[1:]).swapaxes(0, 1).reshape(slots.shape)
     groups = piece.shape[0]
     rows = piece.shape[1]
     piece_real = piece[..., :WROWS]

time: 82.8 us -> 86 us (1.039)
  the two profiles are of different devices: /device:TPU:25 before, /device:TPU:16 now
where the time goes in v4:
time: 86 us; the launch traced here: 85.7 us
  Pallas kernels  66.1 us (77%)
  local copies, waits for them, and re-layouts  10.1 us (12%)
  other arithmetic  6.5 us (8%)
  matrix products  2.92 us (3%)
    pallas_call x1, Pallas kernels, gather(): pl.pallas_call(functools.partial(gather_kernel, width), out_shape=jax.Sha...  37.3 us
    pallas_call x1, Pallas kernels, scatter_sum(): pl.pallas_call(functools.partial(scatter_sum_kernel, n), out_shape=jax.Sh...  18 us
    pallas_call x1, Pallas kernels, front(): pl.pallas_call(front_kernel, grid=(basis // block,), out_shape=jax.ShapeD...  10.8 us
    slice x2, local copies, waits for them, and re-layouts, on_device(): mix_real = mixing[0].reshape(templates, groups, local_basis)  3.17 us
    another operation x1, local copies, waits for them, and re-layouts, on_device(): return jnp.stack([real_sum, imag_sum], axis=0).astype(jnp.bfloat16)  2.56 us
    convert_element_type x1, other arithmetic, wave_block(): sine = jnp.sin(angle).astype(jnp.bfloat16)  2.48 us
    neg x1, other arithmetic, wave_block(): lower = jnp.concatenate([-sine, cosine], axis=1)  2.29 us

profile of v4, /device:TPU:16, one launch (start us, length us, event | category | flops | bytes accessed | tf_op | source)
XLA Modules:
  0.0 85.7 jit_solution(18061785975095095072)
XLA Ops:
  0.0 0.0 copy-start
  0.0 0.1 fusion.28
  0.2 0.2 sine_convert_fusion.1
  0.3 0.1 maximum_maximum_fusion.1.table_ref
  0.4 2.3 %fusion.21 = bf16[1024,128]{1,0:T(8,128)(2,1)S(1)} fusion(s32[128]{0:T(128)S(1)} %iota_add_fusion.1, s32[1024]{0:T(1024)S(1)} %iota_add_fusion), kind=kLoop, calls=%fused_computation.39 | loop fusion | flops 2359296 | bytes 266752 | tf_op jit(solution)/shard_map/neg | solution.py:34
  2.7 2.5 %sine_convert_fusion = (bf16[1024,128]{1,0:T(8,128)(2,1)S(1)}, bf16[1024,128]{1,0:T(8,128)(2,1)S(1)}) fusion(s32[128]{0:T(128)S(1)} %iota_add_fusion.1, s32[1024]{0:T(1024)S(1)} %iota_add_fusion), kind=kLoop, calls=%fused_computation.17 | loop fusion | flops 2097152 | bytes 528896 | tf_op jit(solution)/shard_map/convert_element_type | solution.py:32
  5.2 0.1 maximum_maximum_fusion.wave_ref
  5.3 1.0 %fusion.19 = (f32[64,1024]{1,0:T(8,128)S(1)}, f32[64,1024]{1,0:T(8,128)S(1)}) fusion(s32[1024]{0:T(1024)S(1)} %iota_add_fusion), kind=kLoop, calls=%fused_computation.34 | loop fusion | flops 917504 | bytes 528384 | tf_op jit(solution)/shard_map/sin | solution.py:42
  6.3 0.0 copy-done
  6.4 10.8 %shard_map.37 = bf16[32,64,256]{2,1,0:T(8,128)(2,1)S(1)} custom-call(f32[2,64,1024]{2,1,0:T(8,128)S(1)} %copy-done, bf16[2,32,64,1024]{3,2,1,0:T(8,128)(2,1)} %filt_ref.1, bf16[128,128]{1,0:T(8,128)(2,1)S(1)} %maximum_maximum_fusion.1.table_ref, f32[64,1024]{1,0:T(8,128)S(1)} %get-tuple-element.10.tcos_ref, f32[64,1024]{1,0:T(8,128)S(1)} %get-tuple-element.9.tsin_ref, ...), custom_call_target="tpu_custom_call" | custom-call | tf_op jit(solution)/shard_map/pallas_call | solution.py:212
  17.1 1.6 %copy.14 = bf16[32,64,256]{2,0,1:T(8,128)(2,1)} copy(bf16[32,64,256]{2,1,0:T(8,128)(2,1)S(1)} %shard_map.37) | data formatting | bytes 2097152 | tf_op jit(solution)/shard_map/pallas_call | solution.py:212
  18.7 18.0 %shard_map.38.x_ref = bf16[4,32,256]{2,1,0:T(8,128)(2,1)} custom-call(bf16[64,32,256]{2,1,0:T(8,128)(2,1)} %bitcast.57), custom_call_target="tpu_custom_call" | custom-call | tf_op jit(solution)/shard_map/pallas_call | solution.py:96
  36.7 37.3 %shard_map.39 = bf16[16,4,32,256]{3,2,1,0:T(8,128)(2,1)} custom-call(bf16[4,32,256]{2,1,0:T(8,128)(2,1)} %shard_map.38.x_ref), custom_call_target="tpu_custom_call" | custom-call | tf_op jit(solution)/shard_map/pallas_call | solution.py:168
  74.0 1.3 %copy.5 = bf16[4,4,4,32,256]{4,3,1,0,2:T(8,128)(2,1)S(1)} copy(bf16[4,4,4,32,256]{4,3,2,0,1:T(8,128)(2,1)} %bitcast.58) | data formatting | bytes 2097152 | tf_op jit(solution)/shard_map/transpose | solution.py:246
  75.4 2.6 %fusion.29 = (bf16[1,1024,512]{2,1,0:T(8,128)(2,1)S(1)}, bf16[1,1024,512]{2,1,0:T(8,128)(2,1)}) fusion(bf16[2,1024,512]{2,1,0:T(8,128)(2,1)} %param.5), kind=kLoop, calls=%fused_computation.52 | loop fusion | bytes 4194304 | tf_op jit(solution)/shard_map/slice | solution.py:252
  78.0 0.5 copy.6
  78.5 1.5 %copy.7 = bf16[1,1024,512]{1,2,0:T(8,128)(2,1)S(1)} copy(bf16[1,1024,512]{2,1,0:T(8,128)(2,1)} %get-tuple-element.6) | data formatting | bytes 2097152 | tf_op jit(solution)/shard_map/slice | solution.py:253
  80.0 0.7 fusion.7
  80.8 0.7 fusion.3
  81.5 0.7 fusion.11
  82.2 0.7 fusion.2
  83.0 0.2 pad_maximum_fusion
  83.2 2.6 %copy.8 = bf16[2,4,1024,128]{3,2,1,0:T(8,128)(2,1)} copy(bf16[2,4,1024,128]{2,3,1,0:T(8,128)(2,1)S(1)} %pad_maximum_fusion) | data formatting | bytes 4194304 | tf_op jit(solution)/shard_map/stack | solution.py:261
  (2 shorter events, 0.0 us)
Async XLA Ops:
  0.0 6.3 %copy-start = (f32[2,64,1024]{2,1,0:T(8,128)S(1)}, f32[2,64,1024]{2,1,0:T(8,128)}, u32[]{:S(2)}) copy-start(f32[2,64,1024]{2,1,0:T(8,128)} %spec_ref.1) | copy-start | bytes 1572868

commit v5 on v4

--- a/solution.py
+++ b/solution.py
@@ -177,6 +177,34 @@
         ],
         compiler_params=pltpu.CompilerParams(collective_id=1, has_side_effects=True),
     )(x)
+
+
+def mix_kernel(width, mix_ref, slots_ref, o_ref):
+    n, rows, _, cols = slots_ref.shape
+    depth = n // width
+    half = cols // 2
+    order = [z * width + x for x in range(width) for z in range(depth)]
+    mix_real = mix_ref[0]
+    mix_imag = mix_ref[1]
+    for t in range(rows):
+        plain = jnp.concatenate([slots_ref[slot, t] for slot in order], axis=0)
+        turned = jnp.concatenate([-plain[:, half:], plain[:, :half]], axis=1)
+        result = jnp.dot(mix_real, plain, preferred_element_type=jnp.float32) + jnp.dot(
+            mix_imag, turned, preferred_element_type=jnp.float32
+        )
+        o_ref[0, t] = result[:, :half].astype(o_ref.dtype)
+        o_ref[1, t] = result[:, half:].astype(o_ref.dtype)
+
+
+def mix(mixing, slots, width):
+    _, rows, _, cols = slots.shape
+    templates = mixing.shape[1]
+    return pl.pallas_call(
+        functools.partial(mix_kernel, width),
+        out_shape=jax.ShapeDtypeStruct((2, rows, templates, cols // 2), jnp.bfloat16),
+        in_specs=[pl.BlockSpec(memory_space=pltpu.VMEM)] * 2,
+        out_specs=pl.BlockSpec(memory_space=pltpu.VMEM),
+    )(mixing, slots)
 
 
 def front_kernel(spec_ref, filt_ref, table_ref, tcos_ref, tsin_ref, wave_ref, o_ref, quarter):
@@ -242,23 +270,7 @@
     series = scatter_sum(partial, lax.axis_size("tm"))
     width = 4
     slots = gather(series, lax.axis_size("bank"), width)
-    depth = slots.shape[0] // width
-    piece = slots.reshape((depth, width) + slots.shape[1:]).swapaxes(0, 1).reshape(slots.shape)
-    groups = piece.shape[0]
-    rows = piece.shape[1]
-    piece_real = piece[..., :WROWS]
-    piece_imag = piece[..., WROWS:]
-    templates = mixing.shape[1]
-    mix_real = mixing[0].reshape(templates, groups, local_basis)
-    mix_imag = mixing[1].reshape(templates, groups, local_basis)
-    real_sum = jnp.einsum(
-        "jgk,gtks->tjs", mix_real, piece_real, preferred_element_type=jnp.float32
-    ) - jnp.einsum("jgk,gtks->tjs", mix_imag, piece_imag, preferred_element_type=jnp.float32)
-    imag_sum = jnp.einsum(
-        "jgk,gtks->tjs", mix_real, piece_imag, preferred_element_type=jnp.float32
-    ) + jnp.einsum("jgk,gtks->tjs", mix_imag, piece_real, preferred_element_type=jnp.float32)
-    del rows
-    return jnp.stack([real_sum, imag_sum], axis=0).astype(jnp.bfloat16)
+    return mix(mixing, slots, width)
 
 
 def solution(mesh):

time: 86 us -> 79.7 us (0.927)
  local copies, waits for them, and re-layouts: 10.1 us -> 1.56 us
  Pallas kernels: 66.1 us -> 71.6 us
  matrix products: 2.92 us -> 0 us
    pallas_call x0 -> x1, Pallas kernels: none -> 5.51 us  [mix(): pl.pallas_call(functools.partial(mix_kernel, width), out_shape=jax.ShapeD...]
    slice x3 -> x0, local copies, waits for them, and re-layouts: 4.66 us -> none  [the longest x2 3.17 us: on_device(): mix_real = mixing[0].reshape(templates, groups, local_basis)]
    dot_general x4 -> x0, matrix products: 2.92 us -> none  [the longest x1 0.73 us: on_device(): jnp.einsum('jgk,gtks->tjs', mix_imag, piece_real, preferred_element_type=...]
    another operation x1 -> x0, local copies, waits for them, and re-layouts: 2.56 us -> none  [on_device(): return jnp.stack([real_sum, imag_sum], axis=0).astype(jnp.bfloat16)]
    transpose x1 -> x0, local copies, waits for them, and re-layouts: 1.31 us -> none  [on_device(): slots.reshape((depth, width) + slots.shape[1:]).swapaxes(0, 1)]
where the time goes in v5:
time: 79.7 us; the launch traced here: 79.5 us
  Pallas kernels  71.6 us (90%)
  other arithmetic  6.3 us (8%)
  local copies, waits for them, and re-layouts  1.56 us (2%)
    pallas_call x1, Pallas kernels, gather(): pl.pallas_call(functools.partial(gather_kernel, width), out_shape=jax.Sha...  37.3 us
    pallas_call x1, Pallas kernels, scatter_sum(): pl.pallas_call(functools.partial(scatter_sum_kernel, n), out_shape=jax.Sh...  18 us
    pallas_call x1, Pallas kernels, front(): pl.pallas_call(front_kernel, grid=(basis // block,), out_shape=jax.ShapeD...  10.8 us
    pallas_call x1, Pallas kernels, mix(): pl.pallas_call(functools.partial(mix_kernel, width), out_shape=jax.ShapeD...  5.51 us
    convert_element_type x1, other arithmetic, wave_block(): sine = jnp.sin(angle).astype(jnp.bfloat16)  2.48 us
    neg x1, other arithmetic, wave_block(): lower = jnp.concatenate([-sine, cosine], axis=1)  2.29 us

profile of v5, /device:TPU:16, one launch (start us, length us, event | category | flops | bytes accessed | tf_op | source)
XLA Modules:
  0.0 79.5 jit_solution(2792126850103399510)
XLA Ops:
  0.0 0.0 copy-start
  0.0 0.1 fusion.18
  0.2 0.2 sine_convert_fusion.1
  0.3 0.1 maximum_maximum_fusion.1.table_ref
  0.4 2.3 %fusion.11 = bf16[1024,128]{1,0:T(8,128)(2,1)S(1)} fusion(s32[128]{0:T(128)S(1)} %iota_add_fusion.1, s32[1024]{0:T(1024)S(1)} %iota_add_fusion), kind=kLoop, calls=%fused_computation.26 | loop fusion | flops 2359296 | bytes 266752 | tf_op jit(solution)/shard_map/neg | solution.py:34
  2.7 2.5 %sine_convert_fusion = (bf16[1024,128]{1,0:T(8,128)(2,1)S(1)}, bf16[1024,128]{1,0:T(8,128)(2,1)S(1)}) fusion(s32[128]{0:T(128)S(1)} %iota_add_fusion.1, s32[1024]{0:T(1024)S(1)} %iota_add_fusion), kind=kLoop, calls=%fused_computation.10 | loop fusion | flops 2097152 | bytes 528896 | tf_op jit(solution)/shard_map/convert_element_type | solution.py:32
  5.2 0.1 maximum_maximum_fusion.wave_ref
  5.3 1.0 %fusion.9 = (f32[64,1024]{1,0:T(8,128)S(1)}, f32[64,1024]{1,0:T(8,128)S(1)}) fusion(s32[1024]{0:T(1024)S(1)} %iota_add_fusion), kind=kLoop, calls=%fused_computation.21 | loop fusion | flops 917504 | bytes 528384 | tf_op jit(solution)/shard_map/sin | solution.py:42
  6.3 0.0 copy-done
  6.4 10.8 %shard_map.37 = bf16[32,64,256]{2,1,0:T(8,128)(2,1)S(1)} custom-call(f32[2,64,1024]{2,1,0:T(8,128)S(1)} %copy-done, bf16[2,32,64,1024]{3,2,1,0:T(8,128)(2,1)} %filt_ref.1, bf16[128,128]{1,0:T(8,128)(2,1)S(1)} %maximum_maximum_fusion.1.table_ref, f32[64,1024]{1,0:T(8,128)S(1)} %get-tuple-element.8.tcos_ref, f32[64,1024]{1,0:T(8,128)S(1)} %get-tuple-element.7.tsin_ref, ...), custom_call_target="tpu_custom_call" | custom-call | tf_op jit(solution)/shard_map/pallas_call | solution.py:240
  17.1 1.6 %copy.6 = bf16[32,64,256]{2,0,1:T(8,128)(2,1)} copy(bf16[32,64,256]{2,1,0:T(8,128)(2,1)S(1)} %shard_map.37) | data formatting | bytes 2097152 | tf_op jit(solution)/shard_map/pallas_call | solution.py:240
  18.7 18.0 %shard_map.38.x_ref = bf16[4,32,256]{2,1,0:T(8,128)(2,1)} custom-call(bf16[64,32,256]{2,1,0:T(8,128)(2,1)} %bitcast.3), custom_call_target="tpu_custom_call" | custom-call | tf_op jit(solution)/shard_map/pallas_call | solution.py:96
  36.7 37.3 %shard_map.39.slots_ref = bf16[16,4,32,256]{3,2,1,0:T(8,128)(2,1)} custom-call(bf16[4,32,256]{2,1,0:T(8,128)(2,1)} %shard_map.38.x_ref), custom_call_target="tpu_custom_call" | custom-call | tf_op jit(solution)/shard_map/pallas_call | solution.py:168
  74.0 5.5 %shard_map.40 = bf16[2,4,1024,128]{3,2,1,0:T(8,128)(2,1)} custom-call(bf16[2,1024,512]{2,1,0:T(8,128)(2,1)} %mix_ref.1, bf16[16,4,32,256]{3,2,1,0:T(8,128)(2,1)} %shard_map.39.slots_ref), custom_call_target="tpu_custom_call" | custom-call | tf_op jit(solution)/shard_map/pallas_call | solution.py:202
  (2 shorter events, 0.0 us)
Async XLA Ops:
  0.0 6.3 %copy-start = (f32[2,64,1024]{2,1,0:T(8,128)S(1)}, f32[2,64,1024]{2,1,0:T(8,128)}, u32[]{:S(2)}) copy-start(f32[2,64,1024]{2,1,0:T(8,128)} %spec_ref.1) | copy-start | bytes 1572868

commit v6 on v0

v6 whole, which is shorter than its diff:
```python
import functools
import math

import jax
import jax.numpy as jnp
from jax import lax
from jax.experimental import pallas as pl
from jax.experimental.pallas import tpu as pltpu
from jax.sharding import PartitionSpec as P

NSAMP = 1048576
INNER = 64
WROWS = 128
START = 8128


def first_table(inner):
    index = jnp.arange(inner, dtype=jnp.int32)
    phase = index[:, None] * index[None, :] % inner
    angle = phase.astype(jnp.float32) * (2.0 * math.pi / inner)
    cosine = jnp.cos(angle).astype(jnp.bfloat16)
    sine = jnp.sin(angle).astype(jnp.bfloat16)
    upper = jnp.concatenate([cosine, -sine], axis=1)
    lower = jnp.concatenate([sine, cosine], axis=1)
    return jnp.concatenate([upper, lower], axis=0)


def wave_block(freqs, lags, period):
    phase = freqs[:, None] * lags[None, :] % period
    angle = phase.astype(jnp.float32) * (2.0 * math.pi / period)
    cosine = jnp.cos(angle).astype(jnp.bfloat16)
    sine = jnp.sin(angle).astype(jnp.bfloat16)
    upper = jnp.concatenate([cosine, sine], axis=1)
    lower = jnp.concatenate([-sine, cosine], axis=1)
    return jnp.concatenate([upper, lower], axis=0)


def twist_tables(freqs, inner, total):
    rows_index = jnp.arange(inner, dtype=jnp.int32)
    phase = rows_index[:, None] * freqs[None, :] % total
    angle = phase.astype(jnp.float32) * (2.0 * math.pi / total)
    return (jnp.cos(angle), jnp.sin(angle))


MESH = pl.DeviceIdType.MESH


def exchange_kernel(x_ref, o_ref, slots, scatter_send, scatter_recv, gather_send, gather_recv):
    n_tm, n_bank = slots.shape[1], o_ref.shape[0]
    rows = o_ref.shape[1]
    me_tm = lax.axis_index("tm")
    me_bank = lax.axis_index("bank")
    at_tm = lambda peer: (peer, me_bank)
    at_bank = lambda peer: (me_tm, peer)
    barrier = pltpu.get_barrier_semaphore()
    for step in range(1, n_tm):
        pl.semaphore_signal(barrier, inc=1, device_id=at_tm((me_tm + step) % n_tm), device_id_type=MESH)
    for step in range(1, n_bank):
        pl.semaphore_signal(barrier, inc=1, device_id=at_bank((me_bank + step) % n_bank), device_id_type=MESH)
    pl.semaphore_wait(barrier, n_tm + n_bank - 2)

    def remote(src, dst, send, recv, device):
        return pltpu.make_async_remote_copy(
            src_ref=src, dst_ref=dst, send_sem=send, recv_sem=recv, device_id=device, device_id_type=MESH
        )

    sends = []
    for r in range(rows):
        for step in range(1, n_tm):
            peer = (me_tm + step) % n_tm
            copy = remote(
                x_ref.at[peer * rows + r], slots.at[r, me_tm],
                scatter_send.at[r, peer], scatter_recv.at[r, me_tm], at_tm(peer),
            )
            copy.start()
            sends.append(copy)
    for r in range(rows):
        total = x_ref[me_tm * rows + r].astype(jnp.float32)
        for step in range(1, n_tm):
            source = (me_tm + n_tm - step) % n_tm
            remote(
                x_ref.at[r], slots.at[r, source],
                scatter_send.at[r, source], scatter_recv.at[r, source], at_tm(source),
            ).wait_recv()
            total = total + slots[r, source].astype(jnp.float32)
        o_ref[me_bank, r] = total.astype(o_ref.dtype)
        for step in range(1, n_bank):
            peer = (me_bank + step) % n_bank
            copy = remote(
                o_ref.at[me_bank, r], o_ref.at[me_bank, r],
                gather_send.at[r, peer], gather_recv.at[r, me_bank], at_bank(peer),
            )
            copy.start()
            sends.append(copy)
    for r in range(rows):
        for step in range(1, n_bank):
            source = (me_bank + n_bank - step) % n_bank
            remote(
                o_ref.at[source, r], o_ref.at[source, r],
                gather_send.at[r, source], gather_recv.at[r, source], at_bank(source),
            ).wait_recv()
    for copy in sends:
        copy.wait_send()


def exchange(x, n_tm, n_bank):
    rows = x.shape[0] // n_tm
    block = x.shape[1:]
    return pl.pallas_call(
        exchange_kernel,
        out_shape=jax.ShapeDtypeStruct((n_bank, rows) + block, x.dtype),
        in_specs=[pl.BlockSpec(memory_space=pltpu.VMEM)],
        out_specs=pl.BlockSpec(memory_space=pltpu.VMEM),
        scratch_shapes=[
            pltpu.VMEM((rows, n_tm) + block, x.dtype),
            pltpu.SemaphoreType.DMA((rows, n_tm)),
            pltpu.SemaphoreType.DMA((rows, n_tm)),
            pltpu.SemaphoreType.DMA((rows, n_bank)),
            pltpu.SemaphoreType.DMA((rows, n_bank)),
        ],
        compiler_params=pltpu.CompilerParams(collective_id=0, has_side_effects=True),
    )(x)


def mix_kernel(mix_ref, slots_ref, o_ref):
    n, rows, _, cols = slots_ref.shape
    half = cols // 2
    order = range(n)
    mix_real = mix_ref[0]
    mix_imag = mix_ref[1]
    for t in range(rows):
        plain = jnp.concatenate([slots_ref[slot, t] for slot in order], axis=0)
        turned = jnp.concatenate([-plain[:, half:], plain[:, :half]], axis=1)
        result = jnp.dot(mix_real, plain, preferred_element_type=jnp.float32) + jnp.dot(
            mix_imag, turned, preferred_element_type=jnp.float32
        )
        o_ref[0, t] = result[:, :half].astype(o_ref.dtype)
        o_ref[1, t] = result[:, half:].astype(o_ref.dtype)


def mix(mixing, slots):
    _, rows, _, cols = slots.shape
    templates = mixing.shape[1]
    return pl.pallas_call(
        mix_kernel,
        out_shape=jax.ShapeDtypeStruct((2, rows, templates, cols // 2), jnp.bfloat16),
        in_specs=[pl.BlockSpec(memory_space=pltpu.VMEM)] * 2,
        out_specs=pl.BlockSpec(memory_space=pltpu.VMEM),
    )(mixing, slots)


def front_kernel(spec_ref, filt_ref, table_ref, tcos_ref, tsin_ref, wave_ref, o_ref, quarter):
    block, inner = filt_ref.shape[1], filt_ref.shape[2]
    spec_real = spec_ref[0]
    spec_imag = spec_ref[1]
    table = table_ref[...]
    twist_cos = tcos_ref[...]
    twist_sin = tsin_ref[...]
    for kk in range(block):
        filt_real = filt_ref[0, kk].astype(jnp.float32)
        filt_imag = filt_ref[1, kk].astype(jnp.float32)
        prod_real = spec_real * filt_real + spec_imag * filt_imag
        prod_imag = spec_imag * filt_real - spec_real * filt_imag
        packed = jnp.concatenate([prod_real, prod_imag], axis=0).astype(jnp.bfloat16)
        section = jnp.dot(table, packed, preferred_element_type=jnp.float32)
        section_real = section[:inner]
        section_imag = section[inner:]
        quarter_real = section_real * twist_cos - section_imag * twist_sin
        quarter_imag = section_real * twist_sin + section_imag * twist_cos
        width = quarter_real.shape[1]
        rows = pl.ds(kk * inner, inner)
        quarter[rows, pl.ds(0, width)] = quarter_real.astype(jnp.bfloat16)
        quarter[rows, pl.ds(width, width)] = quarter_imag.astype(jnp.bfloat16)
    result = jnp.dot(quarter[...], wave_ref[...], preferred_element_type=jnp.float32)
    o_ref[...] = result.reshape(o_ref.shape).astype(o_ref.dtype)


def front(spectrum, filters, table, twist_cos, twist_sin, wave, block=8):
    _, basis, inner, freq = filters.shape
    cols = wave.shape[1]
    whole = lambda *shape: pl.BlockSpec(shape, lambda i: (0,) * len(shape))
    return pl.pallas_call(
        front_kernel,
        grid=(basis // block,),
        out_shape=jax.ShapeDtypeStruct((basis, inner, cols), jnp.bfloat16),
        in_specs=[
            whole(2, inner, freq),
            pl.BlockSpec((2, block, inner, freq), lambda i: (0, i, 0, 0)),
            whole(2 * inner, 2 * inner),
            whole(inner, freq),
            whole(inner, freq),
            whole(2 * freq, cols),
        ],
        out_specs=pl.BlockSpec((block, inner, cols), lambda i: (i, 0, 0)),
        scratch_shapes=[pltpu.VMEM((block * inner, 2 * freq), jnp.bfloat16)],
        compiler_params=pltpu.CompilerParams(vmem_limit_bytes=48 * 1024 * 1024),
    )(spectrum, filters, table, twist_cos, twist_sin, wave)


def on_device(spectrum, filters, mixing):
    tm_index = lax.axis_index("tm")
    local_freq = filters.shape[3]
    local_basis = filters.shape[1]
    inner = INNER
    outer = NSAMP // INNER
    table = first_table(inner)
    freqs = tm_index * local_freq + jnp.arange(local_freq, dtype=jnp.int32)
    twist_cos, twist_sin = twist_tables(freqs, inner, NSAMP)
    lags = START + jnp.arange(WROWS, dtype=jnp.int32)
    wave = wave_block(freqs, lags, outer)
    partial = front(spectrum, filters, table, twist_cos, twist_sin, wave).transpose(1, 0, 2)
    slots = exchange(partial, lax.axis_size("tm"), lax.axis_size("bank"))
    return mix(mixing, slots)


def solution(mesh):
    return jax.shard_map(
        on_device,
        mesh=mesh,
        in_specs=(P(None, None, "tm"), P(None, "bank", None, "tm"), P(None, "bank", None)),
        out_specs=P(None, "tm", "bank", None),
        check_vma=False,
    )
```

time: 178 us -> 75.7 us (0.43)
  waiting for transfers between devices: 118 us -> 0 us
  Pallas kernels: 0 us -> 66.7 us
  matrix products: 14.9 us -> 0 us
  other arithmetic: 20.4 us -> 6.3 us
  between operations: 13.5 us -> 0.07 us
  local copies, waits for them, and re-layouts: 8.92 us -> 1.56 us
    reduce_scatter x1 -> x0, waiting for transfers between devices: 69.9 us -> none  [on_device(): summed = lax.psum_scatter(partial, 'tm', scatter_dimension=0, tiled=True)]
    pallas_call x0 -> x3, Pallas kernels: none -> 66.7 us  [the longest x1 50.4 us: exchange(): pl.pallas_call(exchange_kernel, out_shape=jax.ShapeDtypeStruct((n_bank, r...]
    all_gather x1 -> x0, waiting for transfers between devices: 47.9 us -> none  [on_device(): piece = lax.all_gather(series, 'bank', axis=0, tiled=False)]
    dot_general x6 -> x0, matrix products: 14.9 us -> none  [the longest x1 4.93 us: on_device(): jnp.einsum('ktf,fs->tks', quarter, wave, preferred_element_type=jnp.float32)]
    another operation x2 -> x0, other arithmetic: 7.66 us -> none
    convert_element_type x2 -> x0, other arithmetic: 6.6 us -> none  [the longest x1 5.06 us: on_device(): (section_real * twist_cos - section_imag * twist_sin).astype(jnp.bfloat16)]
    slice x3 -> x0, local copies, waits for them, and re-layouts: 2.75 us -> none  [the longest x2 2.21 us: on_device(): mix_real = mixing[0].reshape(templates, groups, local_basis)]
    another operation x1 -> x0, local copies, waits for them, and re-layouts: 2.56 us -> none  [on_device(): return jnp.stack([real_sum, imag_sum], axis=0).astype(jnp.bfloat16)]
  transfers between devices with their start and end apart: 2 -> 0, of which waited for: 2 -> 0; matrix products, arithmetic and copies ran while one was open for 2% -> 0% of each run, Pallas kernels for 0% -> 0%
where the time goes in v6:
time: 75.7 us; the launch traced here: 74.6 us
  Pallas kernels  66.7 us (88%)
  other arithmetic  6.3 us (8%)
  local copies, waits for them, and re-layouts  1.56 us (2%)
    pallas_call x1, Pallas kernels, exchange(): pl.pallas_call(exchange_kernel, out_shape=jax.ShapeDtypeStruct((n_bank, r...  50.4 us
    pallas_call x1, Pallas kernels, front(): pl.pallas_call(front_kernel, grid=(basis // block,), out_shape=jax.ShapeD...  10.8 us
    pallas_call x1, Pallas kernels, mix(): pl.pallas_call(mix_kernel, out_shape=jax.ShapeDtypeStruct((2, rows, templ...  5.51 us
    convert_element_type x1, other arithmetic, wave_block(): sine = jnp.sin(angle).astype(jnp.bfloat16)  2.48 us
    neg x1, other arithmetic, wave_block(): lower = jnp.concatenate([-sine, cosine], axis=1)  2.29 us
    pallas_call x1, local copies, waits for them, and re-layouts, front(): pl.pallas_call(front_kernel, grid=(basis // block,), out_shape=jax.ShapeD...  1.55 us

profile of v6, /device:TPU:6, one launch (start us, length us, event | category | flops | bytes accessed | tf_op | source)
XLA Modules:
  0.0 74.6 jit_solution(13732823820261349163)
XLA Ops:
  0.0 0.0 copy-start
  0.0 0.1 fusion.18
  0.2 0.2 sine_convert_fusion.1
  0.3 0.1 maximum_maximum_fusion.1.table_ref
  0.4 2.3 %fusion.11 = bf16[1024,128]{1,0:T(8,128)(2,1)S(1)} fusion(s32[128]{0:T(128)S(1)} %iota_add_fusion.1, s32[1024]{0:T(1024)S(1)} %iota_add_fusion), kind=kLoop, calls=%fused_computation.26 | loop fusion | flops 2359296 | bytes 266752 | tf_op jit(solution)/shard_map/neg | solution.py:34
  2.7 2.5 %sine_convert_fusion = (bf16[1024,128]{1,0:T(8,128)(2,1)S(1)}, bf16[1024,128]{1,0:T(8,128)(2,1)S(1)}) fusion(s32[128]{0:T(128)S(1)} %iota_add_fusion.1, s32[1024]{0:T(1024)S(1)} %iota_add_fusion), kind=kLoop, calls=%fused_computation.10 | loop fusion | flops 2097152 | bytes 528896 | tf_op jit(solution)/shard_map/convert_element_type | solution.py:32
  5.2 0.1 maximum_maximum_fusion.wave_ref
  5.3 1.0 %fusion.9 = (f32[64,1024]{1,0:T(8,128)S(1)}, f32[64,1024]{1,0:T(8,128)S(1)}) fusion(s32[1024]{0:T(1024)S(1)} %iota_add_fusion), kind=kLoop, calls=%fused_computation.21 | loop fusion | flops 917504 | bytes 528384 | tf_op jit(solution)/shard_map/sin | solution.py:42
  6.3 0.0 copy-done
  6.4 10.8 %shard_map.37 = bf16[32,64,256]{2,1,0:T(8,128)(2,1)S(1)} custom-call(f32[2,64,1024]{2,1,0:T(8,128)S(1)} %copy-done, bf16[2,32,64,1024]{3,2,1,0:T(8,128)(2,1)} %filt_ref.1, bf16[128,128]{1,0:T(8,128)(2,1)S(1)} %maximum_maximum_fusion.1.table_ref, f32[64,1024]{1,0:T(8,128)S(1)} %get-tuple-element.8.tcos_ref, f32[64,1024]{1,0:T(8,128)S(1)} %get-tuple-element.7.tsin_ref, ...), custom_call_target="tpu_custom_call" | custom-call | tf_op jit(solution)/shard_map/pallas_call | solution.py:182
  17.1 1.6 %copy.6 = bf16[32,64,256]{2,0,1:T(8,128)(2,1)} copy(bf16[32,64,256]{2,1,0:T(8,128)(2,1)S(1)} %shard_map.37) | data formatting | bytes 2097152 | tf_op jit(solution)/shard_map/pallas_call | solution.py:182
  18.7 50.4 %shard_map.38.slots_ref = bf16[16,4,32,256]{3,2,1,0:T(8,128)(2,1)} custom-call(bf16[64,32,256]{2,1,0:T(8,128)(2,1)} %bitcast.3), custom_call_target="tpu_custom_call" | custom-call | tf_op jit(solution)/shard_map/pallas_call | solution.py:109
  69.1 5.5 %shard_map.39 = bf16[2,4,1024,128]{3,2,1,0:T(8,128)(2,1)} custom-call(bf16[2,1024,512]{2,1,0:T(8,128)(2,1)} %mix_ref.1, bf16[16,4,32,256]{3,2,1,0:T(8,128)(2,1)} %shard_map.38.slots_ref), custom_call_target="tpu_custom_call" | custom-call | tf_op jit(solution)/shard_map/pallas_call | solution.py:144
  (2 shorter events, 0.0 us)
Async XLA Ops:
  0.0 6.3 %copy-start = (f32[2,64,1024]{2,1,0:T(8,128)S(1)}, f32[2,64,1024]{2,1,0:T(8,128)}, u32[]{:S(2)}) copy-start(f32[2,64,1024]{2,1,0:T(8,128)} %spec_ref.1) | copy-start | bytes 1572868

commit v7 on v6

--- a/solution.py
+++ b/solution.py
@@ -45,24 +45,40 @@
 MESH = pl.DeviceIdType.MESH
 
 
-def exchange_kernel(x_ref, o_ref, slots, scatter_send, scatter_recv, gather_send, gather_recv):
+def exchange_kernel(width, x_ref, o_ref, slots, scatter_send, scatter_recv, gather_send, gather_recv,
+                    relay_send, relay_recv):
     n_tm, n_bank = slots.shape[1], o_ref.shape[0]
-    rows = o_ref.shape[1]
+    depth = n_bank // width
+    rows, basis = o_ref.shape[1], o_ref.shape[2]
+    half = basis // 2
     me_tm = lax.axis_index("tm")
     me_bank = lax.axis_index("bank")
+    x = me_bank // depth
+    z = me_bank % depth
+    up = (z + 1) % depth
+    down = (z + depth - 1) % depth
     at_tm = lambda peer: (peer, me_bank)
     at_bank = lambda peer: (me_tm, peer)
+    near = [(x + step) % width * depth + z for step in range(1, width)]
+    near += [xx * depth + up for xx in range(width)] + [xx * depth + down for xx in range(width)]
     barrier = pltpu.get_barrier_semaphore()
     for step in range(1, n_tm):
         pl.semaphore_signal(barrier, inc=1, device_id=at_tm((me_tm + step) % n_tm), device_id_type=MESH)
-    for step in range(1, n_bank):
-        pl.semaphore_signal(barrier, inc=1, device_id=at_bank((me_bank + step) % n_bank), device_id_type=MESH)
-    pl.semaphore_wait(barrier, n_tm + n_bank - 2)
+    for peer in near:
+        pl.semaphore_signal(barrier, inc=1, device_id=at_bank(peer), device_id_type=MESH)
+    pl.semaphore_wait(barrier, n_tm - 1 + len(near))
 
     def remote(src, dst, send, recv, device):
         return pltpu.make_async_remote_copy(
             src_ref=src, dst_ref=dst, send_sem=send, recv_sem=recv, device_id=device, device_id_type=MESH
         )
+
+    def relays(r):
+        out = []
+        for xx in range(width):
+            out.append((xx * depth + down, 0, x * depth + up, 0, xx))
+            out.append((xx * depth + up, half, x * depth + down, 1, xx))
+        return out
 
     sends = []
     for r in range(rows):
@@ -74,6 +90,19 @@
             )
             copy.start()
             sends.append(copy)
+
+    def forward(r):
+        for source in near:
+            remote(
+                o_ref.at[source, r], o_ref.at[source, r],
+                gather_send.at[r, source], gather_recv.at[r, source], at_bank(source),
+            ).wait_recv()
+        for slot, start, target, way, xx in relays(r):
+            block = o_ref.at[slot, r, pl.ds(start, half)]
+            copy = remote(block, block, relay_send.at[r, way, xx], relay_recv.at[r, way, xx], at_bank(target))
+            copy.start()
+            sends.append(copy)
+
     for r in range(rows):
         total = x_ref[me_tm * rows + r].astype(jnp.float32)
         for step in range(1, n_tm):
@@ -84,30 +113,33 @@
             ).wait_recv()
             total = total + slots[r, source].astype(jnp.float32)
         o_ref[me_bank, r] = total.astype(o_ref.dtype)
-        for step in range(1, n_bank):
-            peer = (me_bank + step) % n_bank
+        for peer in near:
             copy = remote(
                 o_ref.at[me_bank, r], o_ref.at[me_bank, r],
                 gather_send.at[r, peer], gather_recv.at[r, me_bank], at_bank(peer),
             )
             copy.start()
             sends.append(copy)
+        if r >= 1:
+            forward(r - 1)
+    forward(rows - 1)
+    across = (z + 2) % depth
     for r in range(rows):
-        for step in range(1, n_bank):
-            source = (me_bank + n_bank - step) % n_bank
-            remote(
-                o_ref.at[source, r], o_ref.at[source, r],
-                gather_send.at[r, source], gather_recv.at[r, source], at_bank(source),
-            ).wait_recv()
+        for xx in range(width):
+            for way, start, via in ((0, 0, down), (1, half, up)):
+                block = o_ref.at[xx * depth + across, r, pl.ds(start, half)]
+                remote(
+                    block, block, relay_send.at[r, way, xx], relay_recv.at[r, way, xx], at_bank(x * depth + via)
+                ).wait_recv()
     for copy in sends:
         copy.wait_send()
 
 
-def exchange(x, n_tm, n_bank):
+def exchange(x, n_tm, n_bank, width):
     rows = x.shape[0] // n_tm
     block = x.shape[1:]
     return pl.pallas_call(
-        exchange_kernel,
+        functools.partial(exchange_kernel, width),
         out_shape=jax.ShapeDtypeStruct((n_bank, rows) + block, x.dtype),
         in_specs=[pl.BlockSpec(memory_space=pltpu.VMEM)],
         out_specs=pl.BlockSpec(memory_space=pltpu.VMEM),
@@ -117,6 +149,8 @@
             pltpu.SemaphoreType.DMA((rows, n_tm)),
             pltpu.SemaphoreType.DMA((rows, n_bank)),
             pltpu.SemaphoreType.DMA((rows, n_bank)),
+            pltpu.SemaphoreType.DMA((rows, 2, width)),
+            pltpu.SemaphoreType.DMA((rows, 2, width)),
         ],
         compiler_params=pltpu.CompilerParams(collective_id=0, has_side_effects=True),
     )(x)
@@ -209,7 +243,7 @@
     lags = START + jnp.arange(WROWS, dtype=jnp.int32)
     wave = wave_block(freqs, lags, outer)
     partial = front(spectrum, filters, table, twist_cos, twist_sin, wave).transpose(1, 0, 2)
-    slots = exchange(partial, lax.axis_size("tm"), lax.axis_size("bank"))
+    slots = exchange(partial, lax.axis_size("tm"), lax.axis_size("bank"), 4)
     return mix(mixing, slots)
 
 

time: 75.7 us -> 73.1 us (0.966); the launches traced: 74.6 us -> 72.9 us
  Pallas kernels: 66.7 us -> 65 us
    pallas_call x1, Pallas kernels: 50.4 us -> 48.7 us  [exchange(): pl.pallas_call(functools.partial(exchange_kernel, width), out_shape=jax.S...]
where the time goes in v7:
time: 73.1 us; the launch traced here: 72.9 us
  Pallas kernels  65 us (89%)
  other arithmetic  6.3 us (9%)
  local copies, waits for them, and re-layouts  1.56 us (2%)
    pallas_call x1, Pallas kernels, exchange(): pl.pallas_call(functools.partial(exchange_kernel, width), out_shape=jax.S...  48.7 us
    pallas_call x1, Pallas kernels, front(): pl.pallas_call(front_kernel, grid=(basis // block,), out_shape=jax.ShapeD...  10.8 us
    pallas_call x1, Pallas kernels, mix(): pl.pallas_call(mix_kernel, out_shape=jax.ShapeDtypeStruct((2, rows, templ...  5.51 us
    convert_element_type x1, other arithmetic, wave_block(): sine = jnp.sin(angle).astype(jnp.bfloat16)  2.48 us
    neg x1, other arithmetic, wave_block(): lower = jnp.concatenate([-sine, cosine], axis=1)  2.29 us
    pallas_call x1, local copies, waits for them, and re-layouts, front(): pl.pallas_call(front_kernel, grid=(basis // block,), out_shape=jax.ShapeD...  1.55 us

profile of v7, /device:TPU:6, one launch (start us, length us, event | category | flops | bytes accessed | tf_op | source)
XLA Modules:
  0.0 72.9 jit_solution(5303144061129344210)
XLA Ops:
  0.0 0.0 copy-start
  0.0 0.1 fusion.18
  0.2 0.2 sine_convert_fusion.1
  0.3 0.1 maximum_maximum_fusion.1.table_ref
  0.4 2.3 %fusion.11 = bf16[1024,128]{1,0:T(8,128)(2,1)S(1)} fusion(s32[128]{0:T(128)S(1)} %iota_add_fusion.1, s32[1024]{0:T(1024)S(1)} %iota_add_fusion), kind=kLoop, calls=%fused_computation.26 | loop fusion | flops 2359296 | bytes 266752 | tf_op jit(solution)/shard_map/neg | solution.py:34
  2.7 2.5 %sine_convert_fusion = (bf16[1024,128]{1,0:T(8,128)(2,1)S(1)}, bf16[1024,128]{1,0:T(8,128)(2,1)S(1)}) fusion(s32[128]{0:T(128)S(1)} %iota_add_fusion.1, s32[1024]{0:T(1024)S(1)} %iota_add_fusion), kind=kLoop, calls=%fused_computation.10 | loop fusion | flops 2097152 | bytes 528896 | tf_op jit(solution)/shard_map/convert_element_type | solution.py:32
  5.2 0.1 maximum_maximum_fusion.wave_ref
  5.3 1.0 %fusion.9 = (f32[64,1024]{1,0:T(8,128)S(1)}, f32[64,1024]{1,0:T(8,128)S(1)}) fusion(s32[1024]{0:T(1024)S(1)} %iota_add_fusion), kind=kLoop, calls=%fused_computation.21 | loop fusion | flops 917504 | bytes 528384 | tf_op jit(solution)/shard_map/sin | solution.py:42
  6.3 0.0 copy-done
  6.4 10.8 %shard_map.37 = bf16[32,64,256]{2,1,0:T(8,128)(2,1)S(1)} custom-call(f32[2,64,1024]{2,1,0:T(8,128)S(1)} %copy-done, bf16[2,32,64,1024]{3,2,1,0:T(8,128)(2,1)} %filt_ref.1, bf16[128,128]{1,0:T(8,128)(2,1)S(1)} %maximum_maximum_fusion.1.table_ref, f32[64,1024]{1,0:T(8,128)S(1)} %get-tuple-element.8.tcos_ref, f32[64,1024]{1,0:T(8,128)S(1)} %get-tuple-element.7.tsin_ref, ...), custom_call_target="tpu_custom_call" | custom-call | tf_op jit(solution)/shard_map/pallas_call | solution.py:216
  17.1 1.6 %copy.6 = bf16[32,64,256]{2,0,1:T(8,128)(2,1)} copy(bf16[32,64,256]{2,1,0:T(8,128)(2,1)S(1)} %shard_map.37) | data formatting | bytes 2097152 | tf_op jit(solution)/shard_map/pallas_call | solution.py:216
  18.7 48.7 %shard_map.38.slots_ref = bf16[16,4,32,256]{3,2,1,0:T(8,128)(2,1)} custom-call(bf16[64,32,256]{2,1,0:T(8,128)(2,1)} %bitcast.3), custom_call_target="tpu_custom_call" | custom-call | tf_op jit(solution)/shard_map/pallas_call | solution.py:141
  67.4 5.5 %shard_map.39 = bf16[2,4,1024,128]{3,2,1,0:T(8,128)(2,1)} custom-call(bf16[2,1024,512]{2,1,0:T(8,128)(2,1)} %mix_ref.1, bf16[16,4,32,256]{3,2,1,0:T(8,128)(2,1)} %shard_map.38.slots_ref), custom_call_target="tpu_custom_call" | custom-call | tf_op jit(solution)/shard_map/pallas_call | solution.py:178
  (2 shorter events, 0.0 us)
Async XLA Ops:
  0.0 6.3 %copy-start = (f32[2,64,1024]{2,1,0:T(8,128)S(1)}, f32[2,64,1024]{2,1,0:T(8,128)}, u32[]{:S(2)}) copy-start(f32[2,64,1024]{2,1,0:T(8,128)} %spec_ref.1) | copy-start | bytes 1572868

commit v8 on v7

--- a/solution.py
+++ b/solution.py
@@ -30,9 +30,7 @@
     angle = phase.astype(jnp.float32) * (2.0 * math.pi / period)
     cosine = jnp.cos(angle).astype(jnp.bfloat16)
     sine = jnp.sin(angle).astype(jnp.bfloat16)
-    upper = jnp.concatenate([cosine, sine], axis=1)
-    lower = jnp.concatenate([-sine, cosine], axis=1)
-    return jnp.concatenate([upper, lower], axis=0)
+    return jnp.concatenate([cosine, sine], axis=1)
 
 
 def twist_tables(freqs, inner, total):
@@ -205,7 +203,13 @@
         rows = pl.ds(kk * inner, inner)
         quarter[rows, pl.ds(0, width)] = quarter_real.astype(jnp.bfloat16)
         quarter[rows, pl.ds(width, width)] = quarter_imag.astype(jnp.bfloat16)
-    result = jnp.dot(quarter[...], wave_ref[...], preferred_element_type=jnp.float32)
+    wave = wave_ref[...]
+    cols = wave.shape[1] // 2
+    from_real = jnp.dot(quarter[:, :width], wave, preferred_element_type=jnp.float32)
+    from_imag = jnp.dot(quarter[:, width:], wave, preferred_element_type=jnp.float32)
+    result = jnp.concatenate(
+        [from_real[:, :cols] - from_imag[:, cols:], from_real[:, cols:] + from_imag[:, :cols]], axis=1
+    )
     o_ref[...] = result.reshape(o_ref.shape).astype(o_ref.dtype)
 
 
@@ -223,7 +227,7 @@
             whole(2 * inner, 2 * inner),
             whole(inner, freq),
             whole(inner, freq),
-            whole(2 * freq, cols),
+            whole(freq, cols),
         ],
         out_specs=pl.BlockSpec((block, inner, cols), lambda i: (i, 0, 0)),
         scratch_shapes=[pltpu.VMEM((block * inner, 2 * freq), jnp.bfloat16)],

time: 73.1 us -> 70.7 us (0.967)
  other arithmetic: 6.3 us -> 3.97 us
    neg x1 -> x0, other arithmetic: 2.29 us -> none  [wave_block(): lower = jnp.concatenate([-sine, cosine], axis=1)]
where the time goes in v8:
time: 70.7 us; the launch traced here: 70.6 us
  Pallas kernels  65 us (92%)
  other arithmetic  3.97 us (6%)
  local copies, waits for them, and re-layouts  1.56 us (2%)
    pallas_call x1, Pallas kernels, exchange(): pl.pallas_call(functools.partial(exchange_kernel, width), out_shape=jax.S...  48.7 us
    pallas_call x1, Pallas kernels, front(): pl.pallas_call(front_kernel, grid=(basis // block,), out_shape=jax.ShapeD...  10.8 us
    pallas_call x1, Pallas kernels, mix(): pl.pallas_call(mix_kernel, out_shape=jax.ShapeDtypeStruct((2, rows, templ...  5.51 us
    convert_element_type x1, other arithmetic, wave_block(): cosine = jnp.cos(angle).astype(jnp.bfloat16)  2.48 us
    pallas_call x1, local copies, waits for them, and re-layouts, front(): pl.pallas_call(front_kernel, grid=(basis // block,), out_shape=jax.ShapeD...  1.55 us

profile of v8, /device:TPU:6, one launch (start us, length us, event | category | flops | bytes accessed | tf_op | source)
XLA Modules:
  0.0 70.6 jit_solution(11201140535418991229)
XLA Ops:
  0.0 0.0 copy-start
  0.0 0.1 fusion.17
  0.2 0.2 sine_convert_fusion.1
  0.3 0.1 maximum_maximum_fusion.table_ref
  0.4 2.5 %cosine_convert_fusion = (bf16[1024,128]{1,0:T(8,128)(2,1)S(1)}, bf16[1024,128]{1,0:T(8,128)(2,1)S(1)}) fusion(s32[128]{0:T(128)S(1)} %iota_add_fusion.1, s32[1024]{0:T(1024)S(1)} %iota_add_fusion), kind=kLoop, calls=%fused_computation.11 | loop fusion | flops 2097152 | bytes 528896 | tf_op jit(solution)/shard_map/convert_element_type | solution.py:31
  2.9 0.1 pad_maximum_fusion.wave_ref
  3.0 1.0 %fusion.9 = (f32[64,1024]{1,0:T(8,128)S(1)}, f32[64,1024]{1,0:T(8,128)S(1)}) fusion(s32[1024]{0:T(1024)S(1)} %iota_add_fusion), kind=kLoop, calls=%fused_computation.21 | loop fusion | flops 917504 | bytes 528384 | tf_op jit(solution)/shard_map/sin | solution.py:40
  4.0 0.0 copy-done
  4.0 10.8 %shard_map.37 = bf16[32,64,256]{2,1,0:T(8,128)(2,1)S(1)} custom-call(f32[2,64,1024]{2,1,0:T(8,128)S(1)} %copy-done, bf16[2,32,64,1024]{3,2,1,0:T(8,128)(2,1)} %filt_ref.1, bf16[128,128]{1,0:T(8,128)(2,1)S(1)} %maximum_maximum_fusion.table_ref, f32[64,1024]{1,0:T(8,128)S(1)} %get-tuple-element.8.tcos_ref, f32[64,1024]{1,0:T(8,128)S(1)} %get-tuple-element.7.tsin_ref, ...), custom_call_target="tpu_custom_call" | custom-call | tf_op jit(solution)/shard_map/pallas_call | solution.py:220
  14.8 1.6 %copy.6 = bf16[32,64,256]{2,0,1:T(8,128)(2,1)} copy(bf16[32,64,256]{2,1,0:T(8,128)(2,1)S(1)} %shard_map.37) | data formatting | bytes 2097152 | tf_op jit(solution)/shard_map/pallas_call | solution.py:220
  16.3 48.7 %shard_map.38.slots_ref = bf16[16,4,32,256]{3,2,1,0:T(8,128)(2,1)} custom-call(bf16[64,32,256]{2,1,0:T(8,128)(2,1)} %bitcast.3), custom_call_target="tpu_custom_call" | custom-call | tf_op jit(solution)/shard_map/pallas_call | solution.py:139
  65.1 5.5 %shard_map.39 = bf16[2,4,1024,128]{3,2,1,0:T(8,128)(2,1)} custom-call(bf16[2,1024,512]{2,1,0:T(8,128)(2,1)} %mix_ref.1, bf16[16,4,32,256]{3,2,1,0:T(8,128)(2,1)} %shard_map.38.slots_ref), custom_call_target="tpu_custom_call" | custom-call | tf_op jit(solution)/shard_map/pallas_call | solution.py:176
  (2 shorter events, 0.0 us)
Async XLA Ops:
  0.0 4.0 %copy-start = (f32[2,64,1024]{2,1,0:T(8,128)S(1)}, f32[2,64,1024]{2,1,0:T(8,128)}, u32[]{:S(2)}) copy-start(f32[2,64,1024]{2,1,0:T(8,128)} %spec_ref.1) | copy-start | bytes 1572868

commit v9 on v8

--- a/solution.py
+++ b/solution.py
@@ -79,7 +79,8 @@
         return out
 
     sends = []
-    for r in range(rows):
+
+    def scatter(r):
         for step in range(1, n_tm):
             peer = (me_tm + step) % n_tm
             copy = remote(
@@ -88,6 +89,10 @@
             )
             copy.start()
             sends.append(copy)
+
+    ahead = 2
+    for r in range(min(ahead, rows)):
+        scatter(r)
 
     def forward(r):
         for source in near:
@@ -118,6 +123,8 @@
             )
             copy.start()
             sends.append(copy)
+        if r + ahead < rows:
+            scatter(r + ahead)
         if r >= 1:
             forward(r - 1)
     forward(rows - 1)

time: 70.7 us -> 72.2 us (1.021)
  Pallas kernels: 65 us -> 66.5 us
    pallas_call x1, Pallas kernels: 48.7 us -> 50.2 us  [exchange(): pl.pallas_call(functools.partial(exchange_kernel, width), out_shape=jax.S...]
where the time goes in v9:
time: 72.2 us; the launch traced here: 72.1 us
  Pallas kernels  66.5 us (92%)
  other arithmetic  3.97 us (5%)
  local copies, waits for them, and re-layouts  1.56 us (2%)
    pallas_call x1, Pallas kernels, exchange(): pl.pallas_call(functools.partial(exchange_kernel, width), out_shape=jax.S...  50.2 us
    pallas_call x1, Pallas kernels, front(): pl.pallas_call(front_kernel, grid=(basis // block,), out_shape=jax.ShapeD...  10.8 us
    pallas_call x1, Pallas kernels, mix(): pl.pallas_call(mix_kernel, out_shape=jax.ShapeDtypeStruct((2, rows, templ...  5.51 us
    convert_element_type x1, other arithmetic, wave_block(): cosine = jnp.cos(angle).astype(jnp.bfloat16)  2.48 us
    pallas_call x1, local copies, waits for them, and re-layouts, front(): pl.pallas_call(front_kernel, grid=(basis // block,), out_shape=jax.ShapeD...  1.55 us

profile of v9, /device:TPU:6, one launch (start us, length us, event | category | flops | bytes accessed | tf_op | source)
XLA Modules:
  0.0 72.1 jit_solution(5182866783343281042)
XLA Ops:
  0.0 0.0 copy-start
  0.0 0.1 fusion.17
  0.2 0.2 sine_convert_fusion.1
  0.3 0.1 maximum_maximum_fusion.table_ref
  0.4 2.5 %cosine_convert_fusion = (bf16[1024,128]{1,0:T(8,128)(2,1)S(1)}, bf16[1024,128]{1,0:T(8,128)(2,1)S(1)}) fusion(s32[128]{0:T(128)S(1)} %iota_add_fusion.1, s32[1024]{0:T(1024)S(1)} %iota_add_fusion), kind=kLoop, calls=%fused_computation.11 | loop fusion | flops 2097152 | bytes 528896 | tf_op jit(solution)/shard_map/convert_element_type | solution.py:31
  2.9 0.1 pad_maximum_fusion.wave_ref
  3.0 1.0 %fusion.9 = (f32[64,1024]{1,0:T(8,128)S(1)}, f32[64,1024]{1,0:T(8,128)S(1)}) fusion(s32[1024]{0:T(1024)S(1)} %iota_add_fusion), kind=kLoop, calls=%fused_computation.21 | loop fusion | flops 917504 | bytes 528384 | tf_op jit(solution)/shard_map/sin | solution.py:40
  4.0 0.0 copy-done
  4.0 10.8 %shard_map.37 = bf16[32,64,256]{2,1,0:T(8,128)(2,1)S(1)} custom-call(f32[2,64,1024]{2,1,0:T(8,128)S(1)} %copy-done, bf16[2,32,64,1024]{3,2,1,0:T(8,128)(2,1)} %filt_ref.1, bf16[128,128]{1,0:T(8,128)(2,1)S(1)} %maximum_maximum_fusion.table_ref, f32[64,1024]{1,0:T(8,128)S(1)} %get-tuple-element.8.tcos_ref, f32[64,1024]{1,0:T(8,128)S(1)} %get-tuple-element.7.tsin_ref, ...), custom_call_target="tpu_custom_call" | custom-call | tf_op jit(solution)/shard_map/pallas_call | solution.py:227
  14.8 1.6 %copy.6 = bf16[32,64,256]{2,0,1:T(8,128)(2,1)} copy(bf16[32,64,256]{2,1,0:T(8,128)(2,1)S(1)} %shard_map.37) | data formatting | bytes 2097152 | tf_op jit(solution)/shard_map/pallas_call | solution.py:227
  16.3 50.2 %shard_map.38.slots_ref = bf16[16,4,32,256]{3,2,1,0:T(8,128)(2,1)} custom-call(bf16[64,32,256]{2,1,0:T(8,128)(2,1)} %bitcast.3), custom_call_target="tpu_custom_call" | custom-call | tf_op jit(solution)/shard_map/pallas_call | solution.py:146
  66.6 5.5 %shard_map.39 = bf16[2,4,1024,128]{3,2,1,0:T(8,128)(2,1)} custom-call(bf16[2,1024,512]{2,1,0:T(8,128)(2,1)} %mix_ref.1, bf16[16,4,32,256]{3,2,1,0:T(8,128)(2,1)} %shard_map.38.slots_ref), custom_call_target="tpu_custom_call" | custom-call | tf_op jit(solution)/shard_map/pallas_call | solution.py:183
  (2 shorter events, 0.0 us)
Async XLA Ops:
  0.0 4.0 %copy-start = (f32[2,64,1024]{2,1,0:T(8,128)S(1)}, f32[2,64,1024]{2,1,0:T(8,128)}, u32[]{:S(2)}) copy-start(f32[2,64,1024]{2,1,0:T(8,128)} %spec_ref.1) | copy-start | bytes 1572868

commit v10 on v8

--- a/solution.py
+++ b/solution.py
@@ -45,9 +45,9 @@
 
 def exchange_kernel(width, x_ref, o_ref, slots, scatter_send, scatter_recv, gather_send, gather_recv,
                     relay_send, relay_recv):
-    n_tm, n_bank = slots.shape[1], o_ref.shape[0]
+    n_tm, n_bank = slots.shape[1], o_ref.shape[1]
     depth = n_bank // width
-    rows, basis = o_ref.shape[1], o_ref.shape[2]
+    rows, basis = o_ref.shape[0], o_ref.shape[2]
     half = basis // 2
     me_tm = lax.axis_index("tm")
     me_bank = lax.axis_index("bank")
@@ -92,11 +92,11 @@
     def forward(r):
         for source in near:
             remote(
-                o_ref.at[source, r], o_ref.at[source, r],
+                o_ref.at[r, source], o_ref.at[r, source],
                 gather_send.at[r, source], gather_recv.at[r, source], at_bank(source),
             ).wait_recv()
         for slot, start, target, way, xx in relays(r):
-            block = o_ref.at[slot, r, pl.ds(start, half)]
+            block = o_ref.at[r, slot, pl.ds(start, half)]
             copy = remote(block, block, relay_send.at[r, way, xx], relay_recv.at[r, way, xx], at_bank(target))
             copy.start()
             sends.append(copy)
@@ -110,10 +110,10 @@
                 scatter_send.at[r, source], scatter_recv.at[r, source], at_tm(source),
             ).wait_recv()
             total = total + slots[r, source].astype(jnp.float32)
-        o_ref[me_bank, r] = total.astype(o_ref.dtype)
+        o_ref[r, me_bank] = total.astype(o_ref.dtype)
         for peer in near:
             copy = remote(
-                o_ref.at[me_bank, r], o_ref.at[me_bank, r],
+                o_ref.at[r, me_bank], o_ref.at[r, me_bank],
                 gather_send.at[r, peer], gather_recv.at[r, me_bank], at_bank(peer),
             )
             copy.start()
@@ -125,7 +125,7 @@
     for r in range(rows):
         for xx in range(width):
             for way, start, via in ((0, 0, down), (1, half, up)):
-                block = o_ref.at[xx * depth + across, r, pl.ds(start, half)]
+                block = o_ref.at[r, xx * depth + across, pl.ds(start, half)]
                 remote(
                     block, block, relay_send.at[r, way, xx], relay_recv.at[r, way, xx], at_bank(x * depth + via)
                 ).wait_recv()
@@ -138,7 +138,7 @@
     block = x.shape[1:]
     return pl.pallas_call(
         functools.partial(exchange_kernel, width),
-        out_shape=jax.ShapeDtypeStruct((n_bank, rows) + block, x.dtype),
+        out_shape=jax.ShapeDtypeStruct((rows, n_bank) + block, x.dtype),
         in_specs=[pl.BlockSpec(memory_space=pltpu.VMEM)],
         out_specs=pl.BlockSpec(memory_space=pltpu.VMEM),
         scratch_shapes=[
@@ -155,23 +155,20 @@
 
 
 def mix_kernel(mix_ref, slots_ref, o_ref):
-    n, rows, _, cols = slots_ref.shape
+    rows, n, basis, cols = slots_ref.shape
     half = cols // 2
-    order = range(n)
     mix_real = mix_ref[0]
     mix_imag = mix_ref[1]
     for t in range(rows):
-        plain = jnp.concatenate([slots_ref[slot, t] for slot in order], axis=0)
-        turned = jnp.concatenate([-plain[:, half:], plain[:, :half]], axis=1)
-        result = jnp.dot(mix_real, plain, preferred_element_type=jnp.float32) + jnp.dot(
-            mix_imag, turned, preferred_element_type=jnp.float32
-        )
-        o_ref[0, t] = result[:, :half].astype(o_ref.dtype)
-        o_ref[1, t] = result[:, half:].astype(o_ref.dtype)
+        plain = slots_ref[t].reshape(n * basis, cols)
+        from_real = jnp.dot(mix_real, plain, preferred_element_type=jnp.float32)
+        from_imag = jnp.dot(mix_imag, plain, preferred_element_type=jnp.float32)
+        o_ref[0, t] = (from_real[:, :half] - from_imag[:, half:]).astype(o_ref.dtype)
+        o_ref[1, t] = (from_real[:, half:] + from_imag[:, :half]).astype(o_ref.dtype)
 
 
 def mix(mixing, slots):
-    _, rows, _, cols = slots.shape
+    rows, _, _, cols = slots.shape
     templates = mixing.shape[1]
     return pl.pallas_call(
         mix_kernel,

time: 70.7 us -> 70.7 us (level)
  no operation moved by 1% of the time
where the time goes in v10:
time: 70.7 us; the launch traced here: 70.6 us
  Pallas kernels  65 us (92%)
  other arithmetic  3.97 us (6%)
  local copies, waits for them, and re-layouts  1.56 us (2%)
    pallas_call x1, Pallas kernels, exchange(): pl.pallas_call(functools.partial(exchange_kernel, width), out_shape=jax.S...  48.7 us
    pallas_call x1, Pallas kernels, front(): pl.pallas_call(front_kernel, grid=(basis // block,), out_shape=jax.ShapeD...  10.8 us
    pallas_call x1, Pallas kernels, mix(): pl.pallas_call(mix_kernel, out_shape=jax.ShapeDtypeStruct((2, rows, templ...  5.51 us
    convert_element_type x1, other arithmetic, wave_block(): cosine = jnp.cos(angle).astype(jnp.bfloat16)  2.48 us
    pallas_call x1, local copies, waits for them, and re-layouts, front(): pl.pallas_call(front_kernel, grid=(basis // block,), out_shape=jax.ShapeD...  1.55 us

profile of v10, /device:TPU:6, one launch (start us, length us, event | category | flops | bytes accessed | tf_op | source)
XLA Modules:
  0.0 70.6 jit_solution(12913484691739542196)
XLA Ops:
  0.0 0.0 copy-start
  0.0 0.1 fusion.17
  0.2 0.2 sine_convert_fusion.1
  0.3 0.1 maximum_maximum_fusion.table_ref
  0.4 2.5 %cosine_convert_fusion = (bf16[1024,128]{1,0:T(8,128)(2,1)S(1)}, bf16[1024,128]{1,0:T(8,128)(2,1)S(1)}) fusion(s32[128]{0:T(128)S(1)} %iota_add_fusion.1, s32[1024]{0:T(1024)S(1)} %iota_add_fusion), kind=kLoop, calls=%fused_computation.11 | loop fusion | flops 2097152 | bytes 528896 | tf_op jit(solution)/shard_map/convert_element_type | solution.py:31
  2.9 0.1 pad_maximum_fusion.wave_ref
  3.0 1.0 %fusion.9 = (f32[64,1024]{1,0:T(8,128)S(1)}, f32[64,1024]{1,0:T(8,128)S(1)}) fusion(s32[1024]{0:T(1024)S(1)} %iota_add_fusion), kind=kLoop, calls=%fused_computation.21 | loop fusion | flops 917504 | bytes 528384 | tf_op jit(solution)/shard_map/sin | solution.py:40
  4.0 0.0 copy-done
  4.0 10.8 %shard_map.37 = bf16[32,64,256]{2,1,0:T(8,128)(2,1)S(1)} custom-call(f32[2,64,1024]{2,1,0:T(8,128)S(1)} %copy-done, bf16[2,32,64,1024]{3,2,1,0:T(8,128)(2,1)} %filt_ref.1, bf16[128,128]{1,0:T(8,128)(2,1)S(1)} %maximum_maximum_fusion.table_ref, f32[64,1024]{1,0:T(8,128)S(1)} %get-tuple-element.8.tcos_ref, f32[64,1024]{1,0:T(8,128)S(1)} %get-tuple-element.7.tsin_ref, ...), custom_call_target="tpu_custom_call" | custom-call | tf_op jit(solution)/shard_map/pallas_call | solution.py:217
  14.8 1.6 %copy.6 = bf16[32,64,256]{2,0,1:T(8,128)(2,1)} copy(bf16[32,64,256]{2,1,0:T(8,128)(2,1)S(1)} %shard_map.37) | data formatting | bytes 2097152 | tf_op jit(solution)/shard_map/pallas_call | solution.py:217
  16.3 48.7 %shard_map.38.slots_ref = bf16[4,16,32,256]{3,2,1,0:T(8,128)(2,1)} custom-call(bf16[64,32,256]{2,1,0:T(8,128)(2,1)} %bitcast.3), custom_call_target="tpu_custom_call" | custom-call | tf_op jit(solution)/shard_map/pallas_call | solution.py:139
  65.1 5.5 %shard_map.39 = bf16[2,4,1024,128]{3,2,1,0:T(8,128)(2,1)} custom-call(bf16[2,1024,512]{2,1,0:T(8,128)(2,1)} %mix_ref.1, bf16[4,16,32,256]{3,2,1,0:T(8,128)(2,1)} %shard_map.38.slots_ref), custom_call_target="tpu_custom_call" | custom-call | tf_op jit(solution)/shard_map/pallas_call | solution.py:173
  (2 shorter events, 0.0 us)
Async XLA Ops:
  0.0 4.0 %copy-start = (f32[2,64,1024]{2,1,0:T(8,128)S(1)}, f32[2,64,1024]{2,1,0:T(8,128)}, u32[]{:S(2)}) copy-start(f32[2,64,1024]{2,1,0:T(8,128)} %spec_ref.1) | copy-start | bytes 1572868

commit v11 on v10

--- a/solution.py
+++ b/solution.py
@@ -43,14 +43,20 @@
 MESH = pl.DeviceIdType.MESH
 
 
-def exchange_kernel(width, x_ref, o_ref, slots, scatter_send, scatter_recv, gather_send, gather_recv,
-                    relay_send, relay_recv):
-    n_tm, n_bank = slots.shape[1], o_ref.shape[1]
+def exchange_kernel(width, x_ref, o_ref, plane_slots, part_buf, cross_slot, plane_send, plane_recv, cross_send,
+                    cross_recv, gather_send, gather_recv, relay_send, relay_recv):
+    plane = plane_slots.shape[2]
+    n_bank = o_ref.shape[1]
     depth = n_bank // width
     rows, basis = o_ref.shape[0], o_ref.shape[2]
     half = basis // 2
     me_tm = lax.axis_index("tm")
     me_bank = lax.axis_index("bank")
+    side = (me_tm // 2) % 2
+    partner = me_tm + 2 - 4 * side
+    in_plane = lambda q: (q // 2) * 4 + side * 2 + q % 2
+    partner_of = lambda t: t + 2 - 4 * side
+    me_q = (me_tm // 4) * 2 + me_tm % 2
     x = me_bank // depth
     z = me_bank % depth
     up = (z + 1) % depth
@@ -60,57 +66,55 @@
     near = [(x + step) % width * depth + z for step in range(1, width)]
     near += [xx * depth + up for xx in range(width)] + [xx * depth + down for xx in range(width)]
     barrier = pltpu.get_barrier_semaphore()
-    for step in range(1, n_tm):
-        pl.semaphore_signal(barrier, inc=1, device_id=at_tm((me_tm + step) % n_tm), device_id_type=MESH)
+    for step in range(1, plane):
+        pl.semaphore_signal(barrier, inc=1, device_id=at_tm(in_plane((me_q + step) % plane)), device_id_type=MESH)
+    pl.semaphore_signal(barrier, inc=1, device_id=at_tm(partner), device_id_type=MESH)
     for peer in near:
         pl.semaphore_signal(barrier, inc=1, device_id=at_bank(peer), device_id_type=MESH)
-    pl.semaphore_wait(barrier, n_tm - 1 + len(near))
+    pl.semaphore_wait(barrier, plane + len(near))
 
     def remote(src, dst, send, recv, device):
         return pltpu.make_async_remote_copy(
             src_ref=src, dst_ref=dst, send_sem=send, recv_sem=recv, device_id=device, device_id_type=MESH
         )
 
-    def relays(r):
-        out = []
-        for xx in range(width):
-            out.append((xx * depth + down, 0, x * depth + up, 0, xx))
-            out.append((xx * depth + up, half, x * depth + down, 1, xx))
-        return out
-
     sends = []
     for r in range(rows):
-        for step in range(1, n_tm):
-            peer = (me_tm + step) % n_tm
-            copy = remote(
-                x_ref.at[peer * rows + r], slots.at[r, me_tm],
-                scatter_send.at[r, peer], scatter_recv.at[r, me_tm], at_tm(peer),
-            )
-            copy.start()
-            sends.append(copy)
-
-    def forward(r):
-        for source in near:
-            remote(
-                o_ref.at[r, source], o_ref.at[r, source],
-                gather_send.at[r, source], gather_recv.at[r, source], at_bank(source),
-            ).wait_recv()
-        for slot, start, target, way, xx in relays(r):
-            block = o_ref.at[r, slot, pl.ds(start, half)]
-            copy = remote(block, block, relay_send.at[r, way, xx], relay_recv.at[r, way, xx], at_bank(target))
-            copy.start()
-            sends.append(copy)
-
-    for r in range(rows):
-        total = x_ref[me_tm * rows + r].astype(jnp.float32)
-        for step in range(1, n_tm):
-            source = (me_tm + n_tm - step) % n_tm
-            remote(
-                x_ref.at[r], slots.at[r, source],
-                scatter_send.at[r, source], scatter_recv.at[r, source], at_tm(source),
-            ).wait_recv()
-            total = total + slots[r, source].astype(jnp.float32)
-        o_ref[r, me_bank] = total.astype(o_ref.dtype)
+        for step in range(1, plane):
+            q = (me_q + step) % plane
+            peer = in_plane(q)
+            for which, owner in ((0, peer), (1, partner_of(peer))):
+                copy = remote(
+                    x_ref.at[owner * rows + r], plane_slots.at[r, which, me_q],
+                    plane_send.at[r, which, q], plane_recv.at[r, which, me_q], at_tm(peer),
+                )
+                copy.start()
+                sends.append(copy)
+
+    def cross(r):
+        return remote(part_buf.at[r], cross_slot.at[r], cross_send.at[r], cross_recv.at[r], at_tm(partner))
+
+    def reduce_plane(r):
+        own = x_ref[me_tm * rows + r].astype(jnp.float32)
+        other = x_ref[partner * rows + r].astype(jnp.float32)
+        for step in range(1, plane):
+            q = (me_q + plane - step) % plane
+            for which in (0, 1):
+                remote(
+                    x_ref.at[r], plane_slots.at[r, which, q],
+                    plane_send.at[r, which, q], plane_recv.at[r, which, q], at_tm(in_plane(q)),
+                ).wait_recv()
+            own = own + plane_slots[r, 0, q].astype(jnp.float32)
+            other = other + plane_slots[r, 1, q].astype(jnp.float32)
+        part_buf[r] = other
+        copy = cross(r)
+        copy.start()
+        sends.append(copy)
+        return own
+
+    def finish(r, own):
+        cross(r).wait_recv()
+        o_ref[r, me_bank] = (own + cross_slot[r]).astype(o_ref.dtype)
         for peer in near:
             copy = remote(
                 o_ref.at[r, me_bank], o_ref.at[r, me_bank],
@@ -118,9 +122,31 @@
             )
             copy.start()
             sends.append(copy)
-        if r >= 1:
-            forward(r - 1)
-    forward(rows - 1)
+
+    def forward(r):
+        for source in near:
+            remote(
+                o_ref.at[r, source], o_ref.at[r, source],
+                gather_send.at[r, source], gather_recv.at[r, source], at_bank(source),
+            ).wait_recv()
+        for xx in range(width):
+            for slot, start, target, way in (
+                (xx * depth + down, 0, x * depth + up, 0),
+                (xx * depth + up, half, x * depth + down, 1),
+            ):
+                block = o_ref.at[r, slot, pl.ds(start, half)]
+                copy = remote(block, block, relay_send.at[r, way, xx], relay_recv.at[r, way, xx], at_bank(target))
+                copy.start()
+                sends.append(copy)
+
+    sums = [None] * rows
+    for r in range(rows + 2):
+        if r < rows:
+            sums[r] = reduce_plane(r)
+        if 1 <= r <= rows:
+            finish(r - 1, sums[r - 1])
+        if r >= 2:
+            forward(r - 2)
     across = (z + 2) % depth
     for r in range(rows):
         for xx in range(width):
@@ -136,15 +162,20 @@
 def exchange(x, n_tm, n_bank, width):
     rows = x.shape[0] // n_tm
     block = x.shape[1:]
+    plane = n_tm // 2
     return pl.pallas_call(
         functools.partial(exchange_kernel, width),
         out_shape=jax.ShapeDtypeStruct((rows, n_bank) + block, x.dtype),
         in_specs=[pl.BlockSpec(memory_space=pltpu.VMEM)],
         out_specs=pl.BlockSpec(memory_space=pltpu.VMEM),
         scratch_shapes=[
-            pltpu.VMEM((rows, n_tm) + block, x.dtype),
-            pltpu.SemaphoreType.DMA((rows, n_tm)),
-            pltpu.SemaphoreType.DMA((rows, n_tm)),
+            pltpu.VMEM((rows, 2, plane) + block, x.dtype),
+            pltpu.VMEM((rows,) + block, jnp.float32),
+            pltpu.VMEM((rows,) + block, jnp.float32),
+            pltpu.SemaphoreType.DMA((rows, 2, plane)),
+            pltpu.SemaphoreType.DMA((rows, 2, plane)),
+            pltpu.SemaphoreType.DMA((rows,)),
+            pltpu.SemaphoreType.DMA((rows,)),
             pltpu.SemaphoreType.DMA((rows, n_bank)),
             pltpu.SemaphoreType.DMA((rows, n_bank)),
             pltpu.SemaphoreType.DMA((rows, 2, width)),

time: 70.7 us -> 71.9 us (1.017)
  no operation moved by 1% of the time
where the time goes in v11:
time: 71.9 us; the launch traced here: 71.2 us
  Pallas kernels  65.7 us (91%)
  other arithmetic  3.97 us (6%)
  local copies, waits for them, and re-layouts  1.56 us (2%)
    pallas_call x1, Pallas kernels, exchange(): pl.pallas_call(functools.partial(exchange_kernel, width), out_shape=jax.S...  49.4 us
    pallas_call x1, Pallas kernels, front(): pl.pallas_call(front_kernel, grid=(basis // block,), out_shape=jax.ShapeD...  10.8 us
    pallas_call x1, Pallas kernels, mix(): pl.pallas_call(mix_kernel, out_shape=jax.ShapeDtypeStruct((2, rows, templ...  5.52 us
    convert_element_type x1, other arithmetic, wave_block(): cosine = jnp.cos(angle).astype(jnp.bfloat16)  2.48 us
    pallas_call x1, local copies, waits for them, and re-layouts, front(): pl.pallas_call(front_kernel, grid=(basis // block,), out_shape=jax.ShapeD...  1.55 us

profile of v11, /device:TPU:6, one launch (start us, length us, event | category | flops | bytes accessed | tf_op | source)
XLA Modules:
  0.0 71.2 jit_solution(2793053366219956763)
XLA Ops:
  0.0 0.0 copy-start
  0.0 0.1 fusion.17
  0.2 0.2 sine_convert_fusion.1
  0.3 0.1 maximum_maximum_fusion.table_ref
  0.4 2.5 %cosine_convert_fusion = (bf16[1024,128]{1,0:T(8,128)(2,1)S(1)}, bf16[1024,128]{1,0:T(8,128)(2,1)S(1)}) fusion(s32[128]{0:T(128)S(1)} %iota_add_fusion.1, s32[1024]{0:T(1024)S(1)} %iota_add_fusion), kind=kLoop, calls=%fused_computation.11 | loop fusion | flops 2097152 | bytes 528896 | tf_op jit(solution)/shard_map/convert_element_type | solution.py:31
  2.9 0.1 pad_maximum_fusion.wave_ref
  3.0 1.0 %fusion.9 = (f32[64,1024]{1,0:T(8,128)S(1)}, f32[64,1024]{1,0:T(8,128)S(1)}) fusion(s32[1024]{0:T(1024)S(1)} %iota_add_fusion), kind=kLoop, calls=%fused_computation.21 | loop fusion | flops 917504 | bytes 528384 | tf_op jit(solution)/shard_map/sin | solution.py:40
  4.0 0.0 copy-done
  4.0 10.8 %shard_map.37 = bf16[32,64,256]{2,1,0:T(8,128)(2,1)S(1)} custom-call(f32[2,64,1024]{2,1,0:T(8,128)S(1)} %copy-done, bf16[2,32,64,1024]{3,2,1,0:T(8,128)(2,1)} %filt_ref.1, bf16[128,128]{1,0:T(8,128)(2,1)S(1)} %maximum_maximum_fusion.table_ref, f32[64,1024]{1,0:T(8,128)S(1)} %get-tuple-element.8.tcos_ref, f32[64,1024]{1,0:T(8,128)S(1)} %get-tuple-element.7.tsin_ref, ...), custom_call_target="tpu_custom_call" | custom-call | tf_op jit(solution)/shard_map/pallas_call | solution.py:248
  14.8 1.6 %copy.6 = bf16[32,64,256]{2,0,1:T(8,128)(2,1)} copy(bf16[32,64,256]{2,1,0:T(8,128)(2,1)S(1)} %shard_map.37) | data formatting | bytes 2097152 | tf_op jit(solution)/shard_map/pallas_call | solution.py:248
  16.3 49.4 %shard_map.38.slots_ref = bf16[4,16,32,256]{3,2,1,0:T(8,128)(2,1)} custom-call(bf16[64,32,256]{2,1,0:T(8,128)(2,1)} %bitcast.3), custom_call_target="tpu_custom_call" | custom-call | tf_op jit(solution)/shard_map/pallas_call | solution.py:166
  65.7 5.5 %shard_map.39 = bf16[2,4,1024,128]{3,2,1,0:T(8,128)(2,1)} custom-call(bf16[2,1024,512]{2,1,0:T(8,128)(2,1)} %mix_ref.1, bf16[4,16,32,256]{3,2,1,0:T(8,128)(2,1)} %shard_map.38.slots_ref), custom_call_target="tpu_custom_call" | custom-call | tf_op jit(solution)/shard_map/pallas_call | solution.py:204
  (2 shorter events, 0.0 us)
Async XLA Ops:
  0.0 4.0 %copy-start = (f32[2,64,1024]{2,1,0:T(8,128)S(1)}, f32[2,64,1024]{2,1,0:T(8,128)}, u32[]{:S(2)}) copy-start(f32[2,64,1024]{2,1,0:T(8,128)} %spec_ref.1) | copy-start | bytes 1572868

commit v12 on v8

--- a/solution.py
+++ b/solution.py
@@ -43,11 +43,12 @@
 MESH = pl.DeviceIdType.MESH
 
 
-def exchange_kernel(width, x_ref, o_ref, slots, scatter_send, scatter_recv, gather_send, gather_recv,
+def exchange_kernel(width, group, x_ref, o_ref, slots, scatter_send, scatter_recv, gather_send, gather_recv,
                     relay_send, relay_recv):
     n_tm, n_bank = slots.shape[1], o_ref.shape[0]
     depth = n_bank // width
     rows, basis = o_ref.shape[1], o_ref.shape[2]
+    stages = rows // group
     half = basis // 2
     me_tm = lax.axis_index("tm")
     me_bank = lax.axis_index("bank")
@@ -71,7 +72,7 @@
             src_ref=src, dst_ref=dst, send_sem=send, recv_sem=recv, device_id=device, device_id_type=MESH
         )
 
-    def relays(r):
+    def relays(g):
         out = []
         for xx in range(width):
             out.append((xx * depth + down, 0, x * depth + up, 0, xx))
@@ -79,76 +80,81 @@
         return out
 
     sends = []
-    for r in range(rows):
+    for g in range(stages):
+        part = pl.ds(g * group, group)
         for step in range(1, n_tm):
             peer = (me_tm + step) % n_tm
             copy = remote(
-                x_ref.at[peer * rows + r], slots.at[r, me_tm],
-                scatter_send.at[r, peer], scatter_recv.at[r, me_tm], at_tm(peer),
+                x_ref.at[pl.ds(peer * rows + g * group, group)], slots.at[part, me_tm],
+                scatter_send.at[g, peer], scatter_recv.at[g, me_tm], at_tm(peer),
             )
             copy.start()
             sends.append(copy)
 
-    def forward(r):
+    def forward(g):
+        part = pl.ds(g * group, group)
         for source in near:
             remote(
-                o_ref.at[source, r], o_ref.at[source, r],
-                gather_send.at[r, source], gather_recv.at[r, source], at_bank(source),
+                o_ref.at[source, part], o_ref.at[source, part],
+                gather_send.at[g, source], gather_recv.at[g, source], at_bank(source),
             ).wait_recv()
-        for slot, start, target, way, xx in relays(r):
-            block = o_ref.at[slot, r, pl.ds(start, half)]
-            copy = remote(block, block, relay_send.at[r, way, xx], relay_recv.at[r, way, xx], at_bank(target))
+        for slot, start, target, way, xx in relays(g):
+            block = o_ref.at[slot, part, pl.ds(start, half)]
+            copy = remote(block, block, relay_send.at[g, way, xx], relay_recv.at[g, way, xx], at_bank(target))
             copy.start()
             sends.append(copy)
 
-    for r in range(rows):
-        total = x_ref[me_tm * rows + r].astype(jnp.float32)
+    for g in range(stages):
+        part = pl.ds(g * group, group)
+        total = x_ref[pl.ds(me_tm * rows + g * group, group)].astype(jnp.float32)
         for step in range(1, n_tm):
             source = (me_tm + n_tm - step) % n_tm
             remote(
-                x_ref.at[r], slots.at[r, source],
-                scatter_send.at[r, source], scatter_recv.at[r, source], at_tm(source),
+                x_ref.at[pl.ds(0, group)], slots.at[part, source],
+                scatter_send.at[g, source], scatter_recv.at[g, source], at_tm(source),
             ).wait_recv()
-            total = total + slots[r, source].astype(jnp.float32)
-        o_ref[me_bank, r] = total.astype(o_ref.dtype)
+            total = total + slots[part, source].astype(jnp.float32)
+        o_ref[me_bank, part] = total.astype(o_ref.dtype)
         for peer in near:
             copy = remote(
-                o_ref.at[me_bank, r], o_ref.at[me_bank, r],
-                gather_send.at[r, peer], gather_recv.at[r, me_bank], at_bank(peer),
+                o_ref.at[me_bank, part], o_ref.at[me_bank, part],
+                gather_send.at[g, peer], gather_recv.at[g, me_bank], at_bank(peer),
             )
             copy.start()
             sends.append(copy)
-        if r >= 1:
-            forward(r - 1)
-    forward(rows - 1)
+        if g >= 1:
+            forward(g - 1)
+    forward(stages - 1)
     across = (z + 2) % depth
-    for r in range(rows):
+    for g in range(stages):
+        part = pl.ds(g * group, group)
         for xx in range(width):
             for way, start, via in ((0, 0, down), (1, half, up)):
-                block = o_ref.at[xx * depth + across, r, pl.ds(start, half)]
+                block = o_ref.at[xx * depth + across, part, pl.ds(start, half)]
                 remote(
-                    block, block, relay_send.at[r, way, xx], relay_recv.at[r, way, xx], at_bank(x * depth + via)
+                    block, block, relay_send.at[g, way, xx], relay_recv.at[g, way, xx], at_bank(x * depth + via)
                 ).wait_recv()
     for copy in sends:
         copy.wait_send()
 
 
-def exchange(x, n_tm, n_bank, width):
+def exchange(x, n_tm, n_bank, width, group=2):
     rows = x.shape[0] // n_tm
+    stages = rows // group
     block = x.shape[1:]
     return pl.pallas_call(
-        functools.partial(exchange_kernel, width),
+        functools.partial(exchange_kernel, width, group),
         out_shape=jax.ShapeDtypeStruct((n_bank, rows) + block, x.dtype),
         in_specs=[pl.BlockSpec(memory_space=pltpu.VMEM)],
         out_specs=pl.BlockSpec(memory_space=pltpu.VMEM),
         scratch_shapes=[
             pltpu.VMEM((rows, n_tm) + block, x.dtype),
-            pltpu.SemaphoreType.DMA((rows, n_tm)),
-            pltpu.SemaphoreType.DMA((rows, n_tm)),
-            pltpu.SemaphoreType.DMA((rows, n_bank)),
-            pltpu.SemaphoreType.DMA((rows, n_bank)),
-            pltpu.SemaphoreType.DMA((rows, 2, width)),
-            pltpu.SemaphoreType.DMA((rows, 2, width)),
+            pltpu.SemaphoreType.DMA((stages, n_tm)),
+            pltpu.SemaphoreType.DMA((stages, n_tm)),
+            pltpu.SemaphoreType.DMA((stages, n_bank)),
+            pltpu.SemaphoreType.DMA((stages, n_bank)),
+            pltpu.SemaphoreType.DMA((stages, 2, width)),
+            pltpu.SemaphoreType.DMA((stages, 2, width)),
         ],
         compiler_params=pltpu.CompilerParams(collective_id=0, has_side_effects=True),
     )(x)

time: 70.7 us -> 67.5 us (0.955)
  Pallas kernels: 65 us -> 61.8 us
    pallas_call x1, Pallas kernels: 48.7 us -> 45.6 us  [exchange(): pl.pallas_call(functools.partial(exchange_kernel, width, group), out_shap...]
where the time goes in v12:
time: 67.5 us; the launch traced here: 67.4 us
  Pallas kernels  61.8 us (92%)
  other arithmetic  3.97 us (6%)
  local copies, waits for them, and re-layouts  1.56 us (2%)
    pallas_call x1, Pallas kernels, exchange(): pl.pallas_call(functools.partial(exchange_kernel, width, group), out_shap...  45.6 us
    pallas_call x1, Pallas kernels, front(): pl.pallas_call(front_kernel, grid=(basis // block,), out_shape=jax.ShapeD...  10.8 us
    pallas_call x1, Pallas kernels, mix(): pl.pallas_call(mix_kernel, out_shape=jax.ShapeDtypeStruct((2, rows, templ...  5.51 us
    convert_element_type x1, other arithmetic, wave_block(): cosine = jnp.cos(angle).astype(jnp.bfloat16)  2.48 us
    pallas_call x1, local copies, waits for them, and re-layouts, front(): pl.pallas_call(front_kernel, grid=(basis // block,), out_shape=jax.ShapeD...  1.55 us

profile of v12, /device:TPU:6, one launch (start us, length us, event | category | flops | bytes accessed | tf_op | source)
XLA Modules:
  0.0 67.4 jit_solution(6454777539756778802)
XLA Ops:
  0.0 0.0 copy-start
  0.0 0.1 fusion.17
  0.2 0.2 sine_convert_fusion.1
  0.3 0.1 maximum_maximum_fusion.table_ref
  0.4 2.5 %cosine_convert_fusion = (bf16[1024,128]{1,0:T(8,128)(2,1)S(1)}, bf16[1024,128]{1,0:T(8,128)(2,1)S(1)}) fusion(s32[128]{0:T(128)S(1)} %iota_add_fusion.1, s32[1024]{0:T(1024)S(1)} %iota_add_fusion), kind=kLoop, calls=%fused_computation.11 | loop fusion | flops 2097152 | bytes 528896 | tf_op jit(solution)/shard_map/convert_element_type | solution.py:31
  2.9 0.1 pad_maximum_fusion.wave_ref
  3.0 1.0 %fusion.9 = (f32[64,1024]{1,0:T(8,128)S(1)}, f32[64,1024]{1,0:T(8,128)S(1)}) fusion(s32[1024]{0:T(1024)S(1)} %iota_add_fusion), kind=kLoop, calls=%fused_computation.21 | loop fusion | flops 917504 | bytes 528384 | tf_op jit(solution)/shard_map/sin | solution.py:40
  4.0 0.0 copy-done
  4.0 10.8 %shard_map.37 = bf16[32,64,256]{2,1,0:T(8,128)(2,1)S(1)} custom-call(f32[2,64,1024]{2,1,0:T(8,128)S(1)} %copy-done, bf16[2,32,64,1024]{3,2,1,0:T(8,128)(2,1)} %filt_ref.1, bf16[128,128]{1,0:T(8,128)(2,1)S(1)} %maximum_maximum_fusion.table_ref, f32[64,1024]{1,0:T(8,128)S(1)} %get-tuple-element.8.tcos_ref, f32[64,1024]{1,0:T(8,128)S(1)} %get-tuple-element.7.tsin_ref, ...), custom_call_target="tpu_custom_call" | custom-call | tf_op jit(solution)/shard_map/pallas_call | solution.py:226
  14.8 1.6 %copy.6 = bf16[32,64,256]{2,0,1:T(8,128)(2,1)} copy(bf16[32,64,256]{2,1,0:T(8,128)(2,1)S(1)} %shard_map.37) | data formatting | bytes 2097152 | tf_op jit(solution)/shard_map/pallas_call | solution.py:226
  16.3 45.6 %shard_map.38.slots_ref = bf16[16,4,32,256]{3,2,1,0:T(8,128)(2,1)} custom-call(bf16[64,32,256]{2,1,0:T(8,128)(2,1)} %bitcast.3), custom_call_target="tpu_custom_call" | custom-call | tf_op jit(solution)/shard_map/pallas_call | solution.py:145
  61.9 5.5 %shard_map.39 = bf16[2,4,1024,128]{3,2,1,0:T(8,128)(2,1)} custom-call(bf16[2,1024,512]{2,1,0:T(8,128)(2,1)} %mix_ref.1, bf16[16,4,32,256]{3,2,1,0:T(8,128)(2,1)} %shard_map.38.slots_ref), custom_call_target="tpu_custom_call" | custom-call | tf_op jit(solution)/shard_map/pallas_call | solution.py:182
  (2 shorter events, 0.0 us)
Async XLA Ops:
  0.0 4.0 %copy-start = (f32[2,64,1024]{2,1,0:T(8,128)S(1)}, f32[2,64,1024]{2,1,0:T(8,128)}, u32[]{:S(2)}) copy-start(f32[2,64,1024]{2,1,0:T(8,128)} %spec_ref.1) | copy-start | bytes 1572868

commit v13 on v12

--- a/solution.py
+++ b/solution.py
@@ -138,7 +138,7 @@
         copy.wait_send()
 
 
-def exchange(x, n_tm, n_bank, width, group=2):
+def exchange(x, n_tm, n_bank, width, group=4):
     rows = x.shape[0] // n_tm
     stages = rows // group
     block = x.shape[1:]

time: 67.5 us -> 72.5 us (1.074)
  Pallas kernels: 61.8 us -> 66.6 us
    pallas_call x1, Pallas kernels: 45.6 us -> 50.3 us  [exchange(): pl.pallas_call(functools.partial(exchange_kernel, width, group), out_shap...]
where the time goes in v13:
time: 72.5 us; the launch traced here: 72.2 us
  Pallas kernels  66.6 us (92%)
  other arithmetic  3.97 us (5%)
  local copies, waits for them, and re-layouts  1.56 us (2%)
    pallas_call x1, Pallas kernels, exchange(): pl.pallas_call(functools.partial(exchange_kernel, width, group), out_shap...  50.3 us
    pallas_call x1, Pallas kernels, front(): pl.pallas_call(front_kernel, grid=(basis // block,), out_shape=jax.ShapeD...  10.8 us
    pallas_call x1, Pallas kernels, mix(): pl.pallas_call(mix_kernel, out_shape=jax.ShapeDtypeStruct((2, rows, templ...  5.51 us
    convert_element_type x1, other arithmetic, wave_block(): cosine = jnp.cos(angle).astype(jnp.bfloat16)  2.48 us
    pallas_call x1, local copies, waits for them, and re-layouts, front(): pl.pallas_call(front_kernel, grid=(basis // block,), out_shape=jax.ShapeD...  1.55 us

profile of v13, /device:TPU:6, one launch (start us, length us, event | category | flops | bytes accessed | tf_op | source)
XLA Modules:
  0.0 72.2 jit_solution(12845671859331902299)
XLA Ops:
  0.0 0.0 copy-start
  0.0 0.1 fusion.17
  0.2 0.2 sine_convert_fusion.1
  0.3 0.1 maximum_maximum_fusion.table_ref
  0.4 2.5 %cosine_convert_fusion = (bf16[1024,128]{1,0:T(8,128)(2,1)S(1)}, bf16[1024,128]{1,0:T(8,128)(2,1)S(1)}) fusion(s32[128]{0:T(128)S(1)} %iota_add_fusion.1, s32[1024]{0:T(1024)S(1)} %iota_add_fusion), kind=kLoop, calls=%fused_computation.11 | loop fusion | flops 2097152 | bytes 528896 | tf_op jit(solution)/shard_map/convert_element_type | solution.py:31
  2.9 0.1 pad_maximum_fusion.wave_ref
  3.0 1.0 %fusion.9 = (f32[64,1024]{1,0:T(8,128)S(1)}, f32[64,1024]{1,0:T(8,128)S(1)}) fusion(s32[1024]{0:T(1024)S(1)} %iota_add_fusion), kind=kLoop, calls=%fused_computation.21 | loop fusion | flops 917504 | bytes 528384 | tf_op jit(solution)/shard_map/sin | solution.py:40
  4.0 0.0 copy-done
  4.0 10.8 %shard_map.37 = bf16[32,64,256]{2,1,0:T(8,128)(2,1)S(1)} custom-call(f32[2,64,1024]{2,1,0:T(8,128)S(1)} %copy-done, bf16[2,32,64,1024]{3,2,1,0:T(8,128)(2,1)} %filt_ref.1, bf16[128,128]{1,0:T(8,128)(2,1)S(1)} %maximum_maximum_fusion.table_ref, f32[64,1024]{1,0:T(8,128)S(1)} %get-tuple-element.8.tcos_ref, f32[64,1024]{1,0:T(8,128)S(1)} %get-tuple-element.7.tsin_ref, ...), custom_call_target="tpu_custom_call" | custom-call | tf_op jit(solution)/shard_map/pallas_call | solution.py:226
  14.8 1.6 %copy.6 = bf16[32,64,256]{2,0,1:T(8,128)(2,1)} copy(bf16[32,64,256]{2,1,0:T(8,128)(2,1)S(1)} %shard_map.37) | data formatting | bytes 2097152 | tf_op jit(solution)/shard_map/pallas_call | solution.py:226
  16.3 50.3 %shard_map.38.slots_ref = bf16[16,4,32,256]{3,2,1,0:T(8,128)(2,1)} custom-call(bf16[64,32,256]{2,1,0:T(8,128)(2,1)} %bitcast.3), custom_call_target="tpu_custom_call" | custom-call | tf_op jit(solution)/shard_map/pallas_call | solution.py:145
  66.7 5.5 %shard_map.39 = bf16[2,4,1024,128]{3,2,1,0:T(8,128)(2,1)} custom-call(bf16[2,1024,512]{2,1,0:T(8,128)(2,1)} %mix_ref.1, bf16[16,4,32,256]{3,2,1,0:T(8,128)(2,1)} %shard_map.38.slots_ref), custom_call_target="tpu_custom_call" | custom-call | tf_op jit(solution)/shard_map/pallas_call | solution.py:182
  (2 shorter events, 0.0 us)
Async XLA Ops:
  0.0 4.0 %copy-start = (f32[2,64,1024]{2,1,0:T(8,128)S(1)}, f32[2,64,1024]{2,1,0:T(8,128)}, u32[]{:S(2)}) copy-start(f32[2,64,1024]{2,1,0:T(8,128)} %spec_ref.1) | copy-start | bytes 1572868

commit v14 on v12

--- a/solution.py
+++ b/solution.py
@@ -219,7 +219,7 @@
     o_ref[...] = result.reshape(o_ref.shape).astype(o_ref.dtype)
 
 
-def front(spectrum, filters, table, twist_cos, twist_sin, wave, block=8):
+def front(spectrum, filters, table, twist_cos, twist_sin, wave, block=16):
     _, basis, inner, freq = filters.shape
     cols = wave.shape[1]
     whole = lambda *shape: pl.BlockSpec(shape, lambda i: (0,) * len(shape))

time: 67.5 us -> 67.6 us (level)
  no operation moved by 1% of the time
where the time goes in v14:
time: 67.6 us; the launch traced here: 67.4 us
  Pallas kernels  61.9 us (92%)
  other arithmetic  3.97 us (6%)
  local copies, waits for them, and re-layouts  1.56 us (2%)
    pallas_call x1, Pallas kernels, exchange(): pl.pallas_call(functools.partial(exchange_kernel, width, group), out_shap...  45.6 us
    pallas_call x1, Pallas kernels, front(): pl.pallas_call(front_kernel, grid=(basis // block,), out_shape=jax.ShapeD...  10.8 us
    pallas_call x1, Pallas kernels, mix(): pl.pallas_call(mix_kernel, out_shape=jax.ShapeDtypeStruct((2, rows, templ...  5.51 us
    convert_element_type x1, other arithmetic, wave_block(): cosine = jnp.cos(angle).astype(jnp.bfloat16)  2.48 us
    pallas_call x1, local copies, waits for them, and re-layouts, front(): pl.pallas_call(front_kernel, grid=(basis // block,), out_shape=jax.ShapeD...  1.55 us

profile of v14, /device:TPU:6, one launch (start us, length us, event | category | flops | bytes accessed | tf_op | source)
XLA Modules:
  0.0 67.4 jit_solution(6733188763346450362)
XLA Ops:
  0.0 0.0 copy-start
  0.0 0.1 fusion.17
  0.2 0.2 sine_convert_fusion.1
  0.3 0.1 maximum_maximum_fusion.table_ref
  0.4 2.5 %cosine_convert_fusion = (bf16[1024,128]{1,0:T(8,128)(2,1)S(1)}, bf16[1024,128]{1,0:T(8,128)(2,1)S(1)}) fusion(s32[128]{0:T(128)S(1)} %iota_add_fusion.1, s32[1024]{0:T(1024)S(1)} %iota_add_fusion), kind=kLoop, calls=%fused_computation.11 | loop fusion | flops 2097152 | bytes 528896 | tf_op jit(solution)/shard_map/convert_element_type | solution.py:31
  2.9 0.1 pad_maximum_fusion.wave_ref
  3.0 1.0 %fusion.9 = (f32[64,1024]{1,0:T(8,128)S(1)}, f32[64,1024]{1,0:T(8,128)S(1)}) fusion(s32[1024]{0:T(1024)S(1)} %iota_add_fusion), kind=kLoop, calls=%fused_computation.21 | loop fusion | flops 917504 | bytes 528384 | tf_op jit(solution)/shard_map/sin | solution.py:40
  4.0 0.0 copy-done
  4.0 10.8 %shard_map.37 = bf16[32,64,256]{2,1,0:T(8,128)(2,1)S(1)} custom-call(f32[2,64,1024]{2,1,0:T(8,128)S(1)} %copy-done, bf16[2,32,64,1024]{3,2,1,0:T(8,128)(2,1)} %filt_ref.1, bf16[128,128]{1,0:T(8,128)(2,1)S(1)} %maximum_maximum_fusion.table_ref, f32[64,1024]{1,0:T(8,128)S(1)} %get-tuple-element.8.tcos_ref, f32[64,1024]{1,0:T(8,128)S(1)} %get-tuple-element.7.tsin_ref, ...), custom_call_target="tpu_custom_call" | custom-call | tf_op jit(solution)/shard_map/pallas_call | solution.py:226
  14.8 1.6 %copy.6 = bf16[32,64,256]{2,0,1:T(8,128)(2,1)} copy(bf16[32,64,256]{2,1,0:T(8,128)(2,1)S(1)} %shard_map.37) | data formatting | bytes 2097152 | tf_op jit(solution)/shard_map/pallas_call | solution.py:226
  16.3 45.6 %shard_map.38.slots_ref = bf16[16,4,32,256]{3,2,1,0:T(8,128)(2,1)} custom-call(bf16[64,32,256]{2,1,0:T(8,128)(2,1)} %bitcast.3), custom_call_target="tpu_custom_call" | custom-call | tf_op jit(solution)/shard_map/pallas_call | solution.py:145
  61.9 5.5 %shard_map.39 = bf16[2,4,1024,128]{3,2,1,0:T(8,128)(2,1)} custom-call(bf16[2,1024,512]{2,1,0:T(8,128)(2,1)} %mix_ref.1, bf16[16,4,32,256]{3,2,1,0:T(8,128)(2,1)} %shard_map.38.slots_ref), custom_call_target="tpu_custom_call" | custom-call | tf_op jit(solution)/shard_map/pallas_call | solution.py:182
  (2 shorter events, 0.0 us)
Async XLA Ops:
  0.0 4.0 %copy-start = (f32[2,64,1024]{2,1,0:T(8,128)S(1)}, f32[2,64,1024]{2,1,0:T(8,128)}, u32[]{:S(2)}) copy-start(f32[2,64,1024]{2,1,0:T(8,128)} %spec_ref.1) | copy-start | bytes 1572868

commit v15 on v12

--- a/solution.py
+++ b/solution.py
@@ -216,7 +216,8 @@
     result = jnp.concatenate(
         [from_real[:, :cols] - from_imag[:, cols:], from_real[:, cols:] + from_imag[:, :cols]], axis=1
     )
-    o_ref[...] = result.reshape(o_ref.shape).astype(o_ref.dtype)
+    for kk in range(block):
+        o_ref[:, kk, :] = result[kk * inner:(kk + 1) * inner].astype(o_ref.dtype)
 
 
 def front(spectrum, filters, table, twist_cos, twist_sin, wave, block=8):
@@ -226,7 +227,7 @@
     return pl.pallas_call(
         front_kernel,
         grid=(basis // block,),
-        out_shape=jax.ShapeDtypeStruct((basis, inner, cols), jnp.bfloat16),
+        out_shape=jax.ShapeDtypeStruct((inner, basis, cols), jnp.bfloat16),
         in_specs=[
             whole(2, inner, freq),
             pl.BlockSpec((2, block, inner, freq), lambda i: (0, i, 0, 0)),
@@ -235,7 +236,7 @@
             whole(inner, freq),
             whole(freq, cols),
         ],
-        out_specs=pl.BlockSpec((block, inner, cols), lambda i: (i, 0, 0)),
+        out_specs=pl.BlockSpec((inner, block, cols), lambda i: (0, i, 0)),
         scratch_shapes=[pltpu.VMEM((block * inner, 2 * freq), jnp.bfloat16)],
         compiler_params=pltpu.CompilerParams(vmem_limit_bytes=48 * 1024 * 1024),
     )(spectrum, filters, table, twist_cos, twist_sin, wave)
@@ -252,7 +253,7 @@
     twist_cos, twist_sin = twist_tables(freqs, inner, NSAMP)
     lags = START + jnp.arange(WROWS, dtype=jnp.int32)
     wave = wave_block(freqs, lags, outer)
-    partial = front(spectrum, filters, table, twist_cos, twist_sin, wave).transpose(1, 0, 2)
+    partial = front(spectrum, filters, table, twist_cos, twist_sin, wave)
     slots = exchange(partial, lax.axis_size("tm"), lax.axis_size("bank"), 4)
     return mix(mixing, slots)
 

time: 67.5 us -> 67.9 us (level)
  Pallas kernels: 61.8 us -> 62.7 us
    pallas_call x1 -> x0, local copies, waits for them, and re-layouts: 1.55 us -> none  [front(): pl.pallas_call(front_kernel, grid=(basis // block,), out_shape=jax.ShapeD...]
    unnamed x2 -> x4, local copies, waits for them, and re-layouts: 0.01 us -> 0.97 us
    pallas_call x1, Pallas kernels: 10.8 us -> 11.6 us  [front(): pl.pallas_call(front_kernel, grid=(basis // block,), out_shape=jax.ShapeD...]
where the time goes in v15:
time: 67.9 us; the launch traced here: 67.8 us
  Pallas kernels  62.7 us (92%)
  other arithmetic  3.97 us (6%)
  local copies, waits for them, and re-layouts  0.97 us (1%)
    pallas_call x1, Pallas kernels, exchange(): pl.pallas_call(functools.partial(exchange_kernel, width, group), out_shap...  45.6 us
    pallas_call x1, Pallas kernels, front(): pl.pallas_call(front_kernel, grid=(basis // block,), out_shape=jax.ShapeD...  11.6 us
    pallas_call x1, Pallas kernels, mix(): pl.pallas_call(mix_kernel, out_shape=jax.ShapeDtypeStruct((2, rows, templ...  5.51 us
    convert_element_type x1, other arithmetic, wave_block(): cosine = jnp.cos(angle).astype(jnp.bfloat16)  2.48 us

profile of v15, /device:TPU:6, one launch (start us, length us, event | category | flops | bytes accessed | tf_op | source)
XLA Modules:
  0.0 67.8 jit_solution(11428842610744317787)
XLA Ops:
  0.0 0.0 copy-start.1
  0.0 0.1 fusion.17
  0.2 0.2 sine_convert_fusion.1
  0.3 0.1 maximum_maximum_fusion.table_ref
  0.4 2.5 %cosine_convert_fusion = (bf16[1024,128]{1,0:T(8,128)(2,1)S(1)}, bf16[1024,128]{1,0:T(8,128)(2,1)S(1)}) fusion(s32[128]{0:T(128)S(1)} %iota_add_fusion.1, s32[1024]{0:T(1024)S(1)} %iota_add_fusion), kind=kLoop, calls=%fused_computation.10 | loop fusion | flops 2097152 | bytes 528896 | tf_op jit(solution)/shard_map/convert_element_type | solution.py:31
  2.9 0.1 pad_maximum_fusion.wave_ref
  3.0 1.0 %fusion.9 = (f32[64,1024]{1,0:T(8,128)S(1)}, f32[64,1024]{1,0:T(8,128)S(1)}) fusion(s32[1024]{0:T(1024)S(1)} %iota_add_fusion), kind=kLoop, calls=%fused_computation.20 | loop fusion | flops 917504 | bytes 528384 | tf_op jit(solution)/shard_map/sin | solution.py:40
  4.0 0.0 copy-done.1
  4.0 11.6 %shard_map.37.x_ref = bf16[64,32,256]{2,1,0:T(8,128)(2,1)S(1)} custom-call(f32[2,64,1024]{2,1,0:T(8,128)S(1)} %copy-done.1, bf16[2,32,64,1024]{3,2,1,0:T(8,128)(2,1)} %filt_ref.1, bf16[128,128]{1,0:T(8,128)(2,1)S(1)} %maximum_maximum_fusion.table_ref, f32[64,1024]{1,0:T(8,128)S(1)} %get-tuple-element.8.tcos_ref, f32[64,1024]{1,0:T(8,128)S(1)} %get-tuple-element.7.tsin_ref, ...), custom_call_target="tpu_custom_call" | custom-call | tf_op jit(solution)/shard_map/pallas_call | solution.py:227
  15.7 0.0 copy-start
  15.7 1.0 %copy-done = bf16[64,32,256]{2,1,0:T(8,128)(2,1)} copy-done((bf16[64,32,256]{2,1,0:T(8,128)(2,1)}, bf16[64,32,256]{2,1,0:T(8,128)(2,1)S(1)}, u32[]{:S(2)}) %copy-start) | copy-done | bytes 1048600
  16.6 45.6 %shard_map.38.slots_ref = bf16[16,4,32,256]{3,2,1,0:T(8,128)(2,1)} custom-call(bf16[64,32,256]{2,1,0:T(8,128)(2,1)} %copy-done), custom_call_target="tpu_custom_call" | custom-call | tf_op jit(solution)/shard_map/pallas_call | solution.py:145
  62.2 5.5 %shard_map.39 = bf16[2,4,1024,128]{3,2,1,0:T(8,128)(2,1)} custom-call(bf16[2,1024,512]{2,1,0:T(8,128)(2,1)} %mix_ref.1, bf16[16,4,32,256]{3,2,1,0:T(8,128)(2,1)} %shard_map.38.slots_ref), custom_call_target="tpu_custom_call" | custom-call | tf_op jit(solution)/shard_map/pallas_call | solution.py:182
  (2 shorter events, 0.0 us)
Async XLA Ops:
  0.0 4.0 %copy-start.1 = (f32[2,64,1024]{2,1,0:T(8,128)S(1)}, f32[2,64,1024]{2,1,0:T(8,128)}, u32[]{:S(2)}) copy-start(f32[2,64,1024]{2,1,0:T(8,128)} %spec_ref.1) | copy-start | bytes 1572868
  15.7 1.0 %copy-start = (bf16[64,32,256]{2,1,0:T(8,128)(2,1)}, bf16[64,32,256]{2,1,0:T(8,128)(2,1)S(1)}, u32[]{:S(2)}) copy-start(bf16[64,32,256]{2,1,0:T(8,128)(2,1)S(1)} %shard_map.37.x_ref) | copy-start | bytes 3145732

commit v16 on v12

--- a/solution.py
+++ b/solution.py
@@ -58,8 +58,8 @@
     down = (z + depth - 1) % depth
     at_tm = lambda peer: (peer, me_bank)
     at_bank = lambda peer: (me_tm, peer)
-    near = [(x + step) % width * depth + z for step in range(1, width)]
-    near += [xx * depth + up for xx in range(width)] + [xx * depth + down for xx in range(width)]
+    near = [xx * depth + up for xx in range(width)] + [xx * depth + down for xx in range(width)]
+    near += [(x + step) % width * depth + z for step in range(1, width)]
     barrier = pltpu.get_barrier_semaphore()
     for step in range(1, n_tm):
         pl.semaphore_signal(barrier, inc=1, device_id=at_tm((me_tm + step) % n_tm), device_id_type=MESH)

time: 67.5 us -> 67.6 us (level)
  no operation moved by 1% of the time
where the time goes in v16:
time: 67.6 us; the launch traced here: 67.5 us
  Pallas kernels  61.9 us (92%)
  other arithmetic  3.97 us (6%)
  local copies, waits for them, and re-layouts  1.56 us (2%)
    pallas_call x1, Pallas kernels, exchange(): pl.pallas_call(functools.partial(exchange_kernel, width, group), out_shap...  45.6 us
    pallas_call x1, Pallas kernels, front(): pl.pallas_call(front_kernel, grid=(basis // block,), out_shape=jax.ShapeD...  10.8 us
    pallas_call x1, Pallas kernels, mix(): pl.pallas_call(mix_kernel, out_shape=jax.ShapeDtypeStruct((2, rows, templ...  5.51 us
    convert_element_type x1, other arithmetic, wave_block(): cosine = jnp.cos(angle).astype(jnp.bfloat16)  2.48 us
    pallas_call x1, local copies, waits for them, and re-layouts, front(): pl.pallas_call(front_kernel, grid=(basis // block,), out_shape=jax.ShapeD...  1.55 us

profile of v16, /device:TPU:6, one launch (start us, length us, event | category | flops | bytes accessed | tf_op | source)
XLA Modules:
  0.0 67.5 jit_solution(2169588822684062766)
XLA Ops:
  0.0 0.0 copy-start
  0.0 0.1 fusion.17
  0.2 0.2 sine_convert_fusion.1
  0.3 0.1 maximum_maximum_fusion.table_ref
  0.4 2.5 %cosine_convert_fusion = (bf16[1024,128]{1,0:T(8,128)(2,1)S(1)}, bf16[1024,128]{1,0:T(8,128)(2,1)S(1)}) fusion(s32[128]{0:T(128)S(1)} %iota_add_fusion.1, s32[1024]{0:T(1024)S(1)} %iota_add_fusion), kind=kLoop, calls=%fused_computation.11 | loop fusion | flops 2097152 | bytes 528896 | tf_op jit(solution)/shard_map/convert_element_type | solution.py:31
  2.9 0.1 pad_maximum_fusion.wave_ref
  3.0 1.0 %fusion.9 = (f32[64,1024]{1,0:T(8,128)S(1)}, f32[64,1024]{1,0:T(8,128)S(1)}) fusion(s32[1024]{0:T(1024)S(1)} %iota_add_fusion), kind=kLoop, calls=%fused_computation.21 | loop fusion | flops 917504 | bytes 528384 | tf_op jit(solution)/shard_map/sin | solution.py:40
  4.0 0.0 copy-done
  4.0 10.8 %shard_map.37 = bf16[32,64,256]{2,1,0:T(8,128)(2,1)S(1)} custom-call(f32[2,64,1024]{2,1,0:T(8,128)S(1)} %copy-done, bf16[2,32,64,1024]{3,2,1,0:T(8,128)(2,1)} %filt_ref.1, bf16[128,128]{1,0:T(8,128)(2,1)S(1)} %maximum_maximum_fusion.table_ref, f32[64,1024]{1,0:T(8,128)S(1)} %get-tuple-element.8.tcos_ref, f32[64,1024]{1,0:T(8,128)S(1)} %get-tuple-element.7.tsin_ref, ...), custom_call_target="tpu_custom_call" | custom-call | tf_op jit(solution)/shard_map/pallas_call | solution.py:226
  14.8 1.6 %copy.6 = bf16[32,64,256]{2,0,1:T(8,128)(2,1)} copy(bf16[32,64,256]{2,1,0:T(8,128)(2,1)S(1)} %shard_map.37) | data formatting | bytes 2097152 | tf_op jit(solution)/shard_map/pallas_call | solution.py:226
  16.3 45.6 %shard_map.38.slots_ref = bf16[16,4,32,256]{3,2,1,0:T(8,128)(2,1)} custom-call(bf16[64,32,256]{2,1,0:T(8,128)(2,1)} %bitcast.3), custom_call_target="tpu_custom_call" | custom-call | tf_op jit(solution)/shard_map/pallas_call | solution.py:145
  61.9 5.5 %shard_map.39 = bf16[2,4,1024,128]{3,2,1,0:T(8,128)(2,1)} custom-call(bf16[2,1024,512]{2,1,0:T(8,128)(2,1)} %mix_ref.1, bf16[16,4,32,256]{3,2,1,0:T(8,128)(2,1)} %shard_map.38.slots_ref), custom_call_target="tpu_custom_call" | custom-call | tf_op jit(solution)/shard_map/pallas_call | solution.py:182
  (2 shorter events, 0.0 us)
Async XLA Ops:
  0.0 4.0 %copy-start = (f32[2,64,1024]{2,1,0:T(8,128)S(1)}, f32[2,64,1024]{2,1,0:T(8,128)}, u32[]{:S(2)}) copy-start(f32[2,64,1024]{2,1,0:T(8,128)} %spec_ref.1) | copy-start | bytes 1572868

commit v17 on v12

--- a/solution.py
+++ b/solution.py
@@ -161,29 +161,31 @@
 
 
 def mix_kernel(mix_ref, slots_ref, o_ref):
-    n, rows, _, cols = slots_ref.shape
+    n, _, _, cols = slots_ref.shape
     half = cols // 2
-    order = range(n)
     mix_real = mix_ref[0]
     mix_imag = mix_ref[1]
-    for t in range(rows):
-        plain = jnp.concatenate([slots_ref[slot, t] for slot in order], axis=0)
-        turned = jnp.concatenate([-plain[:, half:], plain[:, :half]], axis=1)
-        result = jnp.dot(mix_real, plain, preferred_element_type=jnp.float32) + jnp.dot(
-            mix_imag, turned, preferred_element_type=jnp.float32
-        )
-        o_ref[0, t] = result[:, :half].astype(o_ref.dtype)
-        o_ref[1, t] = result[:, half:].astype(o_ref.dtype)
+    plain = jnp.concatenate([slots_ref[slot, 0] for slot in range(n)], axis=0)
+    turned = jnp.concatenate([-plain[:, half:], plain[:, :half]], axis=1)
+    result = jnp.dot(mix_real, plain, preferred_element_type=jnp.float32) + jnp.dot(
+        mix_imag, turned, preferred_element_type=jnp.float32
+    )
+    o_ref[0, 0] = result[:, :half].astype(o_ref.dtype)
+    o_ref[1, 0] = result[:, half:].astype(o_ref.dtype)
 
 
 def mix(mixing, slots):
-    _, rows, _, cols = slots.shape
+    n, rows, basis, cols = slots.shape
     templates = mixing.shape[1]
     return pl.pallas_call(
         mix_kernel,
+        grid=(rows,),
         out_shape=jax.ShapeDtypeStruct((2, rows, templates, cols // 2), jnp.bfloat16),
-        in_specs=[pl.BlockSpec(memory_space=pltpu.VMEM)] * 2,
-        out_specs=pl.BlockSpec(memory_space=pltpu.VMEM),
+        in_specs=[
+            pl.BlockSpec(mixing.shape, lambda t: (0, 0, 0)),
+            pl.BlockSpec((n, 1, basis, cols), lambda t: (0, t, 0, 0)),
+        ],
+        out_specs=pl.BlockSpec((2, 1, templates, cols // 2), lambda t: (0, t, 0, 0)),
     )(mixing, slots)
 
 

time: 67.5 us -> 67.9 us (level)
  no operation moved by 1% of the time
where the time goes in v17:
time: 67.9 us; the launch traced here: 67.8 us
  Pallas kernels  62.2 us (92%)
  other arithmetic  3.97 us (6%)
  local copies, waits for them, and re-layouts  1.56 us (2%)
    pallas_call x1, Pallas kernels, exchange(): pl.pallas_call(functools.partial(exchange_kernel, width, group), out_shap...  45.6 us
    pallas_call x1, Pallas kernels, front(): pl.pallas_call(front_kernel, grid=(basis // block,), out_shape=jax.ShapeD...  10.8 us
    pallas_call x1, Pallas kernels, mix(): pl.pallas_call(mix_kernel, grid=(rows,), out_shape=jax.ShapeDtypeStruct((...  5.84 us
    convert_element_type x1, other arithmetic, wave_block(): cosine = jnp.cos(angle).astype(jnp.bfloat16)  2.48 us
    pallas_call x1, local copies, waits for them, and re-layouts, front(): pl.pallas_call(front_kernel, grid=(basis // block,), out_shape=jax.ShapeD...  1.55 us

profile of v17, /device:TPU:6, one launch (start us, length us, event | category | flops | bytes accessed | tf_op | source)
XLA Modules:
  0.0 67.8 jit_solution(15369430384115915528)
XLA Ops:
  0.0 0.0 copy-start
  0.0 0.1 fusion.17
  0.2 0.2 sine_convert_fusion.1
  0.3 0.1 maximum_maximum_fusion.table_ref
  0.4 2.5 %cosine_convert_fusion = (bf16[1024,128]{1,0:T(8,128)(2,1)S(1)}, bf16[1024,128]{1,0:T(8,128)(2,1)S(1)}) fusion(s32[128]{0:T(128)S(1)} %iota_add_fusion.1, s32[1024]{0:T(1024)S(1)} %iota_add_fusion), kind=kLoop, calls=%fused_computation.11 | loop fusion | flops 2097152 | bytes 528896 | tf_op jit(solution)/shard_map/convert_element_type | solution.py:31
  2.9 0.1 pad_maximum_fusion.wave_ref
  3.0 1.0 %fusion.9 = (f32[64,1024]{1,0:T(8,128)S(1)}, f32[64,1024]{1,0:T(8,128)S(1)}) fusion(s32[1024]{0:T(1024)S(1)} %iota_add_fusion), kind=kLoop, calls=%fused_computation.21 | loop fusion | flops 917504 | bytes 528384 | tf_op jit(solution)/shard_map/sin | solution.py:40
  4.0 0.0 copy-done
  4.0 10.8 %shard_map.37 = bf16[32,64,256]{2,1,0:T(8,128)(2,1)S(1)} custom-call(f32[2,64,1024]{2,1,0:T(8,128)S(1)} %copy-done, bf16[2,32,64,1024]{3,2,1,0:T(8,128)(2,1)} %filt_ref.1, bf16[128,128]{1,0:T(8,128)(2,1)S(1)} %maximum_maximum_fusion.table_ref, f32[64,1024]{1,0:T(8,128)S(1)} %get-tuple-element.8.tcos_ref, f32[64,1024]{1,0:T(8,128)S(1)} %get-tuple-element.7.tsin_ref, ...), custom_call_target="tpu_custom_call" | custom-call | tf_op jit(solution)/shard_map/pallas_call | solution.py:228
  14.8 1.6 %copy.6 = bf16[32,64,256]{2,0,1:T(8,128)(2,1)} copy(bf16[32,64,256]{2,1,0:T(8,128)(2,1)S(1)} %shard_map.37) | data formatting | bytes 2097152 | tf_op jit(solution)/shard_map/pallas_call | solution.py:228
  16.3 45.6 %shard_map.38.slots_ref = bf16[16,4,32,256]{3,2,1,0:T(8,128)(2,1)} custom-call(bf16[64,32,256]{2,1,0:T(8,128)(2,1)} %bitcast.3), custom_call_target="tpu_custom_call" | custom-call | tf_op jit(solution)/shard_map/pallas_call | solution.py:145
  61.9 5.8 %shard_map.39 = bf16[2,4,1024,128]{3,2,1,0:T(8,128)(2,1)} custom-call(bf16[2,1024,512]{2,1,0:T(8,128)(2,1)} %mix_ref.1, bf16[16,4,32,256]{3,2,1,0:T(8,128)(2,1)} %shard_map.38.slots_ref), custom_call_target="tpu_custom_call" | custom-call | tf_op jit(solution)/shard_map/pallas_call | solution.py:180
  (2 shorter events, 0.0 us)
Async XLA Ops:
  0.0 4.0 %copy-start = (f32[2,64,1024]{2,1,0:T(8,128)S(1)}, f32[2,64,1024]{2,1,0:T(8,128)}, u32[]{:S(2)}) copy-start(f32[2,64,1024]{2,1,0:T(8,128)} %spec_ref.1) | copy-start | bytes 1572868

commit v18 on v12

--- a/solution.py
+++ b/solution.py
@@ -60,6 +60,8 @@
     at_bank = lambda peer: (me_tm, peer)
     near = [(x + step) % width * depth + z for step in range(1, width)]
     near += [xx * depth + up for xx in range(width)] + [xx * depth + down for xx in range(width)]
+    slot_of = lambda b: (b % depth) * width + b // depth
+    me_slot = z * width + x
     barrier = pltpu.get_barrier_semaphore()
     for step in range(1, n_tm):
         pl.semaphore_signal(barrier, inc=1, device_id=at_tm((me_tm + step) % n_tm), device_id_type=MESH)
@@ -73,11 +75,7 @@
         )
 
     def relays(g):
-        out = []
-        for xx in range(width):
-            out.append((xx * depth + down, 0, x * depth + up, 0, xx))
-            out.append((xx * depth + up, half, x * depth + down, 1, xx))
-        return out
+        return [(down * width, 0, x * depth + up, 0), (up * width, half, x * depth + down, 1)]
 
     sends = []
     for g in range(stages):
@@ -95,12 +93,12 @@
         part = pl.ds(g * group, group)
         for source in near:
             remote(
-                o_ref.at[source, part], o_ref.at[source, part],
+                o_ref.at[slot_of(source), part], o_ref.at[slot_of(source), part],
                 gather_send.at[g, source], gather_recv.at[g, source], at_bank(source),
             ).wait_recv()
-        for slot, start, target, way, xx in relays(g):
-            block = o_ref.at[slot, part, pl.ds(start, half)]
-            copy = remote(block, block, relay_send.at[g, way, xx], relay_recv.at[g, way, xx], at_bank(target))
+        for first, start, target, way in relays(g):
+            block = o_ref.at[pl.ds(first, width), part, pl.ds(start, half)]
+            copy = remote(block, block, relay_send.at[g, way], relay_recv.at[g, way], at_bank(target))
             copy.start()
             sends.append(copy)
 
@@ -114,10 +112,10 @@
                 scatter_send.at[g, source], scatter_recv.at[g, source], at_tm(source),
             ).wait_recv()
             total = total + slots[part, source].astype(jnp.float32)
-        o_ref[me_bank, part] = total.astype(o_ref.dtype)
+        o_ref[me_slot, part] = total.astype(o_ref.dtype)
         for peer in near:
             copy = remote(
-                o_ref.at[me_bank, part], o_ref.at[me_bank, part],
+                o_ref.at[me_slot, part], o_ref.at[me_slot, part],
                 gather_send.at[g, peer], gather_recv.at[g, me_bank], at_bank(peer),
             )
             copy.start()
@@ -128,12 +126,11 @@
     across = (z + 2) % depth
     for g in range(stages):
         part = pl.ds(g * group, group)
-        for xx in range(width):
-            for way, start, via in ((0, 0, down), (1, half, up)):
-                block = o_ref.at[xx * depth + across, part, pl.ds(start, half)]
-                remote(
-                    block, block, relay_send.at[g, way, xx], relay_recv.at[g, way, xx], at_bank(x * depth + via)
-                ).wait_recv()
+        for way, start, via in ((0, 0, down), (1, half, up)):
+            block = o_ref.at[pl.ds(across * width, width), part, pl.ds(start, half)]
+            remote(
+                block, block, relay_send.at[g, way], relay_recv.at[g, way], at_bank(x * depth + via)
+            ).wait_recv()
     for copy in sends:
         copy.wait_send()
 
@@ -153,17 +150,18 @@
             pltpu.SemaphoreType.DMA((stages, n_tm)),
             pltpu.SemaphoreType.DMA((stages, n_bank)),
             pltpu.SemaphoreType.DMA((stages, n_bank)),
-            pltpu.SemaphoreType.DMA((stages, 2, width)),
-            pltpu.SemaphoreType.DMA((stages, 2, width)),
+            pltpu.SemaphoreType.DMA((stages, 2)),
+            pltpu.SemaphoreType.DMA((stages, 2)),
         ],
         compiler_params=pltpu.CompilerParams(collective_id=0, has_side_effects=True),
     )(x)
 
 
-def mix_kernel(mix_ref, slots_ref, o_ref):
+def mix_kernel(width, mix_ref, slots_ref, o_ref):
     n, rows, _, cols = slots_ref.shape
     half = cols // 2
-    order = range(n)
+    depth = n // width
+    order = [z * width + x for x in range(width) for z in range(depth)]
     mix_real = mix_ref[0]
     mix_imag = mix_ref[1]
     for t in range(rows):
@@ -176,11 +174,11 @@
         o_ref[1, t] = result[:, half:].astype(o_ref.dtype)
 
 
-def mix(mixing, slots):
+def mix(mixing, slots, width):
     _, rows, _, cols = slots.shape
     templates = mixing.shape[1]
     return pl.pallas_call(
-        mix_kernel,
+        functools.partial(mix_kernel, width),
         out_shape=jax.ShapeDtypeStruct((2, rows, templates, cols // 2), jnp.bfloat16),
         in_specs=[pl.BlockSpec(memory_space=pltpu.VMEM)] * 2,
         out_specs=pl.BlockSpec(memory_space=pltpu.VMEM),
@@ -254,7 +252,7 @@
     wave = wave_block(freqs, lags, outer)
     partial = front(spectrum, filters, table, twist_cos, twist_sin, wave).transpose(1, 0, 2)
     slots = exchange(partial, lax.axis_size("tm"), lax.axis_size("bank"), 4)
-    return mix(mixing, slots)
+    return mix(mixing, slots, 4)
 
 
 def solution(mesh):

time: 67.5 us -> 67.3 us (level)
  no operation moved by 1% of the time
where the time goes in v18:
time: 67.3 us; the launch traced here: 67.2 us
  Pallas kernels  61.6 us (92%)
  other arithmetic  3.97 us (6%)
  local copies, waits for them, and re-layouts  1.56 us (2%)
    pallas_call x1, Pallas kernels, exchange(): pl.pallas_call(functools.partial(exchange_kernel, width, group), out_shap...  45.4 us
    pallas_call x1, Pallas kernels, front(): pl.pallas_call(front_kernel, grid=(basis // block,), out_shape=jax.ShapeD...  10.8 us
    pallas_call x1, Pallas kernels, mix(): pl.pallas_call(functools.partial(mix_kernel, width), out_shape=jax.ShapeD...  5.51 us
    convert_element_type x1, other arithmetic, wave_block(): cosine = jnp.cos(angle).astype(jnp.bfloat16)  2.48 us
    pallas_call x1, local copies, waits for them, and re-layouts, front(): pl.pallas_call(front_kernel, grid=(basis // block,), out_shape=jax.ShapeD...  1.55 us

profile of v18, /device:TPU:6, one launch (start us, length us, event | category | flops | bytes accessed | tf_op | source)
XLA Modules:
  0.0 67.2 jit_solution(11871150400012555480)
XLA Ops:
  0.0 0.0 copy-start
  0.0 0.1 fusion.17
  0.2 0.2 sine_convert_fusion.1
  0.3 0.1 maximum_maximum_fusion.table_ref
  0.4 2.5 %cosine_convert_fusion = (bf16[1024,128]{1,0:T(8,128)(2,1)S(1)}, bf16[1024,128]{1,0:T(8,128)(2,1)S(1)}) fusion(s32[128]{0:T(128)S(1)} %iota_add_fusion.1, s32[1024]{0:T(1024)S(1)} %iota_add_fusion), kind=kLoop, calls=%fused_computation.11 | loop fusion | flops 2097152 | bytes 528896 | tf_op jit(solution)/shard_map/convert_element_type | solution.py:31
  2.9 0.1 pad_maximum_fusion.wave_ref
  3.0 1.0 %fusion.9 = (f32[64,1024]{1,0:T(8,128)S(1)}, f32[64,1024]{1,0:T(8,128)S(1)}) fusion(s32[1024]{0:T(1024)S(1)} %iota_add_fusion), kind=kLoop, calls=%fused_computation.21 | loop fusion | flops 917504 | bytes 528384 | tf_op jit(solution)/shard_map/sin | solution.py:40
  4.0 0.0 copy-done
  4.0 10.8 %shard_map.37 = bf16[32,64,256]{2,1,0:T(8,128)(2,1)S(1)} custom-call(f32[2,64,1024]{2,1,0:T(8,128)S(1)} %copy-done, bf16[2,32,64,1024]{3,2,1,0:T(8,128)(2,1)} %filt_ref.1, bf16[128,128]{1,0:T(8,128)(2,1)S(1)} %maximum_maximum_fusion.table_ref, f32[64,1024]{1,0:T(8,128)S(1)} %get-tuple-element.8.tcos_ref, f32[64,1024]{1,0:T(8,128)S(1)} %get-tuple-element.7.tsin_ref, ...), custom_call_target="tpu_custom_call" | custom-call | tf_op jit(solution)/shard_map/pallas_call | solution.py:224
  14.8 1.6 %copy.6 = bf16[32,64,256]{2,0,1:T(8,128)(2,1)} copy(bf16[32,64,256]{2,1,0:T(8,128)(2,1)S(1)} %shard_map.37) | data formatting | bytes 2097152 | tf_op jit(solution)/shard_map/pallas_call | solution.py:224
  16.3 45.4 %shard_map.38.slots_ref = bf16[16,4,32,256]{3,2,1,0:T(8,128)(2,1)} custom-call(bf16[64,32,256]{2,1,0:T(8,128)(2,1)} %bitcast.3), custom_call_target="tpu_custom_call" | custom-call | tf_op jit(solution)/shard_map/pallas_call | solution.py:142
  61.7 5.5 %shard_map.39 = bf16[2,4,1024,128]{3,2,1,0:T(8,128)(2,1)} custom-call(bf16[2,1024,512]{2,1,0:T(8,128)(2,1)} %mix_ref.1, bf16[16,4,32,256]{3,2,1,0:T(8,128)(2,1)} %shard_map.38.slots_ref), custom_call_target="tpu_custom_call" | custom-call | tf_op jit(solution)/shard_map/pallas_call | solution.py:180
  (2 shorter events, 0.0 us)
Async XLA Ops:
  0.0 4.0 %copy-start = (f32[2,64,1024]{2,1,0:T(8,128)S(1)}, f32[2,64,1024]{2,1,0:T(8,128)}, u32[]{:S(2)}) copy-start(f32[2,64,1024]{2,1,0:T(8,128)} %spec_ref.1) | copy-start | bytes 1572868

commit v19 on v18

--- a/solution.py
+++ b/solution.py
@@ -217,7 +217,7 @@
     o_ref[...] = result.reshape(o_ref.shape).astype(o_ref.dtype)
 
 
-def front(spectrum, filters, table, twist_cos, twist_sin, wave, block=8):
+def front(spectrum, filters, table, twist_cos, twist_sin, wave, block=4):
     _, basis, inner, freq = filters.shape
     cols = wave.shape[1]
     whole = lambda *shape: pl.BlockSpec(shape, lambda i: (0,) * len(shape))

time: 67.3 us -> 67.9 us (level)
  no operation moved by 1% of the time
where the time goes in v19:
time: 67.9 us; the launch traced here: 67.5 us
  Pallas kernels  62 us (91%)
  other arithmetic  3.97 us (6%)
  local copies, waits for them, and re-layouts  1.56 us (2%)
    pallas_call x1, Pallas kernels, exchange(): pl.pallas_call(functools.partial(exchange_kernel, width, group), out_shap...  45.4 us
    pallas_call x1, Pallas kernels, front(): pl.pallas_call(front_kernel, grid=(basis // block,), out_shape=jax.ShapeD...  11.1 us
    pallas_call x1, Pallas kernels, mix(): pl.pallas_call(functools.partial(mix_kernel, width), out_shape=jax.ShapeD...  5.51 us
    convert_element_type x1, other arithmetic, wave_block(): cosine = jnp.cos(angle).astype(jnp.bfloat16)  2.48 us
    pallas_call x1, local copies, waits for them, and re-layouts, front(): pl.pallas_call(front_kernel, grid=(basis // block,), out_shape=jax.ShapeD...  1.55 us

profile of v19, /device:TPU:6, one launch (start us, length us, event | category | flops | bytes accessed | tf_op | source)
XLA Modules:
  0.0 67.5 jit_solution(4478219241677725865)
XLA Ops:
  0.0 0.0 copy-start
  0.0 0.1 fusion.17
  0.2 0.2 sine_convert_fusion.1
  0.3 0.1 maximum_maximum_fusion.table_ref
  0.4 2.5 %cosine_convert_fusion = (bf16[1024,128]{1,0:T(8,128)(2,1)S(1)}, bf16[1024,128]{1,0:T(8,128)(2,1)S(1)}) fusion(s32[128]{0:T(128)S(1)} %iota_add_fusion.1, s32[1024]{0:T(1024)S(1)} %iota_add_fusion), kind=kLoop, calls=%fused_computation.11 | loop fusion | flops 2097152 | bytes 528896 | tf_op jit(solution)/shard_map/convert_element_type | solution.py:31
  2.9 0.1 pad_maximum_fusion.wave_ref
  3.0 1.0 %fusion.9 = (f32[64,1024]{1,0:T(8,128)S(1)}, f32[64,1024]{1,0:T(8,128)S(1)}) fusion(s32[1024]{0:T(1024)S(1)} %iota_add_fusion), kind=kLoop, calls=%fused_computation.21 | loop fusion | flops 917504 | bytes 528384 | tf_op jit(solution)/shard_map/sin | solution.py:40
  4.0 0.0 copy-done
  4.0 11.1 %shard_map.37 = bf16[32,64,256]{2,1,0:T(8,128)(2,1)S(1)} custom-call(f32[2,64,1024]{2,1,0:T(8,128)S(1)} %copy-done, bf16[2,32,64,1024]{3,2,1,0:T(8,128)(2,1)} %filt_ref.1, bf16[128,128]{1,0:T(8,128)(2,1)S(1)} %maximum_maximum_fusion.table_ref, f32[64,1024]{1,0:T(8,128)S(1)} %get-tuple-element.8.tcos_ref, f32[64,1024]{1,0:T(8,128)S(1)} %get-tuple-element.7.tsin_ref, ...), custom_call_target="tpu_custom_call" | custom-call | tf_op jit(solution)/shard_map/pallas_call | solution.py:224
  15.1 1.6 %copy.6 = bf16[32,64,256]{2,0,1:T(8,128)(2,1)} copy(bf16[32,64,256]{2,1,0:T(8,128)(2,1)S(1)} %shard_map.37) | data formatting | bytes 2097152 | tf_op jit(solution)/shard_map/pallas_call | solution.py:224
  16.6 45.4 %shard_map.38.slots_ref = bf16[16,4,32,256]{3,2,1,0:T(8,128)(2,1)} custom-call(bf16[64,32,256]{2,1,0:T(8,128)(2,1)} %bitcast.3), custom_call_target="tpu_custom_call" | custom-call | tf_op jit(solution)/shard_map/pallas_call | solution.py:142
  62.0 5.5 %shard_map.39 = bf16[2,4,1024,128]{3,2,1,0:T(8,128)(2,1)} custom-call(bf16[2,1024,512]{2,1,0:T(8,128)(2,1)} %mix_ref.1, bf16[16,4,32,256]{3,2,1,0:T(8,128)(2,1)} %shard_map.38.slots_ref), custom_call_target="tpu_custom_call" | custom-call | tf_op jit(solution)/shard_map/pallas_call | solution.py:180
  (2 shorter events, 0.0 us)
Async XLA Ops:
  0.0 4.0 %copy-start = (f32[2,64,1024]{2,1,0:T(8,128)S(1)}, f32[2,64,1024]{2,1,0:T(8,128)}, u32[]{:S(2)}) copy-start(f32[2,64,1024]{2,1,0:T(8,128)} %spec_ref.1) | copy-start | bytes 1572868

commit v20 on v18

--- a/solution.py
+++ b/solution.py
@@ -104,6 +104,8 @@
 
     for g in range(stages):
         part = pl.ds(g * group, group)
+        if g >= 1:
+            forward(g - 1)
         total = x_ref[pl.ds(me_tm * rows + g * group, group)].astype(jnp.float32)
         for step in range(1, n_tm):
             source = (me_tm + n_tm - step) % n_tm
@@ -120,8 +122,6 @@
             )
             copy.start()
             sends.append(copy)
-        if g >= 1:
-            forward(g - 1)
     forward(stages - 1)
     across = (z + 2) % depth
     for g in range(stages):

time: 67.3 us -> 69.9 us (1.039)
  Pallas kernels: 61.6 us -> 64.2 us
    pallas_call x1, Pallas kernels: 45.4 us -> 48 us  [exchange(): pl.pallas_call(functools.partial(exchange_kernel, width, group), out_shap...]
where the time goes in v20:
time: 69.9 us; the launch traced here: 69.8 us
  Pallas kernels  64.2 us (92%)
  other arithmetic  3.97 us (6%)
  local copies, waits for them, and re-layouts  1.56 us (2%)
    pallas_call x1, Pallas kernels, exchange(): pl.pallas_call(functools.partial(exchange_kernel, width, group), out_shap...  48 us
    pallas_call x1, Pallas kernels, front(): pl.pallas_call(front_kernel, grid=(basis // block,), out_shape=jax.ShapeD...  10.8 us
    pallas_call x1, Pallas kernels, mix(): pl.pallas_call(functools.partial(mix_kernel, width), out_shape=jax.ShapeD...  5.51 us
    convert_element_type x1, other arithmetic, wave_block(): cosine = jnp.cos(angle).astype(jnp.bfloat16)  2.48 us
    pallas_call x1, local copies, waits for them, and re-layouts, front(): pl.pallas_call(front_kernel, grid=(basis // block,), out_shape=jax.ShapeD...  1.55 us

profile of v20, /device:TPU:6, one launch (start us, length us, event | category | flops | bytes accessed | tf_op | source)
XLA Modules:
  0.0 69.8 jit_solution(14748603541327924425)
XLA Ops:
  0.0 0.0 copy-start
  0.0 0.1 fusion.17
  0.2 0.2 sine_convert_fusion.1
  0.3 0.1 maximum_maximum_fusion.table_ref
  0.4 2.5 %cosine_convert_fusion = (bf16[1024,128]{1,0:T(8,128)(2,1)S(1)}, bf16[1024,128]{1,0:T(8,128)(2,1)S(1)}) fusion(s32[128]{0:T(128)S(1)} %iota_add_fusion.1, s32[1024]{0:T(1024)S(1)} %iota_add_fusion), kind=kLoop, calls=%fused_computation.11 | loop fusion | flops 2097152 | bytes 528896 | tf_op jit(solution)/shard_map/convert_element_type | solution.py:31
  2.9 0.1 pad_maximum_fusion.wave_ref
  3.0 1.0 %fusion.9 = (f32[64,1024]{1,0:T(8,128)S(1)}, f32[64,1024]{1,0:T(8,128)S(1)}) fusion(s32[1024]{0:T(1024)S(1)} %iota_add_fusion), kind=kLoop, calls=%fused_computation.21 | loop fusion | flops 917504 | bytes 528384 | tf_op jit(solution)/shard_map/sin | solution.py:40
  4.0 0.0 copy-done
  4.0 10.8 %shard_map.37 = bf16[32,64,256]{2,1,0:T(8,128)(2,1)S(1)} custom-call(f32[2,64,1024]{2,1,0:T(8,128)S(1)} %copy-done, bf16[2,32,64,1024]{3,2,1,0:T(8,128)(2,1)} %filt_ref.1, bf16[128,128]{1,0:T(8,128)(2,1)S(1)} %maximum_maximum_fusion.table_ref, f32[64,1024]{1,0:T(8,128)S(1)} %get-tuple-element.8.tcos_ref, f32[64,1024]{1,0:T(8,128)S(1)} %get-tuple-element.7.tsin_ref, ...), custom_call_target="tpu_custom_call" | custom-call | tf_op jit(solution)/shard_map/pallas_call | solution.py:224
  14.8 1.6 %copy.6 = bf16[32,64,256]{2,0,1:T(8,128)(2,1)} copy(bf16[32,64,256]{2,1,0:T(8,128)(2,1)S(1)} %shard_map.37) | data formatting | bytes 2097152 | tf_op jit(solution)/shard_map/pallas_call | solution.py:224
  16.3 48.0 %shard_map.38.slots_ref = bf16[16,4,32,256]{3,2,1,0:T(8,128)(2,1)} custom-call(bf16[64,32,256]{2,1,0:T(8,128)(2,1)} %bitcast.3), custom_call_target="tpu_custom_call" | custom-call | tf_op jit(solution)/shard_map/pallas_call | solution.py:142
  64.3 5.5 %shard_map.39 = bf16[2,4,1024,128]{3,2,1,0:T(8,128)(2,1)} custom-call(bf16[2,1024,512]{2,1,0:T(8,128)(2,1)} %mix_ref.1, bf16[16,4,32,256]{3,2,1,0:T(8,128)(2,1)} %shard_map.38.slots_ref), custom_call_target="tpu_custom_call" | custom-call | tf_op jit(solution)/shard_map/pallas_call | solution.py:180
  (2 shorter events, 0.0 us)
Async XLA Ops:
  0.0 4.0 %copy-start = (f32[2,64,1024]{2,1,0:T(8,128)S(1)}, f32[2,64,1024]{2,1,0:T(8,128)}, u32[]{:S(2)}) copy-start(f32[2,64,1024]{2,1,0:T(8,128)} %spec_ref.1) | copy-start | bytes 1572868
